TPU v7x, 32 devices: a whole 2x2x4 slice. The times are simulated.
32 devices in a mesh: seq: 16 (over z, x, core), batch: 2 (over y).
Axes of the slice: x: 2, y: 2, z: 4, core: 2. Of those that a mesh axis runs over, the one named last changes fastest.
Arguments:
- inputs: bfloat16 [2, 2, 1024, 1024], P(None, 'batch', 'seq'), may hold values from -6 to 6
- cotangent: bfloat16 [2, 2, 1024, 1024], P(None, 'batch', 'seq'), may hold values from -6 to 6
- document_ids: int32 [2, 2, 1024], P(None, 'batch'), may hold values from 0 to 3, never falling along the last dimension, each value on 1 to 512 neighbouring positions
- query_weight: bfloat16 [1024, 1024], P(('seq', 'batch')), may hold values from -0.1875 to 0.1875
- key_weight: bfloat16 [1024, 1024], P(('seq', 'batch')), may hold values from -0.1875 to 0.1875
- value_weight: bfloat16 [1024, 1024], P(('seq', 'batch')), may hold values from -0.1875 to 0.1875
- beta_weight: bfloat16 [1024, 8], P(('seq', 'batch')), may hold values from -0.75 to 0.75
- outgate_weight: bfloat16 [1024, 1024], P(('seq', 'batch')), may hold values from -0.1875 to 0.1875
- output_weight: bfloat16 [1024, 1024], P(('seq', 'batch')), may hold values from -0.375 to 0.375
- gate_weight: bfloat16 [1024, 2816], P(('seq', 'batch')), may hold values from -0.1875 to 0.1875
- up_weight: bfloat16 [1024, 2816], P(('seq', 'batch')), may hold values from -0.1875 to 0.1875
- down_weight: bfloat16 [2816, 1024], P(('seq', 'batch')), may hold values from -0.21875 to 0.21875
- mixer_gain: bfloat16 [1024], P(('seq', 'batch')), may hold values from 0.5 to 1.5
- swiglu_gain: bfloat16 [1024], P(('seq', 'batch')), may hold values from 0.5 to 1.5
- head_gain: bfloat16 [128], replicated, may hold values from 0.5 to 1.5
- conv_weight: bfloat16 [12, 1024], P(None, ('seq', 'batch')), may hold values from -3 to 3
Outputs:
- block_output: bfloat16 [2, 2, 1024, 1024], P(None, 'batch', 'seq')
- input_grad: bfloat16 [2, 2, 1024, 1024], P(None, 'batch', 'seq')
- query_grad: float32 [1024, 1024], P(('seq', 'batch'))
- key_grad: float32 [1024, 1024], P(('seq', 'batch'))
- value_grad: float32 [1024, 1024], P(('seq', 'batch'))
- beta_grad: float32 [1024, 8], P(('seq', 'batch'))
- outgate_grad: float32 [1024, 1024], P(('seq', 'batch'))
- outproj_grad: float32 [1024, 1024], P(('seq', 'batch'))
- gate_grad: float32 [1024, 2816], P(('seq', 'batch'))
- up_grad: float32 [1024, 2816], P(('seq', 'batch'))
- down_grad: float32 [2816, 1024], P(('seq', 'batch'))
- mixer_gain_grad: float32 [1024], P(('seq', 'batch'))
- swiglu_gain_grad: float32 [1024], P(('seq', 'batch'))
- head_gain_grad: float32 [128], replicated
- conv_grad: float32 [12, 1024], P(None, ('seq', 'batch'))
Inputs may be any that keep to these rules, and one draw needn't show every extreme that they name: `document_ids`: along each packed row the ids never fall; each id holds 1 to 512 consecutive tokens, and one holds exactly 512.
All inputs are finite; a program needn't handle non-finite values.
Results may differ from a plain program's by a relative error of at most 0.017.
Values may be sent and summed in bfloat16 or wider, within the bound.
No kernel may reach another device: no remote copies, remote signals or barrier semaphores. Data moves between devices by JAX's collectives and lax.ppermute only.
A program may use at most 320 MiB of HBM per device.

v0:
```python
from functools import partial

import jax
import jax.numpy as jnp
from jax import lax
from jax.experimental import pallas as pl
from jax.experimental.pallas import tpu as pltpu
from jax.sharding import Mesh, PartitionSpec as P

HEADS = 8
HEAD = 128
CONV = 4
EPSILON = 1e-05
UNIT_EPSILON = 1e-06
CHUNK = 128
GROUP = 4
COST = 10**6
F32 = jnp.float32
BF16 = jnp.bfloat16
NN = (((1,), (0,)), ((), ()))
NT = (((1,), (1,)), ((), ()))
TN = (((0,), (0,)), ((), ()))


def split(value):
    high = value.astype(BF16)
    return (high, (value - high.astype(F32)).astype(BF16))


def mm(left, right, dims):
    def dot(a, b):
        return lax.dot_general(a, b, dims, preferred_element_type=F32)

    return dot(left[0], right[0]) + (dot(left[0], right[1]) + dot(left[1], right[0]))


def block_mask(size, width):
    row = lax.broadcasted_iota(jnp.int32, (size, size), 0)
    col = lax.broadcasted_iota(jnp.int32, (size, size), 1)
    return (row // width) == (col // width)


def tri_masks(size):
    row = lax.broadcasted_iota(jnp.int32, (size, size), 0)
    col = lax.broadcasted_iota(jnp.int32, (size, size), 1)
    return (row > col, row >= col, row == col)


def unit_lower_inverses(mats):
    size = mats[0].shape[0]
    eye = tri_masks(size)[2].astype(F32)
    near = block_mask(size, 8)
    base = [split(jnp.where(near, m, 0.0)) for m in mats]
    square = [split(mm(b, b, NN)) for b in base]
    first = [eye - jnp.where(near, m, 0.0) for m in mats]
    second = [f + mm(split(f), s, NN) for f, s in zip(first, square)]
    fourth = [split(mm(s, s, NN)) for s in square]
    inverse = [f + mm(split(f), s, NN) for f, s in zip(second, fourth)]
    width = 8
    while width < size:
        inside, wider = block_mask(size, width), block_mask(size, 2 * width)
        cut = jnp.logical_and(wider, jnp.logical_not(inside))
        off = [split(jnp.where(cut, m, 0.0)) for m in mats]
        halves = [split(t) for t in inverse]
        step = [split(mm(t, o, NN)) for t, o in zip(halves, off)]
        inverse = [t - mm(s, h, NN) for t, s, h in zip(inverse, step, halves)]
        width *= 2
    return inverse


def place_of(pos_ref):
    return (pos_ref[0], pos_ref[1], pos_ref[2], pos_ref[3])


def head_of(pos_ref, chips):
    return pos_ref[2] * (HEADS // 2) + pos_ref[1] // (chips // (HEADS // 2))


def pack_heads(pos_ref, wq_ref, wk_ref, wv_ref, wg_ref, small_ref, *out_refs):
    chips = len(out_refs)
    repeat = chips // (HEADS // 2)
    for d, out_ref in enumerate(out_refs):
        slot = (pos_ref[1] ^ d) // repeat
        for i in range(2):
            cols = pl.ds(pl.multiple_of((i * (HEADS // 2) + slot) * HEAD, HEAD), HEAD)
            for t, w_ref in enumerate((wq_ref, wk_ref, wv_ref, wg_ref)):
                spot = (4 * i + t) * HEAD
                out_ref[:, spot : spot + HEAD] = w_ref[:, cols]
        out_ref[:, 8 * HEAD :] = small_ref[...]


def mixer_prepare(
    pos_ref,
    xown_ref,
    xsib_ref,
    wown_ref,
    wsib_ref,
    flag_ref,
    idc_ref,
    idr_ref,
    normed_ref,
    wcat_ref,
    lin_ref,
    tap_ref,
    gains_ref,
    p_ref,
    qh_ref,
    k_ref,
    v_ref,
    sq_ref,
    sk_ref,
    sv_ref,
    beta_ref,
    t_ref,
    sc_ref,
    pb_ref,
    w_ref,
    map_ref,
    add_ref,
    across_ref,
):
    chips, _, span, width = xown_ref.shape
    length = normed_ref.shape[0]
    count = length // CHUNK
    strict, incl, _ = tri_masks(CHUNK)
    m, q, c, _ = place_of(pos_ref)
    head = head_of(pos_ref, chips)
    rows_here = wown_ref.shape[1]
    for i in range(wown_ref.shape[0]):
        block = (m ^ (i // chips)) * chips + (q ^ (i % chips))
        mine = pl.ds(pl.multiple_of((2 * block + c) * rows_here, rows_here), rows_here)
        theirs = pl.ds(pl.multiple_of((2 * block + 1 - c) * rows_here, rows_here), rows_here)
        cols = pl.ds(pl.multiple_of(c * 4 * HEAD, 4 * HEAD), 4 * HEAD)
        wcat_ref[mine, 0 : 4 * HEAD] = wown_ref[i, :, cols]
        wcat_ref[mine, 4 * HEAD :] = wown_ref[i, :, 8 * HEAD :]
        wcat_ref[theirs, :] = wsib_ref[i, :, :]
    for i in range(width // HEAD):
        rows = slice(i * HEAD, (i + 1) * HEAD)
        across_ref[:, rows] = jnp.transpose(wcat_ref[rows, 4 * HEAD :].astype(F32))
    gain = across_ref[HEADS : HEADS + 1, :]
    gains_ref[...] = across_ref[HEADS : HEADS + 8, :]
    mine = pl.ds(pl.multiple_of(head * HEAD, HEAD), HEAD)
    tap_ref[...] = across_ref[HEADS + 2 : HEADS + 18, mine]
    for i in range(2 * chips):
        block = (m ^ (i % 2)) * chips + (q ^ (i // 2))
        for which, ref in ((c, xown_ref), (1 - c, xsib_ref)):
            x = ref[i // 2, i % 2, :, :].astype(F32)
            scale = lax.rsqrt(jnp.mean(x * x, axis=-1, keepdims=True) + EPSILON)
            spot = pl.ds(pl.multiple_of((2 * block + which) * span, span), span)
            normed_ref[spot, :] = (x * scale * gain).astype(BF16)
    lane = lax.broadcasted_iota(jnp.int32, (1, HEAD), 1)
    pick = (lane == head).astype(F32)
    p_ref[0:8, :] = jnp.zeros((8, 3 * HEAD), F32)

    tall = 4 * CHUNK
    for n in range(length // tall):
        rows = slice(n * tall, (n + 1) * tall)
        y = lax.dot_general(normed_ref[rows, :], wcat_ref[...], NN, preferred_element_type=F32)
        p_ref[8 + n * tall : 8 + (n + 1) * tall, :] = y[:, 0 : 3 * HEAD].astype(BF16).astype(F32)
        lin_ref[rows, :] = y[:, 3 * HEAD : 4 * HEAD]
        logit = jnp.sum(y[:, 4 * HEAD :] * pick, axis=-1, keepdims=True)
        beta_ref[rows, :] = jax.nn.sigmoid(logit)
    for n in range(count):
        r0 = n * CHUNK
        rows = slice(r0, r0 + CHUNK)
        keep = [None] + [flag_ref[rows, j : j + 1] for j in range(CONV - 1)]
        for c in range(3):
            cols = slice(c * HEAD, (c + 1) * HEAD)
            pre = tap_ref[4 * c : 4 * c + 1, :] * p_ref[8 + r0 : 8 + r0 + CHUNK, cols]
            for j in range(1, CONV):
                moved = p_ref[8 + r0 - j : 8 + r0 - j + CHUNK, cols]
                pre = pre + tap_ref[4 * c + j : 4 * c + j + 1, :] * moved * keep[j]
            sig = jax.nn.sigmoid(pre)
            act = pre * sig
            slope = sig * (1.0 + pre * (1.0 - sig))
            if c == 2:
                v_ref[rows, :] = act
                sv_ref[rows, :] = slope
            else:
                scale = lax.rsqrt(jnp.sum(act * act, axis=-1, keepdims=True) + UNIT_EPSILON)
                (qh_ref if c == 0 else k_ref)[rows, :] = act * scale
                (sq_ref if c == 0 else sk_ref)[rows, :] = slope * scale
    def prepare(group, carry):
        spots = [pl.multiple_of((group * GROUP + i) * CHUNK, CHUNK) for i in range(GROUP)]
        rows = [pl.ds(s, CHUNK) for s in spots]
        key = [split(k_ref[r, :]) for r in rows]
        same = [
            idc_ref[r, :] == idr_ref[group * GROUP + i, :, :] for i, r in enumerate(rows)
        ]
        beta = [beta_ref[r, :] for r in rows]
        mats = [
            jnp.where(jnp.logical_and(s, strict), b * mm(k, k, NT), 0.0)
            for s, b, k in zip(same, beta, key)
        ]
        inverse = unit_lower_inverses(mats)
        for i, r in enumerate(rows):
            t_ref[r, :] = inverse[i]
            inv = split(inverse[i])
            pseudo = mm(inv, split(beta[i] * v_ref[r, :]), NN)
            weighed = split(
                mm(inv, split(beta[i] * flag_ref[r, 3:4] * k_ref[r, :]), NN)
            )
            ends = split(flag_ref[r, 4:5] * k_ref[r, :])
            query = split(qh_ref[r, :] * HEAD ** (-0.5))
            sc_ref[r, :] = jnp.where(
                jnp.logical_and(same[i], incl), mm(query, key[i], NT), 0.0
            )
            pb_ref[r, :] = pseudo
            w_ref[r, :] = weighed[0].astype(F32) + weighed[1].astype(F32)
            map_ref[r, :] = mm(weighed, ends, TN)
            add_ref[r, :] = mm(split(pseudo), ends, TN)
        return carry

    lax.fori_loop(0, count // GROUP, prepare, 0)


def mixer_produce(
    lin_ref,
    flag_ref,
    idc_ref,
    idr_ref,
    gain_ref,
    qh_ref,
    k_ref,
    v_ref,
    sc_ref,
    pb_ref,
    w_ref,
    map_ref,
    add_ref,
    heads_ref,
    state_ref,
    ps_ref,
    er_ref,
    oh_ref,
    ro_ref,
):
    length = lin_ref.shape[0]
    count = length // CHUNK
    strict, _, _ = tri_masks(CHUNK)
    state = jnp.zeros((HEAD, HEAD), F32)
    for n in range(count):
        rows = slice(n * CHUNK, (n + 1) * CHUNK)
        state_ref[rows, :] = state
        last = flag_ref[(n + 1) * CHUNK - 1 : (n + 1) * CHUNK, 3:4]
        state = last * state - mm(split(state), split(map_ref[rows, :]), NN) + add_ref[rows, :]

    def produce(group, carry):
        for i in range(GROUP):
            r = pl.ds(pl.multiple_of((group * GROUP + i) * CHUNK, CHUNK), CHUNK)
            same = idc_ref[r, :] == idr_ref[group * GROUP + i, :, :]
            key = split(k_ref[r, :])
            state_i = split(state_ref[r, :])
            flag = flag_ref[r, 3:4]
            pseudo = pb_ref[r, :] - mm(split(w_ref[r, :]), state_i, NT)
            ps_ref[r, :] = pseudo
            halves = split(pseudo)
            gram = jnp.where(jnp.logical_and(same, strict), mm(key, key, NT), 0.0)
            er_ref[r, :] = (
                v_ref[r, :] - flag * mm(key, state_i, NT) - mm(split(gram), halves, NN)
            )
            query = split(qh_ref[r, :] * HEAD ** (-0.5))
            out = flag * mm(query, state_i, NT) + mm(split(sc_ref[r, :]), halves, NN)
            scale = lax.rsqrt(jnp.mean(out * out, axis=-1, keepdims=True) + EPSILON)
            hat = out * scale
            oh_ref[r, :] = hat
            ro_ref[r, :] = scale
            lin = lin_ref[r, :]
            made = (hat * gain_ref[...] * (lin * jax.nn.sigmoid(lin))).astype(BF16)
            half = CHUNK // 2
            spot = pl.ds(pl.multiple_of((group * GROUP + i) * half, half), half)
            for chip in range(heads_ref.shape[0]):
                heads_ref[chip, 0, spot, :] = made[:half]
                heads_ref[chip, 1, spot, :] = made[half:]
        return carry

    lax.fori_loop(0, count // GROUP, produce, 0)


def mixer_backward_states(
    dh_ref,
    lin_ref,
    flag_ref,
    gain_ref,
    qh_ref,
    k_ref,
    beta_ref,
    t_ref,
    sc_ref,
    map_ref,
    oh_ref,
    ro_ref,
    dg_ref,
    headgrad_ref,
    do_ref,
    dpre_ref,
    dstate_ref,
    back_ref,
):
    length = lin_ref.shape[0]
    count = length // CHUNK
    chips = dh_ref.shape[0] // 2
    scale_q = HEAD ** (-0.5)
    headgrad_ref[...] = jnp.zeros(headgrad_ref.shape, F32)

    def first(group, carry):
        for i in range(GROUP):
            r = pl.ds(pl.multiple_of((group * GROUP + i) * CHUNK, CHUNK), CHUNK)
            block = group * GROUP + i
            pair = [dh_ref[2 * (block % chips) + j, block // chips, :, :] for j in range(2)]
            grad = jnp.concatenate(pair, axis=0).astype(F32)
            lin = lin_ref[r, :]
            sig = jax.nn.sigmoid(lin)
            swish = lin * sig
            hat = oh_ref[r, :]
            gain = gain_ref[...]
            both = grad * hat
            headgrad_ref[0:1, :] += jnp.sum(both * swish, axis=0, keepdims=True)
            dg_ref[r, :] = (
                both * gain * (sig * (1.0 + lin * (1.0 - sig)))
            ).astype(BF16)
            lead = grad * gain * swish
            grad_out = ro_ref[r, :] * (
                lead - hat * jnp.mean(lead * hat, axis=-1, keepdims=True)
            )
            do_ref[r, :] = grad_out
            flag = flag_ref[r, 3:4]
            direct = mm(split(sc_ref[r, :]), split(grad_out), TN)
            dpre_ref[r, :] = direct
            zed = mm(split(t_ref[r, :]), split(direct), TN)
            back_ref[r, :] = mm(
                split(flag * grad_out), split(qh_ref[r, :] * scale_q), TN
            ) - mm(split(beta_ref[r, :] * flag * zed), split(k_ref[r, :]), TN)
        return carry

    lax.fori_loop(0, count // GROUP, first, 0)
    grad_state = jnp.zeros((HEAD, HEAD), F32)
    for n in reversed(range(count)):
        rows = slice(n * CHUNK, (n + 1) * CHUNK)
        dstate_ref[rows, :] = grad_state
        last = flag_ref[(n + 1) * CHUNK - 1 : (n + 1) * CHUNK, 3:4]
        grad_state = (
            last * grad_state
            - mm(split(grad_state), split(map_ref[rows, :]), NT)
            + back_ref[rows, :]
        )


def mixer_backward_tokens(
    do_ref,
    dpre_ref,
    dstate_ref,
    flag_ref,
    idc_ref,
    idr_ref,
    pick_ref,
    qh_ref,
    k_ref,
    sq_ref,
    sk_ref,
    sv_ref,
    beta_ref,
    t_ref,
    state_ref,
    ps_ref,
    er_ref,
    du_ref,
    dz_ref,
):
    length = do_ref.shape[0]
    count = length // CHUNK
    strict, incl, _ = tri_masks(CHUNK)
    scale_q = HEAD ** (-0.5)
    du_ref[length : length + 8, :] = jnp.zeros((8, 3 * HEAD), F32)

    def second(group, carry):
        for i in range(GROUP):
            r = pl.ds(pl.multiple_of((group * GROUP + i) * CHUNK, CHUNK), CHUNK)
            same = idc_ref[r, :] == idr_ref[group * GROUP + i, :, :]
            low = jnp.logical_and(same, strict)
            full = jnp.logical_and(same, incl)
            flag = flag_ref[r, 3:4]
            ends = flag_ref[r, 4:5]
            beta = beta_ref[r, :]
            key_f = k_ref[r, :]
            key = split(key_f)
            q_hat = qh_ref[r, :]
            query = split(q_hat * scale_q)
            state_i = split(state_ref[r, :])
            dstate = split(dstate_ref[r, :])
            grad_out = split(do_ref[r, :])
            pseudo = split(ps_ref[r, :])
            dpre = dpre_ref[r, :] + ends * mm(key, dstate, NT)
            zed = mm(split(t_ref[r, :]), split(dpre), TN)
            zeds = split(zed)
            dscore = split(jnp.where(full, mm(grad_out, pseudo, NT), 0.0))
            grad_q = flag * mm(grad_out, state_i, NN) + mm(dscore, key, NN)
            dgram = split(jnp.where(low, -beta * mm(zeds, pseudo, NT), 0.0))
            grad_v = beta * zed
            grad_k = (
                mm(dscore, query, TN)
                + ends * mm(pseudo, dstate, NN)
                + mm(dgram, key, NN)
                + mm(dgram, key, TN)
                - flag * mm(split(grad_v), state_i, NN)
            )
            grad_b = jnp.sum(zed * er_ref[r, :], axis=-1, keepdims=True)
            dz = grad_b * beta * (1.0 - beta)
            dz_ref[r, :] = (dz * pick_ref[...]).astype(BF16)
            lead = scale_q * grad_q
            du_ref[r, 0:HEAD] = sq_ref[r, :] * (
                lead - q_hat * jnp.sum(lead * q_hat, axis=-1, keepdims=True)
            )
            du_ref[r, HEAD : 2 * HEAD] = sk_ref[r, :] * (
                grad_k - key_f * jnp.sum(grad_k * key_f, axis=-1, keepdims=True)
            )
            du_ref[r, 2 * HEAD : 3 * HEAD] = sv_ref[r, :] * grad_v
        return carry

    lax.fori_loop(0, count // GROUP, second, 0)


def mixer_backward_taps(
    du_ref,
    dg_ref,
    dz_ref,
    flag_ref,
    tap_ref,
    p_ref,
    pos_ref,
    normed_ref,
    wcat_ref,
    swiglu_ref,
    dnkeep_ref,
    dnsend_ref,
    dwkeep_ref,
    dwsend_ref,
    dcat_ref,
    tapgrad_ref,
):
    length = dg_ref.shape[0]
    count = length // CHUNK
    blocks, rows_here, _ = dwkeep_ref.shape
    chips = blocks // 2
    repeat = chips // (HEADS // 2)
    span = length // (2 * blocks)
    core, share = pos_ref[2], pos_ref[1] % repeat
    head = head_of(pos_ref, chips)
    dcat_ref[:, 3 * HEAD : 4 * HEAD] = dg_ref[...]
    dcat_ref[:, 4 * HEAD : 5 * HEAD] = dz_ref[...]
    sums = [[jnp.zeros((1, HEAD), F32) for _ in range(CONV)] for _ in range(3)]
    for n in range(count):
        r0 = n * CHUNK
        rows = slice(r0, r0 + CHUNK)
        for c in range(3):
            cols = slice(c * HEAD, (c + 1) * HEAD)
            here = du_ref[rows, cols]
            grad = tap_ref[4 * c : 4 * c + 1, :] * here
            sums[c][0] += jnp.sum(
                here * p_ref[8 + r0 : 8 + r0 + CHUNK, cols], axis=0, keepdims=True
            )
            for j in range(1, CONV):
                after = slice(r0 + j, r0 + j + CHUNK)
                grad = grad + tap_ref[4 * c + j : 4 * c + j + 1, :] * (
                    du_ref[after, cols] * flag_ref[after, j - 1 : j]
                )
                moved = p_ref[8 + r0 - j : 8 + r0 - j + CHUNK, cols]
                sums[c][j] += jnp.sum(
                    here * flag_ref[rows, j - 1 : j] * moved, axis=0, keepdims=True
                )
            dcat_ref[rows, cols] = grad.astype(BF16)
    tapgrad_ref[...] = jnp.concatenate(
        [sums[c][j] for c in range(3) for j in range(CONV)]
        + [jnp.zeros((4, HEAD), F32)],
        axis=0,
    )
    if repeat > 1:
        for n in range(count):
            counts = (n % chips % repeat == share).astype(F32)
            rows = slice(n * CHUNK, (n + 1) * CHUNK)
            dcat_ref[rows, :] = (dcat_ref[rows, :].astype(F32) * counts).astype(BF16)
        tapgrad_ref[...] = tapgrad_ref[...] * (share == 0).astype(F32)
    width = normed_ref.shape[1]

    tall = 4 * CHUNK
    for n in range(length // tall):
        rows = slice(n * tall, (n + 1) * tall)
        part = lax.dot_general(dcat_ref[rows, :], wcat_ref[...], NT, preferred_element_type=F32)
        for j in range(4):
            low = part[2 * j * span : (2 * j + 1) * span]
            high = part[(2 * j + 1) * span : (2 * j + 2) * span]
            dnkeep_ref[4 * n + j, :, :] = jnp.where(core == 1, high, low).astype(BF16)
            dnsend_ref[4 * n + j, :, :] = jnp.where(core == 1, low, high).astype(BF16)
    for i in range(width // HEAD):
        cols = slice(i * HEAD, (i + 1) * HEAD)
        if i % 4 == 0:
            wide = slice(i * HEAD, (i + 4) * HEAD)
            four = lax.dot_general(
                normed_ref[:, wide], dcat_ref[...], TN, preferred_element_type=F32
            )
        grad = four[i % 4 * HEAD : (i % 4 + 1) * HEAD]
        mats = wcat_ref[cols, :].astype(F32)
        gain = mats[:, 4 * HEAD + HEADS : 4 * HEAD + HEADS + 1]
        gain_grad = jnp.sum(grad * mats, axis=-1, keepdims=True) / gain
        here = (head == i).astype(F32)
        lines = jnp.concatenate(
            [
                jnp.zeros((HEADS, HEAD), F32),
                jnp.zeros((1, HEAD), F32),
                swiglu_ref[0:1, cols],
                tapgrad_ref[0 : 3 * CONV, :] * here,
                jnp.zeros((HEAD - HEADS - 2 - 3 * CONV, HEAD), F32),
            ],
            axis=0,
        )
        lane = lax.broadcasted_iota(jnp.int32, (1, HEAD), 1)
        small = grad[:, 4 * HEAD :] + jnp.transpose(lines) + gain_grad * (lane == HEADS)
        grad = jnp.concatenate([grad[:, : 4 * HEAD], small], axis=1)
        per = HEAD // (2 * rows_here)
        for j in range(per):
            low = grad[2 * j * rows_here : (2 * j + 1) * rows_here]
            high = grad[(2 * j + 1) * rows_here : (2 * j + 2) * rows_here]
            dwkeep_ref[i * per + j, :, :] = jnp.where(core == 1, high, low).astype(BF16)
            dwsend_ref[i * per + j, :, :] = jnp.where(core == 1, low, high).astype(BF16)


def feed_forward(
    pos_ref,
    got_ref,
    xown_ref,
    cot_ref,
    oown_ref,
    osib_ref,
    pown_ref,
    psib_ref,
    down_ref,
    gains_ref,
    wo_ref,
    normed_ref,
    grads_ref,
    hidden_ref,
    cots_ref,
    swiglu_ref,
    res_ref,
    norm_ref,
    *rest,
):
    chips, _, span, width = xown_ref.shape
    send_refs, (wp_ref, heads_ref, total_ref, hat_ref, part_ref) = rest[: chips - 1], rest[chips - 1 :]
    repeat = chips // (HEADS // 2)
    tokens = 2 * chips * span
    ff = down_ref.shape[0]
    m, q, c, _ = place_of(pos_ref)
    rows_here = oown_ref.shape[2]
    for i in range(2 * chips):
        d, e = i // 2, i % 2
        block = (m ^ e) * chips + (q ^ d)
        for which, o_ref, p_ref in ((c, oown_ref, pown_ref), (1 - c, osib_ref, psib_ref)):
            spot = pl.ds(pl.multiple_of((2 * block + which) * rows_here, rows_here), rows_here)
            wo_ref[spot, :] = o_ref[d, e, :, :]
            other = (m ^ e) * chips + d
            spot = pl.ds(pl.multiple_of((2 * other + which) * rows_here, rows_here), rows_here)
            wp_ref[spot, :] = p_ref[e, d, :, :]
        spot = pl.ds(pl.multiple_of(block * span, span), span)
        total_ref[spot, :] = xown_ref[d, e, :, :].astype(F32)
        cots_ref[spot, :] = cot_ref[d, e, :, :]
    for i in range(2):
        for j in range(HEADS // 2):
            h = i * (HEADS // 2) + j
            heads_ref[:, h * HEAD : (h + 1) * HEAD] = got_ref[2 * j * repeat + i, :, :]
    total = total_ref[...] + lax.dot_general(
        heads_ref[...], wo_ref[...], NN, preferred_element_type=F32
    )
    total_ref[...] = total
    scale = lax.rsqrt(jnp.mean(total * total, axis=-1, keepdims=True) + EPSILON)
    hat = total * scale
    hat_ref[...] = hat
    normed_ref[...] = (hat * gains_ref[1:2, :]).astype(BF16)
    both = lax.dot_general(normed_ref[...], wp_ref[...], NN, preferred_element_type=F32)
    gate, up = both[:, :ff], both[:, ff:]
    sig = jax.nn.sigmoid(gate)
    act = gate * sig
    hidden_ref[...] = (act * up).astype(BF16)
    back = lax.dot_general(cots_ref[...], down_ref[...], NT, preferred_element_type=F32)
    slope = sig * (1.0 + gate * (1.0 - sig))
    grads_ref[...] = jnp.concatenate([back * up * slope, back * act], axis=1).astype(BF16)
    part_ref[...] = lax.dot_general(grads_ref[...], wp_ref[...], NT, preferred_element_type=F32)
    total = jnp.sum(part_ref[...] * hat_ref[...], axis=0, keepdims=True)
    swiglu_ref[...] = jnp.broadcast_to(total, swiglu_ref.shape)
    for e in range(2):
        spot = pl.ds(pl.multiple_of((e * chips + q) * span, span), span)
        res_ref[e, :, :] = total_ref[spot, :]
        norm_ref[e, :, :] = part_ref[spot, :]
        for d, send_ref in enumerate(send_refs):
            spot = pl.ds(pl.multiple_of((e * chips + (q ^ (d + 1))) * span, span), span)
            send_ref[e, :, :] = part_ref[spot, :].astype(BF16)


def feed_forward_grads(
    pos_ref, normed_ref, grads_ref, hidden_ref, cots_ref, down_ref, keep_ref, send_ref, downgrad_ref, out_ref
):
    rows_here = keep_ref.shape[1]
    chips, _, span, _ = out_ref.shape
    core = pos_ref[2]
    per = HEAD // (2 * rows_here)
    for i in range(normed_ref.shape[1] // HEAD):
        if i % 4 == 0:
            wide = slice(i * HEAD, (i + 4) * HEAD)
            four = lax.dot_general(
                normed_ref[:, wide], grads_ref[...], TN, preferred_element_type=F32
            )
        grad = four[i % 4 * HEAD : (i % 4 + 1) * HEAD]
        for j in range(per):
            low = grad[2 * j * rows_here : (2 * j + 1) * rows_here]
            high = grad[(2 * j + 1) * rows_here : (2 * j + 2) * rows_here]
            keep_ref[i * per + j, :, :] = jnp.where(core == 1, high, low).astype(BF16)
            send_ref[i * per + j, :, :] = jnp.where(core == 1, low, high).astype(BF16)
    downgrad_ref[...] = lax.dot_general(
        hidden_ref[...], cots_ref[...], TN, preferred_element_type=F32
    ).astype(BF16)
    out = lax.dot_general(hidden_ref[...], down_ref[...], NN, preferred_element_type=F32)
    for e in range(2):
        for j in range(chips):
            spot = (e * chips + j) * span
            out_ref[j, e, :, :] = out[spot : spot + span].astype(BF16)


def branch_gradient(pos_ref, norm_ref, res_ref, cot_ref, gains_ref, wo_ref, *rest):
    *got_refs, resid_ref, branch_ref, heads_ref = rest
    m = pos_ref[0]
    chips = heads_ref.shape[0] // 2
    repeat = chips // (HEADS // 2)
    branches = []
    for e in range(2):
        norm = norm_ref[e, :, :]
        for got_ref in got_refs:
            norm = norm + got_ref[e, :, :].astype(F32)
        res = res_ref[e, :, :]
        scale = lax.rsqrt(jnp.mean(res * res, axis=-1, keepdims=True) + EPSILON)
        hat = res * scale
        lead = norm * gains_ref[1:2, :]
        grad = cot_ref[0, m ^ e, :, :].astype(F32) + scale * (
            lead - hat * jnp.mean(lead * hat, axis=-1, keepdims=True)
        )
        resid_ref[e, :, :] = grad
        branch = grad.astype(BF16)
        branch_ref[e, :, :] = branch
        branches.append(branch)
    back = lax.dot_general(
        jnp.concatenate(branches, axis=0), wo_ref[...], NT, preferred_element_type=F32
    ).astype(BF16)
    span = branch_ref.shape[1]
    for e in range(2):
        for j in range(chips):
            for i in range(2):
                h = i * (HEADS // 2) + j // repeat
                heads_ref[2 * j + i, e, :, :] = back[
                    e * span : (e + 1) * span, h * HEAD : (h + 1) * HEAD
                ]


def output_gradient(pos_ref, got_ref, branch_ref, all_ref, rows_ref, duo_ref):
    chips, _, span, width = branch_ref.shape
    repeat = chips // (HEADS // 2)
    q = pos_ref[1]
    share = q % repeat
    for i in range(2 * chips):
        d, e = i // 2, i % 2
        spot = pl.ds(pl.multiple_of((e * chips + (q ^ d)) * span, span), span)
        counts = ((q ^ d) % repeat == share).astype(F32)
        rows_ref[spot, :] = (branch_ref[d, e, :, :].astype(F32) * counts).astype(BF16)
    first = pl.multiple_of((q // repeat) * 2 * repeat, 2)
    for i in range(2):
        duo_ref[:, i * HEAD : (i + 1) * HEAD] = got_ref[first + i, :, :]
    both = lax.dot_general(duo_ref[...], rows_ref[...], TN, preferred_element_type=F32)
    for i in range(2):
        all_ref[i, :, :] = both[i * HEAD : (i + 1) * HEAD].astype(BF16)


def input_gradient(pos_ref, resid_ref, x_ref, gains_ref, keep_ref, *rest):
    *got_refs, out_ref = rest
    m = pos_ref[0]
    for e in range(2):
        norm = keep_ref[e, :, :]
        for got_ref in got_refs:
            norm = norm + got_ref[e, :, :].astype(F32)
        x = x_ref[m ^ e, :, :].astype(F32)
        scale = lax.rsqrt(jnp.mean(x * x, axis=-1, keepdims=True) + EPSILON)
        hat = x * scale
        lead = norm * gains_ref[0:1, :]
        out_ref[e, :, :] = (
            resid_ref[e, :, :]
            + scale * (lead - hat * jnp.mean(lead * hat, axis=-1, keepdims=True))
        ).astype(BF16)


def token_pieces(pos_ref, keep_ref, got_ref, own_ref, *send_refs):
    chips = keep_ref.shape[0] // 2
    q = pos_ref[1]
    for e in range(2):
        for d in range(chips):
            block = e * chips + (q ^ d)
            total = keep_ref[block, :, :].astype(F32) + got_ref[block, :, :].astype(F32)
            if d == 0:
                own_ref[e, :, :] = total
            else:
                send_refs[d - 1][e, :, :] = total.astype(BF16)


def merge_heads(pos_ref, keep_ref, got_ref, out_ref):
    core = pos_ref[2]
    wide = 4 * HEAD
    keep, got = keep_ref[...], got_ref[...]
    out_ref[:, :, :wide] = jnp.where(core == 1, got[:, :, :wide], keep[:, :, :wide])
    out_ref[:, :, wide : 2 * wide] = jnp.where(core == 1, keep[:, :, :wide], got[:, :, :wide])
    out_ref[:, :, 2 * wide :] = (
        keep[:, :, wide:].astype(F32) + got[:, :, wide:].astype(F32)
    ).astype(BF16)


def spread_heads(pos_ref, *refs):
    *got_refs, wq_ref, wk_ref, wv_ref, wg_ref, beta_ref, gains_ref, taps_ref, head_ref, side_ref = refs
    chips = len(got_refs)
    repeat = chips // (HEADS // 2)
    rows = wq_ref.shape[0]
    small = jnp.zeros((rows, HEAD), F32)
    heads = jnp.zeros((1, HEAD), F32)
    if repeat > 1:
        for ref in (wq_ref, wk_ref, wv_ref, wg_ref):
            ref[...] = jnp.zeros(ref.shape, F32)
    for d, got_ref in enumerate(got_refs):
        slot = (pos_ref[1] ^ d) // repeat
        for i in range(2):
            cols = pl.ds(pl.multiple_of((i * (HEADS // 2) + slot) * HEAD, HEAD), HEAD)
            for t, ref in enumerate((wq_ref, wk_ref, wv_ref, wg_ref)):
                spot = (4 * i + t) * HEAD
                value = got_ref[0:rows, spot : spot + HEAD].astype(F32)
                ref[:, cols] = value + ref[:, cols] if repeat > 1 else value
        small = small + got_ref[0:rows, 8 * HEAD :].astype(F32)
        heads = heads + got_ref[rows : rows + 1, 0:HEAD].astype(F32)
    beta_ref[...] = small[:, :HEADS]
    side_ref[...] = jnp.zeros(side_ref.shape, F32)
    side_ref[0:rows, :] = small
    across = jnp.transpose(side_ref[...])
    gains_ref[...] = across[HEADS : HEADS + 8, :rows]
    taps_ref[...] = across[HEADS + 2 : HEADS + 2 + 3 * CONV, :rows]
    head_ref[...] = heads


def spread_pair(got_ref, gate_ref, up_ref):
    chips, _, wide = got_ref.shape
    wide = wide // 4
    for j in range(chips):
        got = got_ref[j, :, :].astype(F32)
        for t, ref in enumerate((gate_ref, up_ref)):
            for e in range(2):
                part = (2 * t + e) * wide
                spot = (e * chips + j) * wide
                ref[:, spot : spot + wide] = got[:, part : part + wide]


VMEM_SPEC = pl.BlockSpec(memory_space=pltpu.VMEM)


def run_kernel(body, name, operands, out_shapes, scratch, micros, scalars=()):
    specs = [VMEM_SPEC] * len(operands)
    for i in scalars:
        specs[i] = pl.BlockSpec(memory_space=pltpu.SMEM)
    return pl.pallas_call(
        body,
        name=name,
        out_shape=[jax.ShapeDtypeStruct(*s) for s in out_shapes],
        in_specs=specs,
        out_specs=[VMEM_SPEC] * len(out_shapes),
        scratch_shapes=[pltpu.VMEM(*s) for s in scratch],
        compiler_params=pltpu.CompilerParams(vmem_limit_bytes=56 * 1024 * 1024),
        cost_estimate=pl.CostEstimate(
            flops=micros * COST, bytes_accessed=1 << 10, transcendentals=0
        ),
    )(*operands)


def tie(value, *others):
    return lax.optimization_barrier((value,) + others)[0]


def together(*values):
    return lax.optimization_barrier(values)


def swap(value, axis, mask):
    return lax.ppermute(value, axis, [(i, i ^ mask) for i in range(lax.axis_size(axis))])


def ordered(bit, mine, other):
    flag = bit == 1
    return (jnp.where(flag, other, mine), jnp.where(flag, mine, other))


def from_chips(value):
    return [value] + [swap(value, "q", d) for d in range(1, lax.axis_size("q"))]


def to_chips(blocks):
    chip = lax.axis_index("q")
    mine = [lax.dynamic_index_in_dim(blocks, chip ^ d, 0, keepdims=False) for d in range(blocks.shape[0])]
    return [mine[0]] + [swap(mine[d], "q", d) for d in range(1, len(mine))]


def gather_batch(value, axis):
    step, batch = 1, lax.axis_index("b")
    lead, rows = value.shape[:axis], value.shape[axis:]
    while step < lax.axis_size("b"):
        got = swap(value, "b", step)
        value = jnp.stack(ordered((batch // step) % 2, value, got), axis=axis)
        step *= 2
    return value.reshape(lead + (lax.axis_size("b") * rows[0],) + rows[1:])


def scatter_bit(value, axis, bit, mesh_axis, mask):
    low, high = (lax.index_in_dim(value, i, axis, keepdims=False) for i in (0, 1))
    flag = bit == 1
    keep, send = jnp.where(flag, high, low), jnp.where(flag, low, high)
    return keep.astype(F32) + swap(send.astype(BF16), mesh_axis, mask).astype(F32)


def scatter_batch(value, axis):
    batch, step = lax.axis_index("b"), lax.axis_size("b") // 2
    while step >= 1:
        shape = value.shape
        value = value.reshape(shape[:axis] + (2, shape[axis] // 2) + shape[axis + 1 :])
        value = scatter_bit(value, axis, (batch // step) % 2, "b", step)
        step //= 2
    return lax.squeeze(value, (axis,))


def token_flags(ids):
    length = ids.shape[0]
    padded = jnp.concatenate([jnp.full((CONV - 1,), -1, jnp.int32), ids])
    by_chunk = ids.reshape(length // CHUNK, CHUNK)
    before = jnp.concatenate([jnp.full((1,), -1, jnp.int32), by_chunk[:-1, -1]])
    columns = [padded[CONV - 1 - j : CONV - 1 - j + length] == ids for j in range(1, CONV)]
    columns.append((by_chunk == before[:, None]).reshape(length))
    columns.append((by_chunk == by_chunk[:, -1:]).reshape(length))
    flags = jnp.stack(columns, axis=1).astype(F32)
    return jnp.pad(flags, ((0, 8), (0, 3))), by_chunk[:, None, :], ids[:, None]


def on_device(
    inputs,
    cotangent,
    document_ids,
    query_weight,
    key_weight,
    value_weight,
    beta_weight,
    outgate_weight,
    output_weight,
    gate_weight,
    up_weight,
    down_weight,
    mixer_gain,
    swiglu_gain,
    head_gain,
    conv_weight,
):
    micro, _, span, width = inputs.shape
    chips, n_batch = lax.axis_size("q"), lax.axis_size("b")
    half_heads = HEADS // 2
    repeat = chips // half_heads
    length = micro * chips * 2 * span
    rows_w = query_weight.shape[0]
    rows_f = down_weight.shape[0]
    rows_all = n_batch * rows_w
    blocks_all = micro * chips
    ff_here = rows_f * micro * 2 * n_batch
    row, chip, core = lax.axis_index("m"), lax.axis_index("q"), lax.axis_index("c")
    share = chip % repeat
    flag_row = row == 1
    pos = jnp.stack([row, chip, core, lax.axis_index("b")]).astype(jnp.int32)

    small = jnp.concatenate(
        [
            beta_weight,
            mixer_gain[:, None],
            swiglu_gain[:, None],
            jnp.swapaxes(conv_weight, 0, 1),
            jnp.zeros((rows_w, HEAD - HEADS - 2 - 3 * CONV), BF16),
        ],
        axis=1,
    )
    mine = run_kernel(
        pack_heads,
        "pack_heads",
        (pos, query_weight, key_weight, value_weight, outgate_weight, small),
        [((rows_w, 9 * HEAD), BF16)] * chips,
        [],
        1,
        (0,),
    )
    head_s = [swap(mine[d], "q", d) for d in range(1, chips)]

    def own_slab(value):
        return jnp.where(flag_row, value[1], value[0])

    def away_slab(value):
        return jnp.where(flag_row, value[0], value[1])

    x_s, out_s = swap(away_slab(inputs[:, 0]), "m", 1), swap(output_weight, "m", 1)
    head_s, x_s, out_s = together(head_s, x_s, out_s)
    head_q = jnp.stack([mine[0]] + head_s, axis=0)
    x_own = jnp.stack([own_slab(inputs[:, 0]), x_s], axis=0)
    head_m = jnp.stack([head_q, swap(head_q, "m", 1)], axis=0)
    x_half = jnp.stack(from_chips(x_own), axis=0)
    out_b = gather_batch(jnp.stack([output_weight, out_s], axis=0), 1)
    ids = own_slab(document_ids[:, 0])
    flags, id_rows, id_cols = token_flags(ids)
    gain_vec = head_gain.astype(F32)[None, :]
    head_m, x_half, out_b, flags, id_rows, id_cols, gain_vec = together(
        head_m, x_half, out_b, flags, id_rows, id_cols, gain_vec
    )
    head_b = gather_batch(head_m.reshape(blocks_all, rows_w, 9 * HEAD), 1)
    x_sib = swap(x_half, "c", 1)
    cot_s = swap(tie(away_slab(cotangent[:, 0]), x_half), "m", 1)
    pair = jnp.stack([gate_weight, up_weight], axis=1).reshape(
        rows_w, 2, micro, chips, 2 * n_batch * rows_f
    )
    pair = jnp.moveaxis(pair, 3, 0).reshape(chips, rows_w, 2 * ff_here)
    pair_q = lax.all_to_all(tie(pair, x_half), ("q",), 0, 0, tiled=True)
    head_b, x_sib, cot_s, pair_q = together(head_b, x_sib, cot_s, pair_q)
    cot_own = jnp.stack([own_slab(cotangent[:, 0]), cot_s], axis=0)
    send = lax.dynamic_slice_in_dim(head_b, (1 - core) * 4 * HEAD, 4 * HEAD, 2)
    head_sib = swap(jnp.concatenate([send, head_b[..., 8 * HEAD :]], axis=-1), "c", 1)
    pair_s = swap(tie(pair_q, head_b), "m", 1)
    out_s = [swap(tie(out_b, head_b), "q", d) for d in range(1, chips)]

    count = length // CHUNK
    tall = ((length, HEAD), F32)
    square = ((length, CHUNK), F32)
    states = ((count * HEAD, HEAD), F32)
    thin = ((length, 1), F32)
    slabs = ((2, span, width), BF16)
    slabs_wide = ((2, span, width), F32)
    normed, w_cat, lin, taps, gains, p_pad, q_hat, k_vec, v_vec, slope_q, slope_k, slope_v, beta, t_mat, score, pseudo, weighed, step_map, step_add = run_kernel(
        mixer_prepare,
        "mixer_prepare",
        (pos, x_half, x_sib, head_b, head_sib, flags, id_cols, id_rows),
        [
            ((length, width), BF16),
            ((width, 5 * HEAD), BF16),
            tall,
            ((16, HEAD), F32),
            ((8, width), F32),
            ((length + 8, 3 * HEAD), F32),
        ]
        + [tall] * 6
        + [thin, square, square, tall, tall, states, states],
        [((HEAD, width), F32)],
        20,
        (0,),
    )
    pair_s, out_s, lin_late = together(pair_s, out_s, lin)
    pair_m = jnp.stack([pair_q, pair_s], axis=0).reshape(blocks_all, rows_w, 2 * ff_here)
    out_q = jnp.stack([out_b] + out_s, axis=0)
    cot_s = [swap(tie(cot_own, lin_late), "q", d) for d in range(1, chips)]
    down_s = swap(tie(down_weight, lin_late), "m", 1)
    pair_b = gather_batch(pair_m, 1)
    heads_here, state, pseudo, error, out_hat, out_scale = run_kernel(
        mixer_produce,
        "mixer_produce",
        (tie(lin_late, pair_m, out_q), flags, id_cols, id_rows, gain_vec)
        + (q_hat, k_vec, v_vec, score, pseudo, weighed, step_map, step_add),
        [((chips, 2, length // 2, HEAD), BF16), states, tall, tall, tall, thin],
        [],
        9,
    )

    got_heads = lax.all_to_all(
        heads_here.reshape(chips * 2, length // 2, HEAD), ("q", "c"), 0, 0, tiled=True
    )
    pair_b, down_s, cot_s = tie((pair_b, down_s, cot_s), heads_here)
    down_m = jnp.stack(ordered(row, down_weight, down_s), axis=0)
    down_b = gather_batch(down_m, 1)
    cot_half = jnp.stack([cot_own] + cot_s, axis=0)
    pair_b = pair_b.reshape(micro, chips, rows_all, 2 * ff_here)
    pair_sib = swap(pair_b, "c", 1)
    out_sib = swap(out_q, "c", 1)
    down_sib = swap(down_b, "c", 1)
    w_down = jnp.stack(ordered(core, down_b, down_sib), axis=1).reshape(ff_here, width)
    half = length // 2
    w_out, normed_two, pair_up, hidden, cot_rows, swiglu_part, res_own, norm_own, *norm_send = run_kernel(
        feed_forward,
        "feed_forward",
        (pos, got_heads, x_half, cot_half, out_q, out_sib, pair_b, pair_sib, w_down, gains),
        [
            ((width, width), BF16),
            ((half, width), BF16),
            ((half, 2 * ff_here), BF16),
            ((half, ff_here), BF16),
            ((half, width), BF16),
            ((8, width), F32),
            slabs_wide,
            slabs_wide,
        ]
        + [slabs] * (chips - 1),
        [
            ((width, 2 * ff_here), BF16),
            ((half, width), BF16),
            ((half, width), F32),
            ((half, width), F32),
            ((half, width), F32),
        ],
        12,
        (0,),
    )
    norm_got = [swap(v, "q", d + 1) for d, v in enumerate(norm_send)]
    pair_keep, pair_send, down_grad, out_part = run_kernel(
        feed_forward_grads,
        "feed_forward_grads",
        (pos, normed_two, pair_up, hidden, cot_rows, w_down),
        [
            ((blocks_all, rows_all, 2 * ff_here), BF16),
            ((blocks_all, rows_all, 2 * ff_here), BF16),
            ((ff_here, width), BF16),
            ((chips, 2, span, width), BF16),
        ],
        [],
        6,
        (0,),
    )
    norm_got, norm_own, pair_keep, pair_send, down_grad, out_part = together(
        norm_got, norm_own, pair_keep, pair_send, down_grad, out_part
    )
    grad_resid, grad_branch, grad_heads = run_kernel(
        branch_gradient,
        "branch_gradient",
        (pos, norm_own, res_own, cot_half, gains, w_out, *norm_got),
        [slabs_wide, slabs, ((chips * 2, 2, span, HEAD), BF16)],
        [],
        2,
        (0,),
    )
    dheads = lax.all_to_all(grad_heads, ("q", "c"), 0, 0, tiled=True)

    pair_got = swap(pair_send, "c", 1)
    down_grad = scatter_bit(
        down_grad.reshape(micro, 2, n_batch, rows_f, width), 1, core, "c", 1
    ).astype(BF16)
    pair_grad = pair_keep.astype(F32) + pair_got.astype(F32)
    dheads, pair_grad, down_grad = together(dheads, pair_grad, down_grad)
    pair_grad = pair_grad.reshape(blocks_all, n_batch, rows_w, 2 * ff_here)
    pair_grad = scatter_batch(pair_grad, 1).reshape(micro, chips, rows_w, 2 * ff_here)
    branch_s = [swap(grad_branch, "q", d) for d in range(1, chips)]
    grad_lin, head_part, grad_out, grad_pre, grad_state = run_kernel(
        mixer_backward_states,
        "mixer_backward_states",
        (dheads, lin, flags, gain_vec, q_hat, k_vec, beta, t_mat, score, step_map, out_hat, out_scale),
        [((length, HEAD), BF16), ((8, HEAD), F32), tall, tall, states],
        [states],
        9,
    )
    branch_s, grad_out = together(branch_s, grad_out)
    branch_all = jnp.stack([grad_branch] + branch_s, axis=0)
    (out_rows,) = run_kernel(
        output_gradient,
        "output_gradient",
        (pos, got_heads, branch_all),
        [((2, HEAD, width), BF16)],
        [((half, width), BF16), ((half, 2 * HEAD), BF16)],
        1,
        (0,),
    )
    if repeat > 1:
        head_part = jnp.where(share == 0, head_part, 0.0)
    step = repeat // 2
    while step >= 1:
        out_rows = out_rows.reshape(micro, 2, out_rows.shape[1] // 2, width)
        out_rows = scatter_bit(out_rows, 1, (share // step) % 2, "q", step)
        step //= 2
    out_rows = out_rows.astype(BF16).reshape(micro, 2, n_batch, rows_w, width)
    head_rows = jnp.pad(head_part, ((0, 0), (0, width - HEAD))).astype(BF16)
    head_rows = jnp.broadcast_to(head_rows, (micro, 2, n_batch, 8, width))
    tail = jnp.concatenate([out_rows, head_rows], axis=3)
    pair_grad, grad_out, tail = together(pair_grad, grad_out, tail)
    tail = scatter_bit(tail, 1, core, "c", 1)
    down_grad = scatter_batch(down_grad, 1)
    pair_rows = scatter_bit(pair_grad, 0, row, "m", 1).astype(BF16)
    out_got = lax.all_to_all(tie(out_part, grad_out), ("q",), 0, 0, tiled=True)
    du, grad_z = run_kernel(
        mixer_backward_tokens,
        "mixer_backward_tokens",
        (grad_out, grad_pre, grad_state, flags, id_cols, id_rows, pick_of(pos, chips), q_hat, k_vec)
        + (slope_q, slope_k, slope_v, beta, t_mat, state, pseudo, error),
        [((length + 8, 3 * HEAD), F32), ((length, HEAD), BF16)],
        [],
        10,
    )
    tail, down_grad, pair_rows, out_got, grad_z = together(
        tail, down_grad, pair_rows, out_got, grad_z
    )
    out_all = (res_own + jnp.sum(out_got.astype(F32), axis=0)).astype(BF16)

    def to_rows(value):
        keep = jnp.where(flag_row, value[1], value[0])
        send = jnp.where(flag_row, value[0], value[1])
        return jnp.stack(ordered(row, keep, swap(send, "m", 1)), axis=0)[:, None]

    tail = scatter_batch(tail, 1)
    down_grad = scatter_bit(down_grad, 0, row, "m", 1)
    pair_got = lax.all_to_all(pair_rows, ("q",), 0, 0, tiled=True)
    out_final = to_rows(out_all)
    norm_keep, norm_send, w_keep, w_send = run_kernel(
        mixer_backward_taps,
        "mixer_backward_taps",
        (du, grad_lin, grad_z, flags, taps, p_pad, pos, normed, w_cat, swiglu_part),
        [
            ((blocks_all, span, width), BF16),
            ((blocks_all, span, width), BF16),
            ((blocks_all, rows_all, 5 * HEAD), BF16),
            ((blocks_all, rows_all, 5 * HEAD), BF16),
        ],
        [((length, 5 * HEAD), BF16), ((16, HEAD), F32)],
        12,
        (6,),
    )

    tail, down_grad, pair_got, out_final, norm_send, w_send = together(
        tail, down_grad, pair_got, out_final, norm_send, w_send
    )
    tail = scatter_bit(tail, 0, row, "m", 1)
    norm_got = swap(norm_send, "c", 1)
    w_got = swap(w_send, "c", 1)
    norm_own, *norm_send = run_kernel(
        token_pieces,
        "token_pieces",
        (pos, norm_keep, norm_got),
        [slabs_wide] + [slabs] * (chips - 1),
        [],
        1,
        (0,),
    )
    (value,) = run_kernel(
        merge_heads,
        "merge_heads",
        (pos, w_keep, w_got),
        [((blocks_all, rows_all, 9 * HEAD), BF16)],
        [],
        1,
        (0,),
    )
    norm_send, value, tail = together(norm_send, value, tail)
    norm_got = [swap(v, "q", d + 1) for d, v in enumerate(norm_send)]
    value = scatter_batch(value.reshape(blocks_all, n_batch, rows_w, 9 * HEAD), 1)
    gate_grad, up_grad = run_kernel(
        spread_pair,
        "spread_pair",
        (pair_got,),
        [(gate_weight.shape[:1] + (chips * ff_here,), F32)] * 2,
        [],
        2,
    )
    value = scatter_bit(value.reshape(micro, chips, rows_w, 9 * HEAD), 0, row, "m", 1)
    (grad_own,) = run_kernel(
        input_gradient,
        "input_gradient",
        (pos, grad_resid, x_own, gains, norm_own, *norm_got),
        [slabs],
        [],
        1,
        (0,),
    )
    grad_final = to_rows(grad_own)
    head_rows = tail[rows_w:, : 9 * HEAD]
    head_rows = jnp.pad(head_rows, ((0, 0), (0, 9 * HEAD - head_rows.shape[1])))
    head_rows = jnp.broadcast_to(head_rows, (chips,) + head_rows.shape)
    value = jnp.concatenate([value, head_rows], axis=1).astype(BF16)
    *merged, beta_sum, gain_sums, tap_sums, head_sum = run_kernel(
        spread_heads,
        "spread_heads",
        (pos, *to_chips(value)),
        [((rows_w, width), F32)] * 4
        + [((rows_w, HEADS), F32), ((8, rows_w), F32), ((3 * CONV, rows_w), F32), ((1, HEAD), F32)],
        [((HEAD, HEAD), F32)],
        1,
        (0,),
    )
    return (
        out_final,
        grad_final,
        merged[0],
        merged[1],
        merged[2],
        beta_sum,
        merged[3],
        tail[:rows_w],
        gate_grad,
        up_grad,
        down_grad,
        gain_sums[0],
        gain_sums[1],
        head_sum[0],
        tap_sums,
    )


def pick_of(pos, chips):
    lane = lax.broadcasted_iota(jnp.int32, (1, HEAD), 1)
    return (lane == head_of(pos, chips)).astype(F32)


def solution(mesh):
    n_seq, n_batch = mesh.shape["seq"], mesh.shape["batch"]

    def program(*arrays):
        micro = arrays[0].shape[0]
        shape = (micro, n_seq // (2 * micro), 2, n_batch)
        fine = Mesh(mesh.devices.reshape(shape), ("m", "q", "c", "b"))
        seq, every = ("m", "q", "c"), ("m", "q", "c", "b")
        tokens, rows, vector, taps = P(None, "b", seq, None), P(every, None), P(every), P(None, every)
        return jax.shard_map(
            on_device,
            mesh=fine,
            in_specs=(tokens, tokens, P(None, "b", None))
            + (rows,) * 9
            + (vector, vector, P(), taps),
            out_specs=(tokens, tokens) + (rows,) * 9 + (vector, vector, P(), taps),
            check_vma=False,
        )(*arrays)

    return program
```

profile of v0, /device:TPU:0, one launch (start us, length us, event | category | flops | bytes accessed | tf_op | source)
XLA Modules:
  0.0 325.3 jit_solution(6777913636969393742)
XLA Ops:
  5.1 1.7 pack_heads.1
  6.8 2.9 collective-permute-start
  9.7 1.6 collective-permute-start.1
  12.3 3.1 collective-permute-start.3
  21.3 2.6 collective-permute-done.4
  27.5 1.8 collective-permute-start.9
  29.4 1.8 collective-permute-start.5
  32.7 8.3 %collective-permute-done.7 = bf16[2,64,1024]{2,1,0:T(8,128)(2,1)S(1)} collective-permute-done((bf16[2,64,1024]{2,1,0:T(8,128)(2,1)S(1)}, bf16[2,64,1024]{2,1,0:T(8,128)(2,1)S(1)}, u32[]{:S(2)}, u32[]{:S(2)}) %collective-permute-start.7) | collective-permute-done | bytes 262176 | tf_op jit(solution)/shard_map/ppermute | solution.py:792
  41.0 3.5 %collective-permute-done.8 = bf16[2,64,1024]{2,1,0:T(8,128)(2,1)S(1)} collective-permute-done((bf16[2,64,1024]{2,1,0:T(8,128)(2,1)S(1)}, bf16[2,64,1024]{2,1,0:T(8,128)(2,1)S(1)}, u32[]{:S(2)}, u32[]{:S(2)}) %collective-permute-start.8) | collective-permute-done | bytes 262176 | tf_op jit(solution)/shard_map/ppermute | solution.py:792
  44.7 1.6 collective-permute-start.10
  50.6 1.7 select_bitcast_fusion.16
  52.3 4.6 %all-to-all-start = ((bf16[4,32,1408]{2,1,0:T(8,128)(2,1)}), bf16[4,32,1408]{2,1,0:T(8,128)(2,1)S(1)}, u32[]{:S(2)}, u32[]{:S(2)}) async-start(bf16[4,32,1408]{2,1,0:T(8,128)(2,1)} %reshape.474), calls=%async_computation | async-start | bytes 720896 | tf_op jit(solution)/shard_map/all_to_all | solution.py:929
  57.0 2.9 collective-permute-start.12
  60.1 4.5 %collective-permute-done.12 = bf16[64,1024]{1,0:T(8,128)(2,1)} collective-permute-done((bf16[64,1024]{1,0:T(8,128)(2,1)}, bf16[64,1024]{1,0:T(8,128)(2,1)}, u32[]{:S(2)}, u32[]{:S(2)}) %collective-permute-start.12) | collective-permute-done | bytes 131104 | tf_op jit(solution)/shard_map/ppermute | solution.py:792
  64.6 2.8 all-to-all-done
  68.3 1.7 collective-permute-start.14
  70.1 2.9 collective-permute-start.15
  74.9 18.5 %mixer_prepare.1 = (bf16[1024,1024]{1,0:T(8,128)(2,1)}, bf16[1024,640]{1,0:T(8,128)(2,1)}, f32[1024,128]{1,0:T(8,128)}, f32[16,128]{1,0:T(8,128)}, f32[8,1024]{1...) custom-call(s32[4]{0:T(128)} %pad_add_fusion.pos_ref, ...), custom_call_target="tpu_custom_call" | custom-call | flops 20000000 | bytes 1024 | tf_op jit(solution)/shard_map/mixer_prepare/pallas_call | solution.py:769
  94.4 1.7 fusion.26
  96.0 1.5 collective-permute-start.20
  97.5 2.0 collective-permute-start.21
  102.1 9.0 %mixer_produce.1 = (bf16[4,2,512,128]{3,2,1,0:T(8,128)(2,1)}, f32[1024,128]{1,0:T(8,128)}, f32[1024,128]{1,0:T(8,128)}, f32[1024,128]{1,0:T(8,128)}, f32[1024,128]{1,0:T(8,128)}, /*index=5*/f32[1024,1]{1,0:T(8,128)}) custom-call(f32[1024,128]{1,0:T(8,128)} %get-tuple-element.183.lin_ref, f32[1032,8]{1,0:T(8,128)} %pad_convert_fusion.flag_ref, ...), custom_call_target="tpu_custom_call" | custom-call | flops 9000000 | bytes 1024 | tf_op jit(solution)/shard_map/mixer_produce/pallas_call | solution.py:769
  111.8 2.0 collective-permute-done.19
  117.1 3.7 %all-to-all-start.1 = ((bf16[8,512,128]{2,1,0:T(8,128)(2,1)}), bf16[8,512,128]{2,1,0:T(8,128)(2,1)S(1)}, u32[]{:S(2)}, u32[]{:S(2)}) async-start(bf16[8,512,128]{2,1,0:T(8,128)(2,1)} %bitcast.263), calls=%async_computation.1 | async-start | bytes 2097152 | tf_op jit(solution)/shard_map/all_to_all | solution.py:978
  121.4 3.7 %collective-permute-done.25 = bf16[2,88,1024]{2,1,0:T(8,128)(2,1)} collective-permute-done((bf16[2,88,1024]{2,1,0:T(8,128)(2,1)}, bf16[2,88,1024]{2,1,0:T(8,128)(2,1)}, u32[]{:S(2)}, u32[]{:S(2)}) %collective-permute-start.25) | collective-permute-done | bytes 360480 | tf_op jit(solution)/shard_map/ppermute | solution.py:792
  127.7 2.3 pad_maximum_fusion.5.cot_ref
  133.5 1.7 all-to-all-done.1.got_ref
  136.2 11.6 %feed_forward.1 = (bf16[1024,1024]{1,0:T(8,128)(2,1)}, bf16[512,1024]{1,0:T(8,128)(2,1)}, bf16[512,1408]{1,0:T(8,128)(2,1)}, bf16[512,704]{1,0:T(8,128)(2,1)}, b...) custom-call(s32[4]{0:T(128)} %pad_add_fusion.pos_ref, ...), custom_call_target="tpu_custom_call" | custom-call | flops 12000000 | bytes 1024 | tf_op jit(solution)/shard_map/feed_forward/pallas_call | solution.py:769
  147.8 1.5 collective-permute-start.27
  151.3 7.1 %feed_forward_grads.1 = (bf16[8,64,1408]{2,1,0:T(8,128)(2,1)}, bf16[8,64,1408]{2,1,0:T(8,128)(2,1)}, bf16[704,1024]{1,0:T(8,128)(2,1)}, bf16[4,2,64,1024]{3,2,1,0:T(8,128)(2,1)}) custom-call(s32[4]{0:T(128)} %pad_add_fusion.pos_ref, bf16[512,1024]{1,0:T(8,128)(2,1)} %get-tuple-element.207.normed_ref, bf16[512,1408]{1,0:T(8,128)(2,1)} %get-tuple-element.208.grads_ref, ...), custom_call_target="tpu_custom_call" | custom-call | flops 6000000 | bytes 1024 | tf_op jit(solution)/shard_map/feed_forward_grads/pallas_call | solution.py:769
  158.8 3.9 %collective-permute-done.29.rest_2_ = bf16[2,64,1024]{2,1,0:T(8,128)(2,1)S(1)} collective-permute-done((bf16[2,64,1024]{2,1,0:T(8,128)(2,1)}, bf16[2,64,1024]{2,1,0:T(8,128)(2,1)S(1)}, u32[]{:S(2)}, u32[]{:S(2)}) %collective-permute-start.29) | collective-permute-done | bytes 262176 | tf_op jit(solution)/shard_map/ppermute | solution.py:792
  162.7 1.6 fusion.29
  164.9 4.1 %branch_gradient.1 = (f32[2,64,1024]{2,1,0:T(8,128)}, bf16[2,64,1024]{2,1,0:T(8,128)(2,1)}, bf16[8,2,64,128]{3,2,1,0:T(8,128)(2,1)}) custom-call(s32[4]{0:T(128)} %pad_add_fusion.pos_ref, f32[2,64,1024]{2,1,0:T(8,128)} %get-tuple-element.215.norm_ref, f32[2,64,1024]{2,1,0:T(8,128)} %get-tuple-element.216.res_ref, ...), custom_call_target="tpu_custom_call" | custom-call | flops 2000000 | bytes 1024 | tf_op jit(solution)/shard_map/branch_gradient/pallas_call | solution.py:769
  169.0 1.5 collective-permute-start.33
  171.0 1.5 collective-permute-start.35
  172.5 3.6 %all-to-all-start.2 = ((bf16[8,2,64,128]{3,2,1,0:T(8,128)(2,1)}), bf16[8,2,64,128]{3,2,1,0:T(8,128)(2,1)S(1)}, u32[]{:S(2)}, u32[]{:S(2)}) async-start(bf16[8,2,64,128]{3,2,1,0:T(8,128)(2,1)} %get-tuple-element.221), calls=%async_computation.2 | async-start | bytes 524288 | tf_op jit(solution)/shard_map/all_to_all | solution.py:1043
  177.6 1.7 convert_add_fusion
  179.2 8.0 %all-to-all-done.2.dh_ref = bf16[8,2,64,128]{3,2,1,0:T(8,128)(2,1)S(1)} async-done(((bf16[8,2,64,128]{3,2,1,0:T(8,128)(2,1)}), bf16[8,2,64,128]{3,2,1,0:T(8,128)(2,1)S(1)}, u32[]{:S(2)}, u32[]{:S(2)}) %all-to-all-start.2) | async-done | bytes 262176 | tf_op jit(solution)/shard_map/all_to_all | solution.py:1043
  188.9 8.4 %mixer_backward_states.1 = (bf16[1024,128]{1,0:T(8,128)(2,1)}, f32[8,128]{1,0:T(8,128)}, f32[1024,128]{1,0:T(8,128)}, f32[1024,128]{1,0:T(8,128)}, f32[1024,128]{1,0:T(8,128)}) custom-call(bf16[8,2,64,128]{3,2,1,0:T(8,128)(2,1)} %copy-done.16, f32[1024,128]{1,0:T(8,128)} %get-tuple-element.183.lin_ref, f32[1032,8]{1,0:T(8,128)} %pad_convert_fusion.flag_ref, ...), custom_call_target="tpu_custom_call" | custom-call | flops 9000000 | bytes 1024 | tf_op jit(solution)/shard_map/mixer_backward_states/pallas_call | solution.py:769
  199.9 2.1 pad_maximum_fusion.6.branch_ref
  202.0 2.9 output_gradient.1
  207.8 4.4 %all-to-all-start.3 = ((bf16[4,2,64,1024]{3,2,1,0:T(8,128)(2,1)}), bf16[4,2,64,1024]{3,2,1,0:T(8,128)(2,1)}, u32[]{:S(2)}, u32[]{:S(2)}) async-start(bf16[4,2,64,1024]{3,2,1,0:T(8,128)(2,1)} %get-tuple-element.243), calls=%async_computation.3 | async-start | bytes 2097152 | tf_op jit(solution)/shard_map/all_to_all | solution.py:1088
  212.4 2.9 collective-permute-start.38
  216.5 10.1 %mixer_backward_tokens.1 = (f32[1032,384]{1,0:T(8,128)}, bf16[1024,128]{1,0:T(8,128)(2,1)}) custom-call(f32[1024,128]{1,0:T(8,128)} %get-tuple-element.242.do_ref, f32[1024,128]{1,0:T(8,128)} %get-tuple-element.244.dpre_ref, f32[1024,128]{1,0:T(8,128)} %get-tuple-element.245.dstate_ref, f32[1032,8]{1,0:T(8,128)} %pad_convert_fusion.flag_ref, ...), custom_call_target="tpu_custom_call" | custom-call | flops 10000000 | bytes 1024 | tf_op jit(solution)/shard_map/mixer_backward_tokens/pallas_call | solution.py:769
  226.7 3.9 %collective-permute-done.38 = bf16[4,32,1408]{2,1,0:T(8,128)(2,1)S(1)} collective-permute-done((bf16[4,32,1408]{2,1,0:T(8,128)(2,1)S(1)}, bf16[4,32,1408]{2,1,0:T(8,128)(2,1)S(1)}, u32[]{:S(2)}, u32[]{:S(2)}) %collective-permute-start.38) | collective-permute-done | bytes 360480 | tf_op jit(solution)/shard_map/ppermute | solution.py:792
  232.9 1.5 convert_reduce_fusion
  234.4 2.1 collective-permute-start.41
  238.6 6.0 %all-to-all-start.4 = ((bf16[4,32,1408]{2,1,0:T(8,128)(2,1)}), bf16[4,32,1408]{2,1,0:T(8,128)(2,1)S(1)}, u32[]{:S(2)}, u32[]{:S(2)}) async-start(bf16[4,32,1408]{2,1,0:T(8,128)(2,1)} %fusion.3), calls=%async_computation.4 | async-start | bytes 720896 | tf_op jit(solution)/shard_map/all_to_all | solution.py:1110
  244.6 10.3 %mixer_backward_taps.1 = (bf16[8,64,1024]{2,1,0:T(8,128)(2,1)}, bf16[8,64,1024]{2,1,0:T(8,128)(2,1)}, bf16[8,64,640]{2,1,0:T(8,128)(2,1)}, bf16[8,64,640]{2,1,0:T(8,128)(2,1)}) custom-call(f32[1032,384]{1,0:T(8,128)} %get-tuple-element.257.du_ref, bf16[1024,128]{1,0:T(8,128)(2,1)} %get-tuple-element.258.dg_ref, bf16[1024,128]{1,0:T(8,128)(2,1)} %get-tuple-element.259.dz_ref, ...), custom_call_target="tpu_custom_call" | custom-call | flops 12000000 | bytes 1024 | tf_op jit(solution)/shard_map/mixer_backward_taps/pallas_call | solution.py:769
  258.3 5.9 %collective-permute-done.44 = bf16[40,1024]{1,0:T(8,128)(2,1)S(1)} collective-permute-done((bf16[40,1024]{1,0:T(8,128)(2,1)S(1)}, bf16[40,1024]{1,0:T(8,128)(2,1)S(1)}, u32[]{:S(2)}, u32[]{:S(2)}) %collective-permute-start.44) | collective-permute-done | bytes 81952 | tf_op jit(solution)/shard_map/ppermute | solution.py:792
  265.1 2.4 merge_heads.1
  268.5 2.7 token_pieces.1
  272.4 2.0 collective-permute-start.45
  274.5 1.5 collective-permute-start.47
  275.9 2.0 spread_pair.1
  277.9 3.9 %collective-permute-done.45.rest_0_ = bf16[2,64,1024]{2,1,0:T(8,128)(2,1)S(1)} collective-permute-done((bf16[2,64,1024]{2,1,0:T(8,128)(2,1)}, bf16[2,64,1024]{2,1,0:T(8,128)(2,1)S(1)}, u32[]{:S(2)}, u32[]{:S(2)}) %collective-permute-start.45) | collective-permute-done | bytes 262176 | tf_op jit(solution)/shard_map/ppermute | solution.py:792
  282.7 2.5 collective-permute-done.47.rest_2_
  285.9 2.6 input_gradient.1
  289.5 3.4 %collective-permute-start.48 = (bf16[64,1024]{1,0:T(8,128)(2,1)S(1)}, bf16[64,1024]{1,0:T(8,128)(2,1)S(1)}, u32[]{:S(2)}, u32[]{:S(2)}) collective-permute-start(bf16[64,1024]{1,0:T(8,128)(2,1)S(1)} %select_bitcast_fusion.14), channel_id=1, source_target_pairs={{0,16},{16,0},{1,17},{17,1},{2,18},{18,2},{3,19},{19,3},{4,20},{20... | collective-permute-start | bytes 393224 | tf_op jit(solution)/shard_map/ppermute | solution.py:792
  293.9 11.9 %collective-permute-done.48 = bf16[64,1024]{1,0:T(8,128)(2,1)S(1)} collective-permute-done((bf16[64,1024]{1,0:T(8,128)(2,1)S(1)}, bf16[64,1024]{1,0:T(8,128)(2,1)S(1)}, u32[]{:S(2)}, u32[]{:S(2)}) %collective-permute-start.48) | collective-permute-done | bytes 131104 | tf_op jit(solution)/shard_map/ppermute | solution.py:792
  305.9 5.3 %collective-permute-done.50 = bf16[4,32,1152]{2,1,0:T(8,128)(2,1)S(1)} collective-permute-done((bf16[4,32,1152]{2,1,0:T(8,128)(2,1)S(1)}, bf16[4,32,1152]{2,1,0:T(8,128)(2,1)S(1)}, u32[]{:S(2)}, u32[]{:S(2)}) %collective-permute-start.50) | collective-permute-done | bytes 294944 | tf_op jit(solution)/shard_map/ppermute | solution.py:792
  316.5 1.6 collective-permute-done.52.refs_2_
  318.1 1.9 collective-permute-done.53.refs_3_
  320.5 1.8 spread_heads.1
  (252 shorter events, 75.5 us)
Async XLA Ops:
  0.6 26.9 %copy-start.21 = (bf16[32,1024]{1,0:T(8,128)(2,1)S(1)}, bf16[32,1024]{1,0:T(8,128)(2,1)}, u32[]{:S(2)}) copy-start(bf16[32,1024]{1,0:T(8,128)(2,1)} %param.24) | copy-start | bytes 196612
  0.7 20.1 %copy-start.38 = (bf16[128]{0:T(256)(128)(2,1)S(1)}, bf16[128]{0:T(256)(128)(2,1)}, u32[]{:S(2)}) copy-start(bf16[128]{0:T(256)(128)(2,1)} %param.30) | copy-start | bytes 772
  6.8 22.5 %copy-start.36 = (bf16[32,1152]{1,0:T(8,128)(2,1)S(1)}, bf16[32,1152]{1,0:T(8,128)(2,1)}, u32[]{:S(2)}) copy-start(bf16[32,1152]{1,0:T(8,128)(2,1)} %get-tuple-element.155) | copy-start | bytes 221188
  6.8 17.1 %collective-permute-start = (bf16[32,1152]{1,0:T(8,128)(2,1)}, bf16[32,1152]{1,0:T(8,128)(2,1)S(1)}, u32[]{:S(2)}, u32[]{:S(2)}) collective-permute-start(bf16[32,1152]{1,0:T(8,128)(2,1)} %get-tuple-element.156), channel_id=1, source_target_pairs={{0,4},{4,0},{8,12},{12,8},{1,5},{5,1},{9,13},{13,9},{2,6},{6,2},{1... | collective-permute-start | bytes 221192 | tf_op jit(solution)/shard_map/ppermute | solution.py:792
  9.7 14.2 %collective-permute-start.1 = (bf16[32,1152]{1,0:T(8,128)(2,1)}, bf16[32,1152]{1,0:T(8,128)(2,1)S(1)}, u32[]{:S(2)}, u32[]{:S(2)}) collective-permute-start(bf16[32,1152]{1,0:T(8,128)(2,1)} %get-tuple-element.157), channel_id=1, source_target_pairs={{0,8},{4,12},{8,0},{12,4},{1,9},{5,13},{9,1},{13,5},{2,10},{6,14},... | collective-permute-start | bytes 221192 | tf_op jit(solution)/shard_map/ppermute | solution.py:792
  11.3 12.6 %collective-permute-start.2 = (bf16[32,1152]{1,0:T(8,128)(2,1)}, bf16[32,1152]{1,0:T(8,128)(2,1)S(1)}, u32[]{:S(2)}, u32[]{:S(2)}) collective-permute-start(bf16[32,1152]{1,0:T(8,128)(2,1)} %get-tuple-element.158), channel_id=1, source_target_pairs={{0,12},{4,8},{8,4},{12,0},{1,13},{5,9},{9,5},{13,1},{2,14},{6,10},... | collective-permute-start | bytes 221192 | tf_op jit(solution)/shard_map/ppermute | solution.py:792
  12.3 11.6 %collective-permute-start.3 = (bf16[64,1024]{1,0:T(8,128)(2,1)S(1)}, bf16[64,1024]{1,0:T(8,128)(2,1)S(1)}, u32[]{:S(2)}, u32[]{:S(2)}) collective-permute-start(bf16[64,1024]{1,0:T(8,128)(2,1)S(1)} %get-tuple-element.371), channel_id=1, source_target_pairs={{0,16},{16,0},{1,17},{17,1},{2,18},{18,2},{3,19},{19,3},{4,20},{20... | collective-permute-start | bytes 393224 | tf_op jit(solution)/shard_map/ppermute | solution.py:792
  15.4 8.5 %collective-permute-start.4 = (bf16[32,1024]{1,0:T(8,128)(2,1)}, bf16[32,1024]{1,0:T(8,128)(2,1)S(1)}, u32[]{:S(2)}, u32[]{:S(2)}) collective-permute-start(bf16[32,1024]{1,0:T(8,128)(2,1)} %param.24), channel_id=1, source_target_pairs={{0,16},{16,0},{1,17},{17,1},{2,18},{18,2},{3,19},{19,3},{4,20},{20... | collective-permute-start | bytes 196616 | tf_op jit(solution)/shard_map/ppermute | solution.py:792
  24.0 20.5 %copy-start.17 = (bf16[2,64,1024]{2,1,0:T(8,128)(2,1)}, bf16[2,64,1024]{2,1,0:T(8,128)(2,1)S(1)}, u32[]{:S(2)}) copy-start(bf16[2,64,1024]{2,1,0:T(8,128)(2,1)S(1)} %get-tuple-element.369.x_ref) | copy-start | bytes 786436
  24.0 8.7 %collective-permute-start.6 = (bf16[2,64,1024]{2,1,0:T(8,128)(2,1)S(1)}, bf16[2,64,1024]{2,1,0:T(8,128)(2,1)S(1)}, u32[]{:S(2)}, u32[]{:S(2)}) collective-permute-start(bf16[2,64,1024]{2,1,0:T(8,128)(2,1)S(1)} %get-tuple-element.369.x_ref), channel_id=1, source_target_pairs={{0,4},{4,0},{8,12},{12,8},{1,5},{5,1},{9,13},{13,9},{2,6},{6,2},{1... | collective-permute-start | bytes 786440 | tf_op jit(solution)/shard_map/ppermute | solution.py:792
  25.4 15.6 %collective-permute-start.7 = (bf16[2,64,1024]{2,1,0:T(8,128)(2,1)S(1)}, bf16[2,64,1024]{2,1,0:T(8,128)(2,1)S(1)}, u32[]{:S(2)}, u32[]{:S(2)}) collective-permute-start(bf16[2,64,1024]{2,1,0:T(8,128)(2,1)S(1)} %get-tuple-element.369.x_ref), channel_id=1, source_target_pairs={{0,8},{4,12},{8,0},{12,4},{1,9},{5,13},{9,1},{13,5},{2,10},{6,14},... | collective-permute-start | bytes 786440 | tf_op jit(solution)/shard_map/ppermute | solution.py:792
  26.1 18.4 %collective-permute-start.8 = (bf16[2,64,1024]{2,1,0:T(8,128)(2,1)S(1)}, bf16[2,64,1024]{2,1,0:T(8,128)(2,1)S(1)}, u32[]{:S(2)}, u32[]{:S(2)}) collective-permute-start(bf16[2,64,1024]{2,1,0:T(8,128)(2,1)S(1)} %get-tuple-element.369.x_ref), channel_id=1, source_target_pairs={{0,12},{4,8},{8,4},{12,0},{1,13},{5,9},{9,5},{13,1},{2,14},{6,10},... | collective-permute-start | bytes 786440 | tf_op jit(solution)/shard_map/ppermute | solution.py:792
  27.5 5.0 %collective-permute-start.9 = (bf16[2,32,1024]{2,1,0:T(8,128)(2,1)S(1)}, bf16[2,32,1024]{2,1,0:T(8,128)(2,1)S(1)}, u32[]{:S(2)}, u32[]{:S(2)}) collective-permute-start(bf16[2,32,1024]{2,1,0:T(8,128)(2,1)S(1)} %pad_maximum_fusion.17), channel_id=1, source_target_pairs={{0,1},{1,0},{2,3},{3,2},{4,5},{5,4},{6,7},{7,6},{8,9},{9,8},{10,11... | collective-permute-start | bytes 393224 | tf_op jit(solution)/shard_map/ppermute | solution.py:792
  29.4 15.3 %collective-permute-start.5 = (bf16[4,32,1152]{2,1,0:T(8,128)(2,1)S(1)}, bf16[4,32,1152]{2,1,0:T(8,128)(2,1)S(1)}, u32[]{:S(2)}, u32[]{:S(2)}) collective-permute-start(bf16[4,32,1152]{2,1,0:T(8,128)(2,1)S(1)} %get-tuple-element.361), channel_id=1, source_target_pairs={{0,16},{16,0},{1,17},{17,1},{2,18},{18,2},{3,19},{19,3},{4,20},{20... | collective-permute-start | bytes 884744 | tf_op jit(solution)/shard_map/ppermute | solution.py:792
  44.7 15.1 %collective-permute-start.10 = (bf16[8,32,1152]{2,1,0:T(8,128)(2,1)S(1)}, bf16[8,32,1152]{2,1,0:T(8,128)(2,1)S(1)}, u32[]{:S(2)}, u32[]{:S(2)}) collective-permute-start(bf16[8,32,1152]{2,1,0:T(8,128)(2,1)S(1)} %bitcast.259), channel_id=1, source_target_pairs={{0,1},{1,0},{2,3},{3,2},{4,5},{5,4},{6,7},{7,6},{8,9},{9,8},{10,11... | collective-permute-start | bytes 1769480 | tf_op jit(solution)/shard_map/ppermute | solution.py:792
  50.6 16.7 %collective-permute-start.11 = (bf16[4,2,64,1024]{3,2,1,0:T(8,128)(2,1)S(1)}, bf16[4,2,64,1024]{3,2,1,0:T(8,128)(2,1)}, u32[]{:S(2)}, u32[]{:S(2)}) collective-permute-start(bf16[4,2,64,1024]{3,2,1,0:T(8,128)(2,1)S(1)} %pad_maximum_fusion.3.xown_ref), channel_id=1, source_target_pairs={{0,2},{2,0},{1,3},{3,1},{4,6},{6,4},{5,7},{7,5},{8,10},{10,8},{9,1... | collective-permute-start | bytes 3145736 | tf_op jit(solution)/shard_map/ppermute | solution.py:792
  52.3 15.1 %all-to-all-start = ((bf16[4,32,1408]{2,1,0:T(8,128)(2,1)}), bf16[4,32,1408]{2,1,0:T(8,128)(2,1)S(1)}, u32[]{:S(2)}, u32[]{:S(2)}) async-start(bf16[4,32,1408]{2,1,0:T(8,128)(2,1)} %reshape.474), calls=%async_computation | async-start | bytes 720896 | tf_op jit(solution)/shard_map/all_to_all | solution.py:929
  57.0 7.6 %collective-permute-start.12 = (bf16[64,1024]{1,0:T(8,128)(2,1)}, bf16[64,1024]{1,0:T(8,128)(2,1)}, u32[]{:S(2)}, u32[]{:S(2)}) collective-permute-start(bf16[64,1024]{1,0:T(8,128)(2,1)} %get-tuple-element.166), channel_id=1, source_target_pairs={{0,16},{16,0},{1,17},{17,1},{2,18},{18,2},{3,19},{19,3},{4,20},{20... | collective-permute-start | bytes 393224 | tf_op jit(solution)/shard_map/ppermute | solution.py:792
  67.5 6.5 %collective-permute-start.17 = (bf16[8,64,640]{2,1,0:T(8,128)(2,1)S(1)}, bf16[8,64,640]{2,1,0:T(8,128)(2,1)S(1)}, u32[]{:S(2)}, u32[]{:S(2)}) collective-permute-start(bf16[8,64,640]{2,1,0:T(8,128)(2,1)S(1)} %pad_maximum_fusion.9), channel_id=1, source_target_pairs={{0,2},{2,0},{1,3},{3,1},{4,6},{6,4},{5,7},{7,5},{8,10},{10,8},{9,1... | collective-permute-start | bytes 1966088 | tf_op jit(solution)/shard_map/ppermute | solution.py:792
  67.6 25.9 %collective-permute-start.13 = (bf16[4,32,1408]{2,1,0:T(8,128)(2,1)S(1)}, bf16[4,32,1408]{2,1,0:T(8,128)(2,1)S(1)}, u32[]{:S(2)}, u32[]{:S(2)}) collective-permute-start(bf16[4,32,1408]{2,1,0:T(8,128)(2,1)S(1)} %all-to-all-done), channel_id=1, source_target_pairs={{0,16},{16,0},{1,17},{17,1},{2,18},{18,2},{3,19},{19,3},{4,20},{20... | collective-permute-start | bytes 1081352 | tf_op jit(solution)/shard_map/ppermute | solution.py:792
  68.3 25.1 %collective-permute-start.14 = (bf16[2,64,1024]{2,1,0:T(8,128)(2,1)S(1)}, bf16[2,64,1024]{2,1,0:T(8,128)(2,1)}, u32[]{:S(2)}, u32[]{:S(2)}) collective-permute-start(bf16[2,64,1024]{2,1,0:T(8,128)(2,1)S(1)} %bitcast.264), channel_id=1, source_target_pairs={{0,4},{4,0},{8,12},{12,8},{1,5},{5,1},{9,13},{13,9},{2,6},{6,2},{1... | collective-permute-start | bytes 786440 | tf_op jit(solution)/shard_map/ppermute | solution.py:792
  70.1 23.4 %collective-permute-start.15 = (bf16[2,64,1024]{2,1,0:T(8,128)(2,1)S(1)}, bf16[2,64,1024]{2,1,0:T(8,128)(2,1)}, u32[]{:S(2)}, u32[]{:S(2)}) collective-permute-start(bf16[2,64,1024]{2,1,0:T(8,128)(2,1)S(1)} %bitcast.265), channel_id=1, source_target_pairs={{0,8},{4,12},{8,0},{12,4},{1,9},{5,13},{9,1},{13,5},{2,10},{6,14},... | collective-permute-start | bytes 786440 | tf_op jit(solution)/shard_map/ppermute | solution.py:792
  73.0 20.5 %collective-permute-start.16 = (bf16[2,64,1024]{2,1,0:T(8,128)(2,1)S(1)}, bf16[2,64,1024]{2,1,0:T(8,128)(2,1)}, u32[]{:S(2)}, u32[]{:S(2)}) collective-permute-start(bf16[2,64,1024]{2,1,0:T(8,128)(2,1)S(1)} %bitcast.266), channel_id=1, source_target_pairs={{0,12},{4,8},{8,4},{12,0},{1,13},{5,9},{9,5},{13,1},{2,14},{6,10},... | collective-permute-start | bytes 786440 | tf_op jit(solution)/shard_map/ppermute | solution.py:792
  93.6 17.7 %collective-permute-start.18 = (bf16[8,32,1408]{2,1,0:T(8,128)(2,1)S(1)}, bf16[8,32,1408]{2,1,0:T(8,128)(2,1)S(1)}, u32[]{:S(2)}, u32[]{:S(2)}) collective-permute-start(bf16[8,32,1408]{2,1,0:T(8,128)(2,1)S(1)} %bitcast.258), channel_id=1, source_target_pairs={{0,1},{1,0},{2,3},{3,2},{4,5},{5,4},{6,7},{7,6},{8,9},{9,8},{10,11... | collective-permute-start | bytes 2162696 | tf_op jit(solution)/shard_map/ppermute | solution.py:792
  96.0 17.8 %collective-permute-start.20 = (bf16[2,64,1024]{2,1,0:T(8,128)(2,1)S(1)}, bf16[2,64,1024]{2,1,0:T(8,128)(2,1)S(1)}, u32[]{:S(2)}, u32[]{:S(2)}) collective-permute-start(bf16[2,64,1024]{2,1,0:T(8,128)(2,1)S(1)} %get-tuple-element.196), channel_id=1, source_target_pairs={{0,4},{4,0},{8,12},{12,8},{1,5},{5,1},{9,13},{13,9},{2,6},{6,2},{1... | collective-permute-start | bytes 786440 | tf_op jit(solution)/shard_map/ppermute | solution.py:792
  97.5 16.3 %collective-permute-start.21 = (bf16[2,64,1024]{2,1,0:T(8,128)(2,1)S(1)}, bf16[2,64,1024]{2,1,0:T(8,128)(2,1)S(1)}, u32[]{:S(2)}, u32[]{:S(2)}) collective-permute-start(bf16[2,64,1024]{2,1,0:T(8,128)(2,1)S(1)} %get-tuple-element.196), channel_id=1, source_target_pairs={{0,8},{4,12},{8,0},{12,4},{1,9},{5,13},{9,1},{13,5},{2,10},{6,14},... | collective-permute-start | bytes 786440 | tf_op jit(solution)/shard_map/ppermute | solution.py:792
  99.5 15.0 %collective-permute-start.22 = (bf16[2,64,1024]{2,1,0:T(8,128)(2,1)S(1)}, bf16[2,64,1024]{2,1,0:T(8,128)(2,1)S(1)}, u32[]{:S(2)}, u32[]{:S(2)}) collective-permute-start(bf16[2,64,1024]{2,1,0:T(8,128)(2,1)S(1)} %get-tuple-element.196), channel_id=1, source_target_pairs={{0,12},{4,8},{8,4},{12,0},{1,13},{5,9},{9,5},{13,1},{2,14},{6,10},... | collective-permute-start | bytes 786440 | tf_op jit(solution)/shard_map/ppermute | solution.py:792
  100.8 26.4 %copy-start.8 = (bf16[4,2,64,1024]{3,2,1,0:T(8,128)(2,1)}, bf16[4,2,64,1024]{3,2,1,0:T(8,128)(2,1)S(1)}, u32[]{:S(2)}) copy-start(bf16[4,2,64,1024]{3,2,1,0:T(8,128)(2,1)S(1)} %pad_maximum_fusion.4.oown_ref) | copy-start | bytes 3145732
  100.8 13.0 %collective-permute-start.19 = (bf16[88,1024]{1,0:T(8,128)(2,1)S(1)}, bf16[88,1024]{1,0:T(8,128)(2,1)S(1)}, u32[]{:S(2)}, u32[]{:S(2)}) collective-permute-start(bf16[88,1024]{1,0:T(8,128)(2,1)S(1)} %copy-done.32), channel_id=1, source_target_pairs={{0,16},{16,0},{1,17},{17,1},{2,18},{18,2},{3,19},{19,3},{4,20},{20... | collective-permute-start | bytes 540680 | tf_op jit(solution)/shard_map/ppermute | solution.py:792
  116.1 9.0 %collective-permute-start.25 = (bf16[2,88,1024]{2,1,0:T(8,128)(2,1)}, bf16[2,88,1024]{2,1,0:T(8,128)(2,1)}, u32[]{:S(2)}, u32[]{:S(2)}) collective-permute-start(bf16[2,88,1024]{2,1,0:T(8,128)(2,1)} %pad_maximum_fusion.12), channel_id=1, source_target_pairs={{0,1},{1,0},{2,3},{3,2},{4,5},{5,4},{6,7},{7,6},{8,9},{9,8},{10,11... | collective-permute-start | bytes 1081352 | tf_op jit(solution)/shard_map/ppermute | solution.py:792
  117.1 18.1 %all-to-all-start.1 = ((bf16[8,512,128]{2,1,0:T(8,128)(2,1)}), bf16[8,512,128]{2,1,0:T(8,128)(2,1)S(1)}, u32[]{:S(2)}, u32[]{:S(2)}) async-start(bf16[8,512,128]{2,1,0:T(8,128)(2,1)} %bitcast.263), calls=%async_computation.1 | async-start | bytes 2097152 | tf_op jit(solution)/shard_map/all_to_all | solution.py:978
  120.9 14.4 %collective-permute-start.24 = (bf16[2,4,64,1408]{3,2,1,0:T(8,128)(2,1)S(1)}, bf16[2,4,64,1408]{3,2,1,0:T(8,128)(2,1)}, u32[]{:S(2)}, u32[]{:S(2)}) collective-permute-start(bf16[2,4,64,1408]{3,2,1,0:T(8,128)(2,1)S(1)} %bitcast.254), channel_id=1, source_target_pairs={{0,2},{2,0},{1,3},{3,1},{4,6},{6,4},{5,7},{7,5},{8,10},{10,8},{9,1... | collective-permute-start | bytes 4325384 | tf_op jit(solution)/shard_map/ppermute | solution.py:792
  127.2 3.5 %collective-permute-start.26 = (bf16[2,176,1024]{2,1,0:T(8,128)(2,1)}, bf16[2,176,1024]{2,1,0:T(8,128)(2,1)}, u32[]{:S(2)}, u32[]{:S(2)}) collective-permute-start(bf16[2,176,1024]{2,1,0:T(8,128)(2,1)} %bitcast.64), channel_id=1, source_target_pairs={{0,2},{2,0},{1,3},{3,1},{4,6},{6,4},{5,7},{7,5},{8,10},{10,8},{9,1... | collective-permute-start | bytes 2162696 | tf_op jit(solution)/shard_map/ppermute | solution.py:792
  127.2 6.3 %collective-permute-start.23 = (bf16[4,2,64,1024]{3,2,1,0:T(8,128)(2,1)S(1)}, bf16[4,2,64,1024]{3,2,1,0:T(8,128)(2,1)}, u32[]{:S(2)}, u32[]{:S(2)}) collective-permute-start(bf16[4,2,64,1024]{3,2,1,0:T(8,128)(2,1)S(1)} %pad_maximum_fusion.4.oown_ref), channel_id=1, source_target_pairs={{0,2},{2,0},{1,3},{3,1},{4,6},{6,4},{5,7},{7,5},{8,10},{10,8},{9,1... | collective-permute-start | bytes 3145736 | tf_op jit(solution)/shard_map/ppermute | solution.py:792
  147.8 10.6 %collective-permute-start.27 = (bf16[2,64,1024]{2,1,0:T(8,128)(2,1)}, bf16[2,64,1024]{2,1,0:T(8,128)(2,1)S(1)}, u32[]{:S(2)}, u32[]{:S(2)}) collective-permute-start(bf16[2,64,1024]{2,1,0:T(8,128)(2,1)} %get-tuple-element.203), channel_id=1, source_target_pairs={{0,4},{4,0},{8,12},{12,8},{1,5},{5,1},{9,13},{13,9},{2,6},{6,2},{1... | collective-permute-start | bytes 786440 | tf_op jit(solution)/shard_map/ppermute | solution.py:792
  149.3 9.5 %collective-permute-start.28 = (bf16[2,64,1024]{2,1,0:T(8,128)(2,1)}, bf16[2,64,1024]{2,1,0:T(8,128)(2,1)S(1)}, u32[]{:S(2)}, u32[]{:S(2)}) collective-permute-start(bf16[2,64,1024]{2,1,0:T(8,128)(2,1)} %get-tuple-element.204), channel_id=1, source_target_pairs={{0,8},{4,12},{8,0},{12,4},{1,9},{5,13},{9,1},{13,5},{2,10},{6,14},... | collective-permute-start | bytes 786440 | tf_op jit(solution)/shard_map/ppermute | solution.py:792
  149.9 12.8 %collective-permute-start.29 = (bf16[2,64,1024]{2,1,0:T(8,128)(2,1)}, bf16[2,64,1024]{2,1,0:T(8,128)(2,1)S(1)}, u32[]{:S(2)}, u32[]{:S(2)}) collective-permute-start(bf16[2,64,1024]{2,1,0:T(8,128)(2,1)} %get-tuple-element.205), channel_id=1, source_target_pairs={{0,12},{4,8},{8,4},{12,0},{1,13},{5,9},{9,5},{13,1},{2,14},{6,10},... | collective-permute-start | bytes 786440 | tf_op jit(solution)/shard_map/ppermute | solution.py:792
  162.7 14.7 %collective-permute-start.30 = (bf16[8,64,1408]{2,1,0:T(8,128)(2,1)}, bf16[8,64,1408]{2,1,0:T(8,128)(2,1)}, u32[]{:S(2)}, u32[]{:S(2)}) collective-permute-start(bf16[8,64,1408]{2,1,0:T(8,128)(2,1)} %get-tuple-element.223), channel_id=1, source_target_pairs={{0,2},{2,0},{1,3},{3,1},{4,6},{6,4},{5,7},{7,5},{8,10},{10,8},{9,1... | collective-permute-start | bytes 4325384 | tf_op jit(solution)/shard_map/ppermute | solution.py:792
  164.4 11.7 %collective-permute-start.31 = (bf16[2,2,88,1024]{3,2,0,1:T(8,128)(2,1)S(1)}, bf16[2,2,88,1024]{3,2,0,1:T(8,128)(2,1)S(1)}, u32[]{:S(2)}, u32[]{:S(2)}) collective-permute-start(bf16[2,2,88,1024]{3,2,0,1:T(8,128)(2,1)S(1)} %select_bitcast_fusion), channel_id=1, source_target_pairs={{0,2},{2,0},{1,3},{3,1},{4,6},{6,4},{5,7},{7,5},{8,10},{10,8},{9,1... | collective-permute-start | bytes 2162696 | tf_op jit(solution)/shard_map/ppermute | solution.py:792
  169.0 28.3 %collective-permute-start.33 = (bf16[2,64,1024]{2,1,0:T(8,128)(2,1)}, bf16[2,64,1024]{2,1,0:T(8,128)(2,1)S(1)}, u32[]{:S(2)}, u32[]{:S(2)}) collective-permute-start(bf16[2,64,1024]{2,1,0:T(8,128)(2,1)} %get-tuple-element.226), channel_id=1, source_target_pairs={{0,4},{4,0},{8,12},{12,8},{1,5},{5,1},{9,13},{13,9},{2,6},{6,2},{1... | collective-permute-start | bytes 786440 | tf_op jit(solution)/shard_map/ppermute | solution.py:792
  170.5 26.8 %collective-permute-start.34 = (bf16[2,64,1024]{2,1,0:T(8,128)(2,1)}, bf16[2,64,1024]{2,1,0:T(8,128)(2,1)}, u32[]{:S(2)}, u32[]{:S(2)}) collective-permute-start(bf16[2,64,1024]{2,1,0:T(8,128)(2,1)} %get-tuple-element.226), channel_id=1, source_target_pairs={{0,8},{4,12},{8,0},{12,4},{1,9},{5,13},{9,1},{13,5},{2,10},{6,14},... | collective-permute-start | bytes 786440 | tf_op jit(solution)/shard_map/ppermute | solution.py:792
  171.0 26.3 %collective-permute-start.35 = (bf16[2,64,1024]{2,1,0:T(8,128)(2,1)}, bf16[2,64,1024]{2,1,0:T(8,128)(2,1)}, u32[]{:S(2)}, u32[]{:S(2)}) collective-permute-start(bf16[2,64,1024]{2,1,0:T(8,128)(2,1)} %get-tuple-element.226), channel_id=1, source_target_pairs={{0,12},{4,8},{8,4},{12,0},{1,13},{5,9},{9,5},{13,1},{2,14},{6,10},... | collective-permute-start | bytes 786440 | tf_op jit(solution)/shard_map/ppermute | solution.py:792
  172.5 14.7 %all-to-all-start.2 = ((bf16[8,2,64,128]{3,2,1,0:T(8,128)(2,1)}), bf16[8,2,64,128]{3,2,1,0:T(8,128)(2,1)S(1)}, u32[]{:S(2)}, u32[]{:S(2)}) async-start(bf16[8,2,64,128]{3,2,1,0:T(8,128)(2,1)} %get-tuple-element.221), calls=%async_computation.2 | async-start | bytes 524288 | tf_op jit(solution)/shard_map/all_to_all | solution.py:1043
  187.4 19.1 %collective-permute-start.32 = (bf16[8,1,32,1408]{3,2,0,1:T(8,128)(2,1)S(1)}, bf16[8,1,32,1408]{3,2,0,1:T(8,128)(2,1)S(1)}, u32[]{:S(2)}, u32[]{:S(2)}) collective-permute-start(bf16[8,1,32,1408]{3,2,0,1:T(8,128)(2,1)S(1)} %fusion.1), channel_id=1, source_target_pairs={{0,1},{1,0},{2,3},{3,2},{4,5},{5,4},{6,7},{7,6},{8,9},{9,8},{10,11... | collective-permute-start | bytes 2162696 | tf_op jit(solution)/shard_map/ppermute | solution.py:792
  198.8 16.5 %collective-permute-start.37 = (bf16[2,1,88,1024]{3,2,0,1:T(8,128)(2,1)}, bf16[2,1,88,1024]{3,2,0,1:T(8,128)(2,1)}, u32[]{:S(2)}, u32[]{:S(2)}) collective-permute-start(bf16[2,1,88,1024]{3,2,0,1:T(8,128)(2,1)} %select_bitcast_fusion.8), channel_id=1, source_target_pairs={{0,1},{1,0},{2,3},{3,2},{4,5},{5,4},{6,7},{7,6},{8,9},{9,8},{10,11... | collective-permute-start | bytes 1081352 | tf_op jit(solution)/shard_map/ppermute | solution.py:792
  207.8 25.1 %all-to-all-start.3 = ((bf16[4,2,64,1024]{3,2,1,0:T(8,128)(2,1)}), bf16[4,2,64,1024]{3,2,1,0:T(8,128)(2,1)}, u32[]{:S(2)}, u32[]{:S(2)}) async-start(bf16[4,2,64,1024]{3,2,1,0:T(8,128)(2,1)} %get-tuple-element.243), calls=%async_computation.3 | async-start | bytes 2097152 | tf_op jit(solution)/shard_map/all_to_all | solution.py:1088
  212.2 14.3 %collective-permute-start.36 = (bf16[2,2,40,1024]{3,2,0,1:T(8,128)(2,1)S(1)}, bf16[2,2,40,1024]{3,2,0,1:T(8,128)(2,1)S(1)}, u32[]{:S(2)}, u32[]{:S(2)}) collective-permute-start(bf16[2,2,40,1024]{3,2,0,1:T(8,128)(2,1)S(1)} %select_bitcast_fusion.11), channel_id=1, source_target_pairs={{0,2},{2,0},{1,3},{3,1},{4,6},{6,4},{5,7},{7,5},{8,10},{10,8},{9,1... | collective-permute-start | bytes 983048 | tf_op jit(solution)/shard_map/ppermute | solution.py:792
  212.4 18.2 %collective-permute-start.38 = (bf16[4,32,1408]{2,1,0:T(8,128)(2,1)S(1)}, bf16[4,32,1408]{2,1,0:T(8,128)(2,1)S(1)}, u32[]{:S(2)}, u32[]{:S(2)}) collective-permute-start(bf16[4,32,1408]{2,1,0:T(8,128)(2,1)S(1)} %fusion.5), channel_id=1, source_target_pairs={{0,16},{16,0},{1,17},{17,1},{2,18},{18,2},{3,19},{19,3},{4,20},{20... | collective-permute-start | bytes 1081352 | tf_op jit(solution)/shard_map/ppermute | solution.py:792
  234.4 20.5 %collective-permute-start.41 = (bf16[64,1024]{1,0:T(8,128)(2,1)S(1)}, bf16[64,1024]{1,0:T(8,128)(2,1)S(1)}, u32[]{:S(2)}, u32[]{:S(2)}) collective-permute-start(bf16[64,1024]{1,0:T(8,128)(2,1)S(1)} %select_bitcast_fusion.15), channel_id=1, source_target_pairs={{0,16},{16,0},{1,17},{17,1},{2,18},{18,2},{3,19},{19,3},{4,20},{20... | collective-permute-start | bytes 393224 | tf_op jit(solution)/shard_map/ppermute | solution.py:792
  236.6 19.1 %collective-permute-start.40 = (bf16[88,1024]{1,0:T(8,128)(2,1)S(1)}, bf16[88,1024]{1,0:T(8,128)(2,1)S(1)}, u32[]{:S(2)}, u32[]{:S(2)}) collective-permute-start(bf16[88,1024]{1,0:T(8,128)(2,1)S(1)} %fusion.8), channel_id=1, source_target_pairs={{0,16},{16,0},{1,17},{17,1},{2,18},{18,2},{3,19},{19,3},{4,20},{20... | collective-permute-start | bytes 540680 | tf_op jit(solution)/shard_map/ppermute | solution.py:792
  237.6 18.1 %collective-permute-start.39 = (bf16[2,1,40,1024]{3,2,0,1:T(8,128)(2,1)S(1)}, bf16[2,1,40,1024]{3,2,0,1:T(8,128)(2,1)S(1)}, u32[]{:S(2)}, u32[]{:S(2)}) collective-permute-start(bf16[2,1,40,1024]{3,2,0,1:T(8,128)(2,1)S(1)} %fusion.9), channel_id=1, source_target_pairs={{0,1},{1,0},{2,3},{3,2},{4,5},{5,4},{6,7},{7,6},{8,9},{9,8},{10,11... | collective-permute-start | bytes 491528 | tf_op jit(solution)/shard_map/ppermute | solution.py:792
  238.6 17.9 %all-to-all-start.4 = ((bf16[4,32,1408]{2,1,0:T(8,128)(2,1)}), bf16[4,32,1408]{2,1,0:T(8,128)(2,1)S(1)}, u32[]{:S(2)}, u32[]{:S(2)}) async-start(bf16[4,32,1408]{2,1,0:T(8,128)(2,1)} %fusion.3), calls=%async_computation.4 | async-start | bytes 720896 | tf_op jit(solution)/shard_map/all_to_all | solution.py:1110
  256.5 11.0 %collective-permute-start.42 = (bf16[8,64,1024]{2,1,0:T(8,128)(2,1)}, bf16[8,64,1024]{2,1,0:T(8,128)(2,1)S(1)}, u32[]{:S(2)}, u32[]{:S(2)}) collective-permute-start(bf16[8,64,1024]{2,1,0:T(8,128)(2,1)} %get-tuple-element.270), channel_id=1, source_target_pairs={{0,2},{2,0},{1,3},{3,1},{4,6},{6,4},{5,7},{7,5},{8,10},{10,8},{9,1... | collective-permute-start | bytes 3145736 | tf_op jit(solution)/shard_map/ppermute | solution.py:792
  256.5 7.7 %collective-permute-start.43 = (bf16[8,64,640]{2,1,0:T(8,128)(2,1)S(1)}, bf16[8,64,640]{2,1,0:T(8,128)(2,1)S(1)}, u32[]{:S(2)}, u32[]{:S(2)}) collective-permute-start(bf16[8,64,640]{2,1,0:T(8,128)(2,1)S(1)} %copy-done.37), channel_id=1, source_target_pairs={{0,2},{2,0},{1,3},{3,1},{4,6},{6,4},{5,7},{7,5},{8,10},{10,8},{9,1... | collective-permute-start | bytes 1966088 | tf_op jit(solution)/shard_map/ppermute | solution.py:792
  257.1 7.2 %collective-permute-start.44 = (bf16[40,1024]{1,0:T(8,128)(2,1)S(1)}, bf16[40,1024]{1,0:T(8,128)(2,1)S(1)}, u32[]{:S(2)}, u32[]{:S(2)}) collective-permute-start(bf16[40,1024]{1,0:T(8,128)(2,1)S(1)} %fusion.22), channel_id=1, source_target_pairs={{0,16},{16,0},{1,17},{17,1},{2,18},{18,2},{3,19},{19,3},{4,20},{20... | collective-permute-start | bytes 245768 | tf_op jit(solution)/shard_map/ppermute | solution.py:792
  271.3 21.5 %collective-permute-start.49 = (bf16[8,1,32,1152]{3,2,0,1:T(8,128)(2,1)S(1)}, bf16[8,1,32,1152]{3,2,0,1:T(8,128)(2,1)S(1)}, u32[]{:S(2)}, u32[]{:S(2)}) collective-permute-start(bf16[8,1,32,1152]{3,2,0,1:T(8,128)(2,1)S(1)} %select_bitcast_fusion.5), channel_id=1, source_target_pairs={{0,1},{1,0},{2,3},{3,2},{4,5},{5,4},{6,7},{7,6},{8,9},{9,8},{10,11... | collective-permute-start | bytes 1769480 | tf_op jit(solution)/shard_map/ppermute | solution.py:792
  272.4 9.4 %collective-permute-start.45 = (bf16[2,64,1024]{2,1,0:T(8,128)(2,1)}, bf16[2,64,1024]{2,1,0:T(8,128)(2,1)S(1)}, u32[]{:S(2)}, u32[]{:S(2)}) collective-permute-start(bf16[2,64,1024]{2,1,0:T(8,128)(2,1)} %get-tuple-element.278), channel_id=1, source_target_pairs={{0,4},{4,0},{8,12},{12,8},{1,5},{5,1},{9,13},{13,9},{2,6},{6,2},{1... | collective-permute-start | bytes 786440 | tf_op jit(solution)/shard_map/ppermute | solution.py:792
  274.5 8.2 %collective-permute-start.46 = (bf16[2,64,1024]{2,1,0:T(8,128)(2,1)}, bf16[2,64,1024]{2,1,0:T(8,128)(2,1)S(1)}, u32[]{:S(2)}, u32[]{:S(2)}) collective-permute-start(bf16[2,64,1024]{2,1,0:T(8,128)(2,1)} %get-tuple-element.279), channel_id=1, source_target_pairs={{0,8},{4,12},{8,0},{12,4},{1,9},{5,13},{9,1},{13,5},{2,10},{6,14},... | collective-permute-start | bytes 786440 | tf_op jit(solution)/shard_map/ppermute | solution.py:792
  274.5 10.8 %collective-permute-start.47 = (bf16[2,64,1024]{2,1,0:T(8,128)(2,1)}, bf16[2,64,1024]{2,1,0:T(8,128)(2,1)S(1)}, u32[]{:S(2)}, u32[]{:S(2)}) collective-permute-start(bf16[2,64,1024]{2,1,0:T(8,128)(2,1)} %get-tuple-element.280), channel_id=1, source_target_pairs={{0,12},{4,8},{8,4},{12,0},{1,13},{5,9},{9,5},{13,1},{2,14},{6,10},... | collective-permute-start | bytes 786440 | tf_op jit(solution)/shard_map/ppermute | solution.py:792
  289.5 16.4 %collective-permute-start.48 = (bf16[64,1024]{1,0:T(8,128)(2,1)S(1)}, bf16[64,1024]{1,0:T(8,128)(2,1)S(1)}, u32[]{:S(2)}, u32[]{:S(2)}) collective-permute-start(bf16[64,1024]{1,0:T(8,128)(2,1)S(1)} %select_bitcast_fusion.14), channel_id=1, source_target_pairs={{0,16},{16,0},{1,17},{17,1},{2,18},{18,2},{3,19},{19,3},{4,20},{20... | collective-permute-start | bytes 393224 | tf_op jit(solution)/shard_map/ppermute | solution.py:792
  293.1 18.0 %collective-permute-start.50 = (bf16[4,32,1152]{2,1,0:T(8,128)(2,1)S(1)}, bf16[4,32,1152]{2,1,0:T(8,128)(2,1)S(1)}, u32[]{:S(2)}, u32[]{:S(2)}) collective-permute-start(bf16[4,32,1152]{2,1,0:T(8,128)(2,1)S(1)} %fusion.7), channel_id=1, source_target_pairs={{0,16},{16,0},{1,17},{17,1},{2,18},{18,2},{3,19},{19,3},{4,20},{20... | collective-permute-start | bytes 884744 | tf_op jit(solution)/shard_map/ppermute | solution.py:792
  311.9 4.6 %collective-permute-start.51 = (bf16[40,1152]{1,0:T(8,128)(2,1)S(1)}, bf16[40,1152]{1,0:T(8,128)(2,1)S(1)}, u32[]{:S(2)}, u32[]{:S(2)}) collective-permute-start(bf16[40,1152]{1,0:T(8,128)(2,1)S(1)} %get-tuple-element.356), channel_id=1, source_target_pairs={{0,4},{4,0},{8,12},{12,8},{1,5},{5,1},{9,13},{13,9},{2,6},{6,2},{1... | collective-permute-start | bytes 276488 | tf_op jit(solution)/shard_map/ppermute | solution.py:792
  313.3 4.7 %collective-permute-start.52 = (bf16[40,1152]{1,0:T(8,128)(2,1)S(1)}, bf16[40,1152]{1,0:T(8,128)(2,1)S(1)}, u32[]{:S(2)}, u32[]{:S(2)}) collective-permute-start(bf16[40,1152]{1,0:T(8,128)(2,1)S(1)} %get-tuple-element.357), channel_id=1, source_target_pairs={{0,8},{4,12},{8,0},{12,4},{1,9},{5,13},{9,1},{13,5},{2,10},{6,14},... | collective-permute-start | bytes 276488 | tf_op jit(solution)/shard_map/ppermute | solution.py:792
  314.0 5.9 %collective-permute-start.53 = (bf16[40,1152]{1,0:T(8,128)(2,1)S(1)}, bf16[40,1152]{1,0:T(8,128)(2,1)S(1)}, u32[]{:S(2)}, u32[]{:S(2)}) collective-permute-start(bf16[40,1152]{1,0:T(8,128)(2,1)S(1)} %get-tuple-element.354), channel_id=1, source_target_pairs={{0,12},{4,8},{8,4},{12,0},{1,13},{5,9},{9,5},{13,1},{2,14},{6,10},... | collective-permute-start | bytes 276488 | tf_op jit(solution)/shard_map/ppermute | solution.py:792
  (34 other events, 148.2 us)
where the time goes:
time: 330 us; the launch traced here: 325 us
  Pallas kernels  95.3 us (29%)
  starting transfers between devices  84.4 us (26%)
  waiting for transfers between devices  84.4 us (26%)
  other arithmetic  37.6 us (11%)
  local copies, waits for them, and re-layouts  21.8 us (7%)
    pallas_call x15, Pallas kernels, run_kernel(): pl.pallas_call(body, name=name, out_shape=[jax.ShapeDtypeStruct(*s) for s...  95.3 us
    ppermute x54, waiting for transfers between devices, swap(): lax.ppermute(value, axis, [(i, i ^ mask) for i in range(lax.axis_size(axi...  70.6 us
    ppermute x54, starting transfers between devices, swap(): lax.ppermute(value, axis, [(i, i ^ mask) for i in range(lax.axis_size(axi...  62.1 us
    unnamed x83, local copies, waits for them, and re-layouts  9.23 us
    all_to_all x1, waiting for transfers between devices, on_device(): dheads = lax.all_to_all(grad_heads, ('q', 'c'), 0, 0, tiled=True)  8 us
  transfers between devices with their start and end apart: 59, of which 27 were waited for; matrix products, arithmetic and copies ran while one was open for 13% of the time, Pallas kernels for 24%

commit v1 on v0

--- a/solution.py
+++ b/solution.py
@@ -14,7 +14,9 @@
 UNIT_EPSILON = 1e-06
 CHUNK = 128
 GROUP = 4
+FREE = 24
 COST = 10**6
+VMEM_BYTES = 56 * 1024 * 1024
 F32 = jnp.float32
 BF16 = jnp.bfloat16
 NN = (((1,), (0,)), ((), ()))
@@ -68,6 +70,10 @@
     return inverse
 
 
+def views(ref):
+    return [ref.at[i] for i in range(ref.shape[0])]
+
+
 def place_of(pos_ref):
     return (pos_ref[0], pos_ref[1], pos_ref[2], pos_ref[3])
 
@@ -76,20 +82,40 @@
     return pos_ref[2] * (HEADS // 2) + pos_ref[1] // (chips // (HEADS // 2))
 
 
-def pack_heads(pos_ref, wq_ref, wk_ref, wv_ref, wg_ref, small_ref, *out_refs):
+def pack_heads(
+    pos_ref, wq_ref, wk_ref, wv_ref, wg_ref, beta_ref, mixer_ref, swiglu_ref, conv_ref, *refs
+):
+    *out_refs, here_ref, side_ref, sems = refs
     chips = len(out_refs)
     repeat = chips // (HEADS // 2)
-    for d, out_ref in enumerate(out_refs):
-        slot = (pos_ref[1] ^ d) // repeat
-        for i in range(2):
-            cols = pl.ds(pl.multiple_of((i * (HEADS // 2) + slot) * HEAD, HEAD), HEAD)
-            for t, w_ref in enumerate((wq_ref, wk_ref, wv_ref, wg_ref)):
+    copies = [
+        pltpu.make_async_copy(ref, here_ref.at[t], sems.at[t])
+        for t, ref in enumerate((wq_ref, wk_ref, wv_ref, wg_ref))
+    ]
+    for copy in copies:
+        copy.start()
+    rows, conv = here_ref.shape[1], HEADS + 2
+    side_ref[...] = jnp.zeros(side_ref.shape, F32)
+    side_ref[0:HEADS, 0:rows] = beta_ref[...].astype(F32)
+    side_ref[HEADS : HEADS + 1, 0:rows] = mixer_ref[...].astype(F32)
+    side_ref[HEADS + 1 : conv, 0:rows] = swiglu_ref[...].astype(F32)
+    side_ref[conv : conv + 3 * CONV, 0:rows] = conv_ref[...].astype(F32)
+    across = jnp.transpose(side_ref[...])
+    side_ref[...] = across
+    small = side_ref[0:rows, :].astype(BF16)
+    for out_ref in out_refs:
+        out_ref[:, 8 * HEAD :] = small
+    for t, copy in enumerate(copies):
+        copy.wait()
+        for d, out_ref in enumerate(out_refs):
+            slot = (pos_ref[1] ^ d) // repeat
+            for i in range(2):
+                cols = pl.ds(pl.multiple_of((i * (HEADS // 2) + slot) * HEAD, HEAD), HEAD)
                 spot = (4 * i + t) * HEAD
-                out_ref[:, spot : spot + HEAD] = w_ref[:, cols]
-        out_ref[:, 8 * HEAD :] = small_ref[...]
-
-
-def mixer_prepare(
+                out_ref[:, spot : spot + HEAD] = here_ref[t, :, cols]
+
+
+def mixer_forward(
     pos_ref,
     xown_ref,
     xsib_ref,
@@ -98,27 +124,39 @@
     flag_ref,
     idc_ref,
     idr_ref,
+    gain_ref,
+    heads_ref,
+    tap_ref,
+    gains_ref,
+    normed_out,
+    wcat_out,
+    p_out,
+    kept_out,
+    slope_out,
+    found_out,
+    shape_out,
+    across_ref,
     normed_ref,
     wcat_ref,
-    lin_ref,
-    tap_ref,
-    gains_ref,
     p_ref,
-    qh_ref,
-    k_ref,
-    v_ref,
-    sq_ref,
-    sk_ref,
-    sv_ref,
-    beta_ref,
-    t_ref,
-    sc_ref,
-    pb_ref,
-    w_ref,
-    map_ref,
-    add_ref,
-    across_ref,
+    kept_ref,
+    slope_ref,
+    found_ref,
+    shape_ref,
+    brief_ref,
+    sems,
 ):
+    qh_ref, k_ref, lin_ref, beta_ref, t_ref, sc_ref, map_ref = views(kept_ref)
+    sq_ref, sk_ref, sv_ref = views(slope_ref)
+    v_ref, pb_ref, w_ref, add_ref = views(brief_ref)
+    state_ref, ps_ref, er_ref = views(found_ref)
+    oh_ref, ro_ref = views(shape_ref)
+    copies = []
+
+    def send(i, source, target):
+        copies.append(pltpu.make_async_copy(source, target, sems.at[i]))
+        copies[-1].start()
+
     chips, _, span, width = xown_ref.shape
     length = normed_ref.shape[0]
     count = length // CHUNK
@@ -159,7 +197,7 @@
         p_ref[8 + n * tall : 8 + (n + 1) * tall, :] = y[:, 0 : 3 * HEAD].astype(BF16).astype(F32)
         lin_ref[rows, :] = y[:, 3 * HEAD : 4 * HEAD]
         logit = jnp.sum(y[:, 4 * HEAD :] * pick, axis=-1, keepdims=True)
-        beta_ref[rows, :] = jax.nn.sigmoid(logit)
+        beta_ref[rows, :] = jnp.broadcast_to(jax.nn.sigmoid(logit), (tall, HEAD))
     for n in range(count):
         r0 = n * CHUNK
         rows = slice(r0, r0 + CHUNK)
@@ -180,6 +218,12 @@
                 scale = lax.rsqrt(jnp.sum(act * act, axis=-1, keepdims=True) + UNIT_EPSILON)
                 (qh_ref if c == 0 else k_ref)[rows, :] = act * scale
                 (sq_ref if c == 0 else sk_ref)[rows, :] = slope * scale
+    send(0, normed_ref, normed_out)
+    send(1, wcat_ref, wcat_out)
+    send(2, p_ref, p_out)
+    send(3, slope_ref, slope_out)
+    send(4, kept_ref.at[0:4], kept_out.at[0:4])
+
     def prepare(group, carry):
         spots = [pl.multiple_of((group * GROUP + i) * CHUNK, CHUNK) for i in range(GROUP)]
         rows = [pl.ds(s, CHUNK) for s in spots]
@@ -212,32 +256,8 @@
         return carry
 
     lax.fori_loop(0, count // GROUP, prepare, 0)
-
-
-def mixer_produce(
-    lin_ref,
-    flag_ref,
-    idc_ref,
-    idr_ref,
-    gain_ref,
-    qh_ref,
-    k_ref,
-    v_ref,
-    sc_ref,
-    pb_ref,
-    w_ref,
-    map_ref,
-    add_ref,
-    heads_ref,
-    state_ref,
-    ps_ref,
-    er_ref,
-    oh_ref,
-    ro_ref,
-):
-    length = lin_ref.shape[0]
-    count = length // CHUNK
-    strict, _, _ = tri_masks(CHUNK)
+    send(5, kept_ref.at[4:7], kept_out.at[4:7])
+
     state = jnp.zeros((HEAD, HEAD), F32)
     for n in range(count):
         rows = slice(n * CHUNK, (n + 1) * CHUNK)
@@ -264,7 +284,7 @@
             scale = lax.rsqrt(jnp.mean(out * out, axis=-1, keepdims=True) + EPSILON)
             hat = out * scale
             oh_ref[r, :] = hat
-            ro_ref[r, :] = scale
+            ro_ref[r, :] = jnp.broadcast_to(scale, (CHUNK, HEAD))
             lin = lin_ref[r, :]
             made = (hat * gain_ref[...] * (lin * jax.nn.sigmoid(lin))).astype(BF16)
             half = CHUNK // 2
@@ -275,31 +295,94 @@
         return carry
 
     lax.fori_loop(0, count // GROUP, produce, 0)
-
-
-def mixer_backward_states(
+    send(6, found_ref, found_out)
+    send(7, shape_ref, shape_out)
+    for copy in copies:
+        copy.wait()
+
+
+def head_fold(rows):
+    row = lax.broadcasted_iota(jnp.int32, (HEAD, HEAD), 0)
+    lane = lax.broadcasted_iota(jnp.int32, (HEAD, HEAD), 1)
+    return (lane // (HEAD // rows) == row % rows).astype(F32)
+
+
+def head_place(rows):
+    row = lax.broadcasted_iota(jnp.int32, (HEAD, HEAD), 0)
+    lane = lax.broadcasted_iota(jnp.int32, (HEAD, HEAD), 1)
+    return (lane == FREE + row % (HEAD // rows)).astype(F32)
+
+
+def mixer_backward(
+    small_rows,
+    pos_ref,
     dh_ref,
-    lin_ref,
     flag_ref,
+    idc_ref,
+    idr_ref,
     gain_ref,
-    qh_ref,
-    k_ref,
-    beta_ref,
-    t_ref,
-    sc_ref,
-    map_ref,
-    oh_ref,
-    ro_ref,
-    dg_ref,
+    tap_ref,
+    swiglu_ref,
+    kept_in,
+    shape_in,
+    found_in,
+    slope_in,
+    p_in,
+    normed_in,
+    wcat_in,
+    dnkeep_ref,
+    dnsend_ref,
+    dwkeep_ref,
+    dwsend_ref,
+    kept_ref,
+    shape_ref,
+    found_ref,
+    slope_ref,
+    p_ref,
+    normed_ref,
+    wcat_ref,
+    back3_ref,
+    back_ref,
+    du_ref,
+    dcat_ref,
+    tapgrad_ref,
     headgrad_ref,
-    do_ref,
-    dpre_ref,
-    dstate_ref,
-    back_ref,
+    sems,
 ):
+    copies = [
+        pltpu.make_async_copy(source, target, sems.at[i])
+        for i, (source, target) in enumerate(
+            (
+                (kept_in, kept_ref),
+                (shape_in, shape_ref),
+                (found_in, found_ref),
+                (slope_in, slope_ref),
+                (p_in, p_ref),
+                (normed_in, normed_ref),
+                (wcat_in, wcat_ref),
+            )
+        )
+    ]
+    for copy in copies:
+        copy.start()
+    qh_ref, k_ref, lin_ref, beta_ref, t_ref, sc_ref, map_ref = views(kept_ref)
+    sq_ref, sk_ref, sv_ref = views(slope_ref)
+    state_ref, ps_ref, er_ref = views(found_ref)
+    oh_ref, ro_ref = views(shape_ref)
+    do_ref, dpre_ref, dstate_ref = views(back3_ref)
     length = lin_ref.shape[0]
+    blocks, rows_here, _ = dwkeep_ref.shape
+    chips = blocks // 2
+    repeat = chips // (HEADS // 2)
+    span = length // (2 * blocks)
+    core, share = pos_ref[2], pos_ref[1] % repeat
+    head = head_of(pos_ref, chips)
+    lane = lax.broadcasted_iota(jnp.int32, (1, HEAD), 1)
+    pick = (lane == head).astype(F32)
+    strict, incl, _ = tri_masks(CHUNK)
+    copies[0].wait()
+    copies[1].wait()
     count = length // CHUNK
-    chips = dh_ref.shape[0] // 2
     scale_q = HEAD ** (-0.5)
     headgrad_ref[...] = jnp.zeros(headgrad_ref.shape, F32)
 
@@ -316,7 +399,7 @@
             gain = gain_ref[...]
             both = grad * hat
             headgrad_ref[0:1, :] += jnp.sum(both * swish, axis=0, keepdims=True)
-            dg_ref[r, :] = (
+            dcat_ref[r, 3 * HEAD : 4 * HEAD] = (
                 both * gain * (sig * (1.0 + lin * (1.0 - sig)))
             ).astype(BF16)
             lead = grad * gain * swish
@@ -344,33 +427,8 @@
             - mm(split(grad_state), split(map_ref[rows, :]), NT)
             + back_ref[rows, :]
         )
-
-
-def mixer_backward_tokens(
-    do_ref,
-    dpre_ref,
-    dstate_ref,
-    flag_ref,
-    idc_ref,
-    idr_ref,
-    pick_ref,
-    qh_ref,
-    k_ref,
-    sq_ref,
-    sk_ref,
-    sv_ref,
-    beta_ref,
-    t_ref,
-    state_ref,
-    ps_ref,
-    er_ref,
-    du_ref,
-    dz_ref,
-):
-    length = do_ref.shape[0]
-    count = length // CHUNK
-    strict, incl, _ = tri_masks(CHUNK)
-    scale_q = HEAD ** (-0.5)
+    copies[2].wait()
+    copies[3].wait()
     du_ref[length : length + 8, :] = jnp.zeros((8, 3 * HEAD), F32)
 
     def second(group, carry):
@@ -406,7 +464,7 @@
             )
             grad_b = jnp.sum(zed * er_ref[r, :], axis=-1, keepdims=True)
             dz = grad_b * beta * (1.0 - beta)
-            dz_ref[r, :] = (dz * pick_ref[...]).astype(BF16)
+            dcat_ref[r, 4 * HEAD : 5 * HEAD] = (dz * pick).astype(BF16)
             lead = scale_q * grad_q
             du_ref[r, 0:HEAD] = sq_ref[r, :] * (
                 lead - q_hat * jnp.sum(lead * q_hat, axis=-1, keepdims=True)
@@ -418,36 +476,7 @@
         return carry
 
     lax.fori_loop(0, count // GROUP, second, 0)
-
-
-def mixer_backward_taps(
-    du_ref,
-    dg_ref,
-    dz_ref,
-    flag_ref,
-    tap_ref,
-    p_ref,
-    pos_ref,
-    normed_ref,
-    wcat_ref,
-    swiglu_ref,
-    dnkeep_ref,
-    dnsend_ref,
-    dwkeep_ref,
-    dwsend_ref,
-    dcat_ref,
-    tapgrad_ref,
-):
-    length = dg_ref.shape[0]
-    count = length // CHUNK
-    blocks, rows_here, _ = dwkeep_ref.shape
-    chips = blocks // 2
-    repeat = chips // (HEADS // 2)
-    span = length // (2 * blocks)
-    core, share = pos_ref[2], pos_ref[1] % repeat
-    head = head_of(pos_ref, chips)
-    dcat_ref[:, 3 * HEAD : 4 * HEAD] = dg_ref[...]
-    dcat_ref[:, 4 * HEAD : 5 * HEAD] = dz_ref[...]
+    copies[4].wait()
     sums = [[jnp.zeros((1, HEAD), F32) for _ in range(CONV)] for _ in range(3)]
     for n in range(count):
         r0 = n * CHUNK
@@ -481,6 +510,8 @@
             dcat_ref[rows, :] = (dcat_ref[rows, :].astype(F32) * counts).astype(BF16)
         tapgrad_ref[...] = tapgrad_ref[...] * (share == 0).astype(F32)
     width = normed_ref.shape[1]
+    copies[5].wait()
+    copies[6].wait()
 
     tall = 4 * CHUNK
     for n in range(length // tall):
@@ -491,6 +522,9 @@
             high = part[(2 * j + 1) * span : (2 * j + 2) * span]
             dnkeep_ref[4 * n + j, :, :] = jnp.where(core == 1, high, low).astype(BF16)
             dnsend_ref[4 * n + j, :, :] = jnp.where(core == 1, low, high).astype(BF16)
+    fold, place = head_fold(small_rows), head_place(small_rows)
+    total = headgrad_ref[0:1, :] * (share == 0).astype(F32)
+    spread = mm(split(fold * total), split(place), NN)
     for i in range(width // HEAD):
         cols = slice(i * HEAD, (i + 1) * HEAD)
         if i % 4 == 0:
@@ -514,7 +548,9 @@
             axis=0,
         )
         lane = lax.broadcasted_iota(jnp.int32, (1, HEAD), 1)
-        small = grad[:, 4 * HEAD :] + jnp.transpose(lines) + gain_grad * (lane == HEADS)
+        small = (
+            grad[:, 4 * HEAD :] + jnp.transpose(lines) + gain_grad * (lane == HEADS) + spread
+        )
         grad = jnp.concatenate([grad[:, : 4 * HEAD], small], axis=1)
         per = HEAD // (2 * rows_here)
         for j in range(per):
@@ -555,15 +591,14 @@
     for i in range(2 * chips):
         d, e = i // 2, i % 2
         block = (m ^ e) * chips + (q ^ d)
+        other = (m ^ e) * chips + d
         for which, o_ref, p_ref in ((c, oown_ref, pown_ref), (1 - c, osib_ref, psib_ref)):
-            spot = pl.ds(pl.multiple_of((2 * block + which) * rows_here, rows_here), rows_here)
+            spot = pl.ds(pl.multiple_of((2 * other + which) * rows_here, rows_here), rows_here)
             wo_ref[spot, :] = o_ref[d, e, :, :]
-            other = (m ^ e) * chips + d
-            spot = pl.ds(pl.multiple_of((2 * other + which) * rows_here, rows_here), rows_here)
             wp_ref[spot, :] = p_ref[e, d, :, :]
         spot = pl.ds(pl.multiple_of(block * span, span), span)
+        cots_ref[spot, :] = cot_ref[d, e, :, :]
         total_ref[spot, :] = xown_ref[d, e, :, :].astype(F32)
-        cots_ref[spot, :] = cot_ref[d, e, :, :]
     for i in range(2):
         for j in range(HEADS // 2):
             h = i * (HEADS // 2) + j
@@ -597,7 +632,8 @@
 
 
 def feed_forward_grads(
-    pos_ref, normed_ref, grads_ref, hidden_ref, cots_ref, down_ref, keep_ref, send_ref, downgrad_ref, out_ref
+    pos_ref, normed_ref, grads_ref, hidden_ref, cots_ref, down_ref,
+    keep_ref, send_ref, downkeep_ref, downsend_ref, out_ref,
 ):
     rows_here = keep_ref.shape[1]
     chips, _, span, _ = out_ref.shape
@@ -615,9 +651,13 @@
             high = grad[(2 * j + 1) * rows_here : (2 * j + 2) * rows_here]
             keep_ref[i * per + j, :, :] = jnp.where(core == 1, high, low).astype(BF16)
             send_ref[i * per + j, :, :] = jnp.where(core == 1, low, high).astype(BF16)
-    downgrad_ref[...] = lax.dot_general(
-        hidden_ref[...], cots_ref[...], TN, preferred_element_type=F32
-    ).astype(BF16)
+    down = lax.dot_general(hidden_ref[...], cots_ref[...], TN, preferred_element_type=F32)
+    rows = downkeep_ref.shape[1]
+    for e in range(2):
+        low = down[2 * e * rows : (2 * e + 1) * rows]
+        high = down[(2 * e + 1) * rows : (2 * e + 2) * rows]
+        downkeep_ref[e, :, :] = jnp.where(core == 1, high, low).astype(BF16)
+        downsend_ref[e, :, :] = jnp.where(core == 1, low, high).astype(BF16)
     out = lax.dot_general(hidden_ref[...], down_ref[...], NN, preferred_element_type=F32)
     for e in range(2):
         for j in range(chips):
@@ -659,16 +699,21 @@
                 ]
 
 
-def output_gradient(pos_ref, got_ref, branch_ref, all_ref, rows_ref, duo_ref):
-    chips, _, span, width = branch_ref.shape
+def output_gradient(pos_ref, got_ref, *refs):
+    *branch_refs, all_ref, rows_ref, duo_ref = refs
+    chips = len(branch_refs)
+    span = branch_refs[0].shape[1]
     repeat = chips // (HEADS // 2)
     q = pos_ref[1]
     share = q % repeat
-    for i in range(2 * chips):
-        d, e = i // 2, i % 2
-        spot = pl.ds(pl.multiple_of((e * chips + (q ^ d)) * span, span), span)
-        counts = ((q ^ d) % repeat == share).astype(F32)
-        rows_ref[spot, :] = (branch_ref[d, e, :, :].astype(F32) * counts).astype(BF16)
+    for d, branch_ref in enumerate(branch_refs):
+        for e in range(2):
+            spot = pl.ds(pl.multiple_of((e * chips + (q ^ d)) * span, span), span)
+            value = branch_ref[e, :, :]
+            if repeat > 1:
+                counts = ((q ^ d) % repeat == share).astype(F32)
+                value = (value.astype(F32) * counts).astype(BF16)
+            rows_ref[spot, :] = value
     first = pl.multiple_of((q // repeat) * 2 * repeat, 2)
     for i in range(2):
         duo_ref[:, i * HEAD : (i + 1) * HEAD] = got_ref[first + i, :, :]
@@ -677,13 +722,12 @@
         all_ref[i, :, :] = both[i * HEAD : (i + 1) * HEAD].astype(BF16)
 
 
-def input_gradient(pos_ref, resid_ref, x_ref, gains_ref, keep_ref, *rest):
-    *got_refs, out_ref = rest
+def input_gradient(pos_ref, resid_ref, x_ref, gains_ref, got_ref, out_ref):
     m = pos_ref[0]
     for e in range(2):
-        norm = keep_ref[e, :, :]
-        for got_ref in got_refs:
-            norm = norm + got_ref[e, :, :].astype(F32)
+        norm = got_ref[0, e, :, :].astype(F32)
+        for j in range(1, got_ref.shape[0]):
+            norm = norm + got_ref[j, e, :, :].astype(F32)
         x = x_ref[m ^ e, :, :].astype(F32)
         scale = lax.rsqrt(jnp.mean(x * x, axis=-1, keepdims=True) + EPSILON)
         hat = x * scale
@@ -694,28 +738,46 @@
         ).astype(BF16)
 
 
-def token_pieces(pos_ref, keep_ref, got_ref, own_ref, *send_refs):
-    chips = keep_ref.shape[0] // 2
-    q = pos_ref[1]
+def token_pieces(keep_ref, got_ref, out_ref):
+    chips = out_ref.shape[0]
     for e in range(2):
-        for d in range(chips):
-            block = e * chips + (q ^ d)
-            total = keep_ref[block, :, :].astype(F32) + got_ref[block, :, :].astype(F32)
-            if d == 0:
-                own_ref[e, :, :] = total
-            else:
-                send_refs[d - 1][e, :, :] = total.astype(BF16)
-
-
-def merge_heads(pos_ref, keep_ref, got_ref, out_ref):
-    core = pos_ref[2]
+        for j in range(chips):
+            block = e * chips + j
+            out_ref[j, e, :, :] = (
+                keep_ref[block, :, :].astype(F32) + got_ref[block, :, :].astype(F32)
+            ).astype(BF16)
+
+
+def merge_heads(pos_ref, keep_ref, got_ref, *out_refs):
+    m, _, core, batch = place_of(pos_ref)
     wide = 4 * HEAD
-    keep, got = keep_ref[...], got_ref[...]
-    out_ref[:, :, :wide] = jnp.where(core == 1, got[:, :, :wide], keep[:, :, :wide])
-    out_ref[:, :, wide : 2 * wide] = jnp.where(core == 1, keep[:, :, :wide], got[:, :, :wide])
-    out_ref[:, :, 2 * wide :] = (
-        keep[:, :, wide:].astype(F32) + got[:, :, wide:].astype(F32)
-    ).astype(BF16)
+
+    def merge(out_ref, keep, got):
+        out_ref[..., :wide] = jnp.where(core == 1, got[..., :wide], keep[..., :wide])
+        out_ref[..., wide : 2 * wide] = jnp.where(core == 1, keep[..., :wide], got[..., :wide])
+        out_ref[..., 2 * wide :] = (
+            keep[..., wide:].astype(F32) + got[..., wide:].astype(F32)
+        ).astype(BF16)
+
+    if len(out_refs) == 1:
+        merge(out_refs[0], keep_ref[...], got_ref[...])
+        return
+    chips, rows, _ = out_refs[0].shape
+    for i, out_ref in enumerate(out_refs):
+        spot = pl.ds(pl.multiple_of((batch ^ (i % 2)) * rows, rows), rows)
+        for j in range(chips):
+            block = (m ^ (i // 2)) * chips + j
+            merge(out_ref.at[j], keep_ref[block, spot, :], got_ref[block, spot, :])
+
+
+def add_partners(pos_ref, *refs):
+    in_refs, out_refs = refs[:4], refs[4:]
+    for d, out_ref in enumerate(out_refs):
+        j = pos_ref[1] ^ d
+        total = in_refs[0][j, :, :].astype(F32)
+        for in_ref in in_refs[1:]:
+            total = total + in_ref[j, :, :].astype(F32)
+        out_ref[...] = total.astype(BF16)
 
 
 def spread_heads(pos_ref, *refs):
@@ -724,7 +786,6 @@
     repeat = chips // (HEADS // 2)
     rows = wq_ref.shape[0]
     small = jnp.zeros((rows, HEAD), F32)
-    heads = jnp.zeros((1, HEAD), F32)
     if repeat > 1:
         for ref in (wq_ref, wk_ref, wv_ref, wg_ref):
             ref[...] = jnp.zeros(ref.shape, F32)
@@ -737,14 +798,17 @@
                 value = got_ref[0:rows, spot : spot + HEAD].astype(F32)
                 ref[:, cols] = value + ref[:, cols] if repeat > 1 else value
         small = small + got_ref[0:rows, 8 * HEAD :].astype(F32)
-        heads = heads + got_ref[rows : rows + 1, 0:HEAD].astype(F32)
-    beta_ref[...] = small[:, :HEADS]
     side_ref[...] = jnp.zeros(side_ref.shape, F32)
     side_ref[0:rows, :] = small
     across = jnp.transpose(side_ref[...])
+    beta_ref[...] = across[:HEADS, :rows]
     gains_ref[...] = across[HEADS : HEADS + 8, :rows]
     taps_ref[...] = across[HEADS + 2 : HEADS + 2 + 3 * CONV, :rows]
-    head_ref[...] = heads
+    found = mm(split(side_ref[...]), split(head_place(rows)), NT)
+    first = lax.broadcasted_iota(jnp.int32, (HEAD, HEAD), 0) < rows
+    head_ref[...] = jnp.sum(
+        jnp.where(first, found * head_fold(rows), 0.0), axis=0, keepdims=True
+    )
 
 
 def spread_pair(got_ref, gate_ref, up_ref):
@@ -762,18 +826,26 @@
 VMEM_SPEC = pl.BlockSpec(memory_space=pltpu.VMEM)
 
 
-def run_kernel(body, name, operands, out_shapes, scratch, micros, scalars=()):
+def run_kernel(body, name, operands, out_shapes, scratch, micros, scalars=(), stays=(), leaves=()):
     specs = [VMEM_SPEC] * len(operands)
     for i in scalars:
         specs[i] = pl.BlockSpec(memory_space=pltpu.SMEM)
+    for i in stays:
+        specs[i] = pl.BlockSpec(memory_space=pl.ANY)
+    room = [pltpu.VMEM(*s) for s in scratch]
+    if stays or leaves:
+        room.append(pltpu.SemaphoreType.DMA((len(stays) + len(leaves) + 1,)))
+    outs = [VMEM_SPEC] * len(out_shapes)
+    for i in leaves:
+        outs[i] = pl.BlockSpec(memory_space=pl.ANY)
     return pl.pallas_call(
         body,
         name=name,
         out_shape=[jax.ShapeDtypeStruct(*s) for s in out_shapes],
         in_specs=specs,
-        out_specs=[VMEM_SPEC] * len(out_shapes),
-        scratch_shapes=[pltpu.VMEM(*s) for s in scratch],
-        compiler_params=pltpu.CompilerParams(vmem_limit_bytes=56 * 1024 * 1024),
+        out_specs=outs,
+        scratch_shapes=room,
+        compiler_params=pltpu.CompilerParams(vmem_limit_bytes=VMEM_BYTES),
         cost_estimate=pl.CostEstimate(
             flops=micros * COST, bytes_accessed=1 << 10, transcendentals=0
         ),
@@ -807,14 +879,26 @@
     return [mine[0]] + [swap(mine[d], "q", d) for d in range(1, len(mine))]
 
 
-def gather_batch(value, axis):
+def gather_batch_start(value, axis):
     step, batch = 1, lax.axis_index("b")
     lead, rows = value.shape[:axis], value.shape[axis:]
-    while step < lax.axis_size("b"):
+    while 2 * step < lax.axis_size("b"):
         got = swap(value, "b", step)
         value = jnp.stack(ordered((batch // step) % 2, value, got), axis=axis)
         step *= 2
-    return value.reshape(lead + (lax.axis_size("b") * rows[0],) + rows[1:])
+    value = value.reshape(lead + (step * rows[0],) + rows[1:])
+    return value, swap(value, "b", step)
+
+
+def gather_batch_end(value, got, axis):
+    lead, rows = value.shape[:axis], value.shape[axis:]
+    high = lax.axis_index("b") // (lax.axis_size("b") // 2) == 1
+    value = jnp.stack(ordered(high.astype(jnp.int32), value, got), axis=axis)
+    return value.reshape(lead + (2 * rows[0],) + rows[1:])
+
+
+def gather_batch(value, axis):
+    return gather_batch_end(*gather_batch_start(value, axis), axis)
 
 
 def scatter_bit(value, axis, bit, mesh_axis, mask):
@@ -824,14 +908,14 @@
     return keep.astype(F32) + swap(send.astype(BF16), mesh_axis, mask).astype(F32)
 
 
-def scatter_batch(value, axis):
+def scatter_batch(value, axis, left=1):
     batch, step = lax.axis_index("b"), lax.axis_size("b") // 2
-    while step >= 1:
+    while step >= left:
         shape = value.shape
         value = value.reshape(shape[:axis] + (2, shape[axis] // 2) + shape[axis + 1 :])
         value = scatter_bit(value, axis, (batch // step) % 2, "b", step)
         step //= 2
-    return lax.squeeze(value, (axis,))
+    return lax.squeeze(value, (axis,)) if left == 1 else value
 
 
 def token_flags(ids):
@@ -879,24 +963,16 @@
     flag_row = row == 1
     pos = jnp.stack([row, chip, core, lax.axis_index("b")]).astype(jnp.int32)
 
-    small = jnp.concatenate(
-        [
-            beta_weight,
-            mixer_gain[:, None],
-            swiglu_gain[:, None],
-            jnp.swapaxes(conv_weight, 0, 1),
-            jnp.zeros((rows_w, HEAD - HEADS - 2 - 3 * CONV), BF16),
-        ],
-        axis=1,
-    )
     mine = run_kernel(
         pack_heads,
         "pack_heads",
-        (pos, query_weight, key_weight, value_weight, outgate_weight, small),
+        (pos, query_weight, key_weight, value_weight, outgate_weight, beta_weight.T)
+        + (mixer_gain[None, :], swiglu_gain[None, :], conv_weight),
         [((rows_w, 9 * HEAD), BF16)] * chips,
-        [],
+        [((4, rows_w, width), BF16), ((HEAD, HEAD), F32)],
         1,
         (0,),
+        (1, 2, 3, 4),
     )
     head_s = [swap(mine[d], "q", d) for d in range(1, chips)]
 
@@ -906,86 +982,81 @@
     def away_slab(value):
         return jnp.where(flag_row, value[0], value[1])
 
-    x_s, out_s = swap(away_slab(inputs[:, 0]), "m", 1), swap(output_weight, "m", 1)
-    head_s, x_s, out_s = together(head_s, x_s, out_s)
+    x_s = swap(away_slab(inputs[:, 0]), "m", 1)
+    head_s, x_s = together(head_s, x_s)
     head_q = jnp.stack([mine[0]] + head_s, axis=0)
     x_own = jnp.stack([own_slab(inputs[:, 0]), x_s], axis=0)
     head_m = jnp.stack([head_q, swap(head_q, "m", 1)], axis=0)
     x_half = jnp.stack(from_chips(x_own), axis=0)
-    out_b = gather_batch(jnp.stack([output_weight, out_s], axis=0), 1)
+    out_s = swap(tie(output_weight, x_s), "m", 1)
     ids = own_slab(document_ids[:, 0])
     flags, id_rows, id_cols = token_flags(ids)
     gain_vec = head_gain.astype(F32)[None, :]
-    head_m, x_half, out_b, flags, id_rows, id_cols, gain_vec = together(
-        head_m, x_half, out_b, flags, id_rows, id_cols, gain_vec
+    pair = jnp.stack([gate_weight, up_weight], axis=1).reshape(
+        rows_w, 2, micro, chips, 2 * n_batch * rows_f
+    )
+    pair = jnp.moveaxis(pair, 3, 0).reshape(chips, rows_w, 2 * ff_here)
+    cot_away = away_slab(cotangent[:, 0])
+    head_m, x_half, out_s, flags, id_rows, id_cols, gain_vec, pair, cot_away = together(
+        head_m, x_half, out_s, flags, id_rows, id_cols, gain_vec, pair, cot_away
     )
     head_b = gather_batch(head_m.reshape(blocks_all, rows_w, 9 * HEAD), 1)
     x_sib = swap(x_half, "c", 1)
-    cot_s = swap(tie(away_slab(cotangent[:, 0]), x_half), "m", 1)
-    pair = jnp.stack([gate_weight, up_weight], axis=1).reshape(
-        rows_w, 2, micro, chips, 2 * n_batch * rows_f
-    )
-    pair = jnp.moveaxis(pair, 3, 0).reshape(chips, rows_w, 2 * ff_here)
-    pair_q = lax.all_to_all(tie(pair, x_half), ("q",), 0, 0, tiled=True)
-    head_b, x_sib, cot_s, pair_q = together(head_b, x_sib, cot_s, pair_q)
-    cot_own = jnp.stack([own_slab(cotangent[:, 0]), cot_s], axis=0)
+    cot_s = swap(cot_away, "m", 1)
+    down_s = swap(tie(down_weight, x_half), "m", 1)
+    out_b = gather_batch(jnp.stack([output_weight, out_s], axis=0), 1)
+    pair_q = lax.all_to_all(pair, ("q",), 0, 0, tiled=True)
+    head_b, x_sib, cot_s, down_s, out_b, pair_q = together(
+        head_b, x_sib, cot_s, down_s, out_b, pair_q
+    )
     send = lax.dynamic_slice_in_dim(head_b, (1 - core) * 4 * HEAD, 4 * HEAD, 2)
     head_sib = swap(jnp.concatenate([send, head_b[..., 8 * HEAD :]], axis=-1), "c", 1)
-    pair_s = swap(tie(pair_q, head_b), "m", 1)
-    out_s = [swap(tie(out_b, head_b), "q", d) for d in range(1, chips)]
+    pair_s = swap(pair_q, "m", 1)
+    cot_own = jnp.stack([own_slab(cotangent[:, 0]), cot_s], axis=0)
+    down_m, down_got = gather_batch_start(jnp.stack(ordered(row, down_weight, down_s), axis=0), 1)
+    out_q = lax.all_to_all(
+        jnp.broadcast_to(out_b, (chips,) + out_b.shape), ("q",), 0, 0, tiled=True
+    )
+    cot_got = [swap(cot_own, "q", d) for d in range(1, chips)]
 
     count = length // CHUNK
-    tall = ((length, HEAD), F32)
-    square = ((length, CHUNK), F32)
-    states = ((count * HEAD, HEAD), F32)
-    thin = ((length, 1), F32)
+    def tall(n):
+        return ((n, length, HEAD), F32)
+
     slabs = ((2, span, width), BF16)
     slabs_wide = ((2, span, width), F32)
-    normed, w_cat, lin, taps, gains, p_pad, q_hat, k_vec, v_vec, slope_q, slope_k, slope_v, beta, t_mat, score, pseudo, weighed, step_map, step_add = run_kernel(
-        mixer_prepare,
-        "mixer_prepare",
-        (pos, x_half, x_sib, head_b, head_sib, flags, id_cols, id_rows),
-        [
-            ((length, width), BF16),
-            ((width, 5 * HEAD), BF16),
-            tall,
-            ((16, HEAD), F32),
-            ((8, width), F32),
-            ((length + 8, 3 * HEAD), F32),
-        ]
-        + [tall] * 6
-        + [thin, square, square, tall, tall, states, states],
-        [((HEAD, width), F32)],
-        20,
+    saved = [
+        ((length, width), BF16),
+        ((width, 5 * HEAD), BF16),
+        ((length + 8, 3 * HEAD), F32),
+        tall(7),
+        tall(3),
+        tall(3),
+        tall(2),
+    ]
+    heads_here, taps, gains, normed, w_cat, p_pad, kept, slopes, found, shaped = run_kernel(
+        mixer_forward,
+        "mixer_forward",
+        (pos, x_half, x_sib, head_b, head_sib, flags, id_cols, id_rows, gain_vec),
+        [((chips, 2, length // 2, HEAD), BF16), ((16, HEAD), F32), ((8, width), F32)] + saved,
+        [((HEAD, width), F32)] + saved + [tall(4)],
+        25,
         (0,),
-    )
-    pair_s, out_s, lin_late = together(pair_s, out_s, lin)
-    pair_m = jnp.stack([pair_q, pair_s], axis=0).reshape(blocks_all, rows_w, 2 * ff_here)
-    out_q = jnp.stack([out_b] + out_s, axis=0)
-    cot_s = [swap(tie(cot_own, lin_late), "q", d) for d in range(1, chips)]
-    down_s = swap(tie(down_weight, lin_late), "m", 1)
-    pair_b = gather_batch(pair_m, 1)
-    heads_here, state, pseudo, error, out_hat, out_scale = run_kernel(
-        mixer_produce,
-        "mixer_produce",
-        (tie(lin_late, pair_m, out_q), flags, id_cols, id_rows, gain_vec)
-        + (q_hat, k_vec, v_vec, score, pseudo, weighed, step_map, step_add),
-        [((chips, 2, length // 2, HEAD), BF16), states, tall, tall, tall, thin],
-        [],
-        9,
-    )
+        (),
+        tuple(range(3, 10)),
+    )
+    pair_s, down_got, out_q, cot_got = tie((pair_s, down_got, out_q, cot_got), heads_here)
 
     got_heads = lax.all_to_all(
         heads_here.reshape(chips * 2, length // 2, HEAD), ("q", "c"), 0, 0, tiled=True
     )
-    pair_b, down_s, cot_s = tie((pair_b, down_s, cot_s), heads_here)
-    down_m = jnp.stack(ordered(row, down_weight, down_s), axis=0)
-    down_b = gather_batch(down_m, 1)
-    cot_half = jnp.stack([cot_own] + cot_s, axis=0)
-    pair_b = pair_b.reshape(micro, chips, rows_all, 2 * ff_here)
-    pair_sib = swap(pair_b, "c", 1)
+    pair_m = jnp.stack([pair_q, pair_s], axis=0).reshape(blocks_all, rows_w, 2 * ff_here)
+    pair_b = gather_batch(pair_m, 1).reshape(micro, chips, rows_all, 2 * ff_here)
+    cot_half = jnp.stack([cot_own] + cot_got, axis=0)
+    down_b = gather_batch_end(down_m, down_got, 1)
     out_sib = swap(out_q, "c", 1)
     down_sib = swap(down_b, "c", 1)
+    pair_sib = swap(pair_b, "c", 1)
     w_down = jnp.stack(ordered(core, down_b, down_sib), axis=1).reshape(ff_here, width)
     half = length // 2
     w_out, normed_two, pair_up, hidden, cot_rows, swiglu_part, res_own, norm_own, *norm_send = run_kernel(
@@ -1014,143 +1085,165 @@
         (0,),
     )
     norm_got = [swap(v, "q", d + 1) for d, v in enumerate(norm_send)]
-    pair_keep, pair_send, down_grad, out_part = run_kernel(
+    pair_keep, pair_send, down_keep, down_send, out_part = run_kernel(
         feed_forward_grads,
         "feed_forward_grads",
         (pos, normed_two, pair_up, hidden, cot_rows, w_down),
         [
             ((blocks_all, rows_all, 2 * ff_here), BF16),
             ((blocks_all, rows_all, 2 * ff_here), BF16),
-            ((ff_here, width), BF16),
+            ((micro, n_batch * rows_f, width), BF16),
+            ((micro, n_batch * rows_f, width), BF16),
             ((chips, 2, span, width), BF16),
         ],
         [],
         6,
         (0,),
     )
-    norm_got, norm_own, pair_keep, pair_send, down_grad, out_part = together(
-        norm_got, norm_own, pair_keep, pair_send, down_grad, out_part
-    )
+    norm_got, norm_own, pair_send, down_send = together(norm_got, norm_own, pair_send, down_send)
     grad_resid, grad_branch, grad_heads = run_kernel(
         branch_gradient,
         "branch_gradient",
-        (pos, norm_own, res_own, cot_half, gains, w_out, *norm_got),
+        (pos, norm_own, res_own, cot_own[None], gains, w_out, *norm_got),
         [slabs_wide, slabs, ((chips * 2, 2, span, HEAD), BF16)],
         [],
         2,
         (0,),
     )
+
+    pair_got = swap(pair_send, "c", 1)
+    down_got = swap(down_send, "c", 1)
     dheads = lax.all_to_all(grad_heads, ("q", "c"), 0, 0, tiled=True)
-
-    pair_got = swap(pair_send, "c", 1)
-    down_grad = scatter_bit(
-        down_grad.reshape(micro, 2, n_batch, rows_f, width), 1, core, "c", 1
-    ).astype(BF16)
-    pair_grad = pair_keep.astype(F32) + pair_got.astype(F32)
-    dheads, pair_grad, down_grad = together(dheads, pair_grad, down_grad)
-    pair_grad = pair_grad.reshape(blocks_all, n_batch, rows_w, 2 * ff_here)
-    pair_grad = scatter_batch(pair_grad, 1).reshape(micro, chips, rows_w, 2 * ff_here)
-    branch_s = [swap(grad_branch, "q", d) for d in range(1, chips)]
-    grad_lin, head_part, grad_out, grad_pre, grad_state = run_kernel(
-        mixer_backward_states,
-        "mixer_backward_states",
-        (dheads, lin, flags, gain_vec, q_hat, k_vec, beta, t_mat, score, step_map, out_hat, out_scale),
-        [((length, HEAD), BF16), ((8, HEAD), F32), tall, tall, states],
-        [states],
-        9,
-    )
-    branch_s, grad_out = together(branch_s, grad_out)
-    branch_all = jnp.stack([grad_branch] + branch_s, axis=0)
+    grad_branch, pair_got, down_got = together(grad_branch, pair_got, down_got)
+    pair_grad = (pair_keep.astype(F32) + pair_got.astype(F32)).astype(BF16)
+    down_grad = (down_keep.astype(F32) + down_got.astype(F32)).astype(BF16)
+    down_grad = down_grad.reshape(micro, n_batch, rows_f, width)
+    dheads, pair_grad, down_grad, grad_branch, out_part = together(
+        dheads, pair_grad, down_grad, grad_branch, out_part
+    )
+    out_got = lax.all_to_all(out_part, ("q",), 0, 0, tiled=True)
+    branch_got = [swap(grad_branch, "q", d) for d in range(1, chips)]
+    pair_grad = pair_grad.reshape(micro, chips, n_batch, rows_w, 2 * ff_here)
+    pair_keep = lax.dynamic_index_in_dim(pair_grad, row, 0, keepdims=False)
+    pair_got = swap(lax.dynamic_index_in_dim(pair_grad, 1 - row, 0, keepdims=False), "m", 1)
+    down_grad = scatter_batch(down_grad, 1)
+
+    def to_rows(value):
+        keep = jnp.where(flag_row, value[1], value[0])
+        send = jnp.where(flag_row, value[0], value[1])
+        return jnp.stack(ordered(row, keep, swap(send, "m", 1)), axis=0)[:, None]
+
+    blocks_out = ((blocks_all, span, width), BF16)
+    weights_out = ((blocks_all, rows_all, 5 * HEAD), BF16)
+    norm_keep, norm_send, w_keep, w_send = run_kernel(
+        partial(mixer_backward, rows_w),
+        "mixer_backward",
+        (pos, dheads, flags, id_cols, id_rows, gain_vec, taps, swiglu_part)
+        + (kept, shaped, found, slopes, p_pad, normed, w_cat),
+        [blocks_out, blocks_out, weights_out, weights_out],
+        [saved[i] for i in (3, 6, 5, 4, 2, 0, 1)]
+        + [
+            tall(3),
+            ((length, HEAD), F32),
+            ((length + 8, 3 * HEAD), F32),
+            ((length, 5 * HEAD), BF16),
+            ((16, HEAD), F32),
+            ((8, HEAD), F32),
+        ],
+        25,
+        (0,),
+        tuple(range(8, 15)),
+    )
+    pair_got, down_grad, branch_got, out_got, w_send, norm_send = together(
+        pair_got, down_grad, branch_got, out_got, w_send, norm_send
+    )
+
+    norm_got = swap(norm_send, "c", 1)
+    w_got = swap(w_send, "c", 1)
     (out_rows,) = run_kernel(
         output_gradient,
         "output_gradient",
-        (pos, got_heads, branch_all),
+        (pos, got_heads, grad_branch, *branch_got),
         [((2, HEAD, width), BF16)],
         [((half, width), BF16), ((half, 2 * HEAD), BF16)],
         1,
         (0,),
     )
-    if repeat > 1:
-        head_part = jnp.where(share == 0, head_part, 0.0)
+    w_got, out_rows = together(w_got, out_rows)
+    piece = ((chips, rows_w, 9 * HEAD), BF16)
+    if n_batch == 2:
+        value = run_kernel(
+            merge_heads, "merge_heads", (pos, w_keep, w_got), [piece] * 4, [], 1, (0,)
+        )
+    else:
+        merged_all = ((blocks_all, rows_all, 9 * HEAD), BF16)
+        (value,) = run_kernel(
+            merge_heads, "merge_heads", (pos, w_keep, w_got), [merged_all], [], 1, (0,)
+        )
+        value = value.reshape(blocks_all, n_batch, rows_w, 9 * HEAD)
+        value = scatter_batch(value, 1, 2).reshape(micro, chips, 2, rows_w, 9 * HEAD)
+        batch = lax.axis_index("b") % 2
+        value = [
+            lax.dynamic_index_in_dim(
+                lax.dynamic_index_in_dim(value, row ^ (i // 2), 0, keepdims=False),
+                batch ^ (i % 2),
+                1,
+                keepdims=False,
+            ).astype(BF16)
+            for i in range(4)
+        ]
+    value, norm_got, out_rows, pair_got = together(value, norm_got, out_rows, pair_got)
+    (norm_send,) = run_kernel(
+        token_pieces,
+        "token_pieces",
+        (norm_keep, norm_got),
+        [((chips, 2, span, width), BF16)],
+        [],
+        1,
+    )
     step = repeat // 2
     while step >= 1:
         out_rows = out_rows.reshape(micro, 2, out_rows.shape[1] // 2, width)
         out_rows = scatter_bit(out_rows, 1, (share // step) % 2, "q", step)
         step //= 2
-    out_rows = out_rows.astype(BF16).reshape(micro, 2, n_batch, rows_w, width)
-    head_rows = jnp.pad(head_part, ((0, 0), (0, width - HEAD))).astype(BF16)
-    head_rows = jnp.broadcast_to(head_rows, (micro, 2, n_batch, 8, width))
-    tail = jnp.concatenate([out_rows, head_rows], axis=3)
-    pair_grad, grad_out, tail = together(pair_grad, grad_out, tail)
-    tail = scatter_bit(tail, 1, core, "c", 1)
-    down_grad = scatter_batch(down_grad, 1)
-    pair_rows = scatter_bit(pair_grad, 0, row, "m", 1).astype(BF16)
-    out_got = lax.all_to_all(tie(out_part, grad_out), ("q",), 0, 0, tiled=True)
-    du, grad_z = run_kernel(
-        mixer_backward_tokens,
-        "mixer_backward_tokens",
-        (grad_out, grad_pre, grad_state, flags, id_cols, id_rows, pick_of(pos, chips), q_hat, k_vec)
-        + (slope_q, slope_k, slope_v, beta, t_mat, state, pseudo, error),
-        [((length + 8, 3 * HEAD), F32), ((length, HEAD), BF16)],
-        [],
-        10,
-    )
-    tail, down_grad, pair_rows, out_got, grad_z = together(
-        tail, down_grad, pair_rows, out_got, grad_z
-    )
-    out_all = (res_own + jnp.sum(out_got.astype(F32), axis=0)).astype(BF16)
-
-    def to_rows(value):
-        keep = jnp.where(flag_row, value[1], value[0])
-        send = jnp.where(flag_row, value[0], value[1])
-        return jnp.stack(ordered(row, keep, swap(send, "m", 1)), axis=0)[:, None]
-
-    tail = scatter_batch(tail, 1)
-    down_grad = scatter_bit(down_grad, 0, row, "m", 1)
-    pair_got = lax.all_to_all(pair_rows, ("q",), 0, 0, tiled=True)
-    out_final = to_rows(out_all)
-    norm_keep, norm_send, w_keep, w_send = run_kernel(
-        mixer_backward_taps,
-        "mixer_backward_taps",
-        (du, grad_lin, grad_z, flags, taps, p_pad, pos, normed, w_cat, swiglu_part),
-        [
-            ((blocks_all, span, width), BF16),
-            ((blocks_all, span, width), BF16),
-            ((blocks_all, rows_all, 5 * HEAD), BF16),
-            ((blocks_all, rows_all, 5 * HEAD), BF16),
-        ],
-        [((length, 5 * HEAD), BF16), ((16, HEAD), F32)],
-        12,
-        (6,),
-    )
-
-    tail, down_grad, pair_got, out_final, norm_send, w_send = together(
-        tail, down_grad, pair_got, out_final, norm_send, w_send
-    )
-    tail = scatter_bit(tail, 0, row, "m", 1)
-    norm_got = swap(norm_send, "c", 1)
-    w_got = swap(w_send, "c", 1)
-    norm_own, *norm_send = run_kernel(
-        token_pieces,
-        "token_pieces",
-        (pos, norm_keep, norm_got),
-        [slabs_wide] + [slabs] * (chips - 1),
+    out_rows = out_rows.reshape(micro, 2, n_batch, rows_w, width)
+    norm_got = lax.all_to_all(norm_send, ("q",), 0, 0, tiled=True)
+    value_got = [
+        swap(value[1], "b", 1),
+        swap(value[2], "m", 1),
+        swap(value[3], ("m", "b"), n_batch + 1),
+    ]
+    pair_rows = (pair_keep.astype(F32) + pair_got.astype(F32)).astype(BF16)
+    pair_rows = scatter_batch(pair_rows, 1)
+    out_rows = scatter_bit(out_rows, 1, core, "c", 1)
+    norm_got, pair_rows, out_rows = together(norm_got, pair_rows, out_rows)
+    pair_got = lax.all_to_all(pair_rows.astype(BF16), ("q",), 0, 0, tiled=True)
+    out_rows = scatter_batch(out_rows, 1)
+    (grad_own,) = run_kernel(
+        input_gradient,
+        "input_gradient",
+        (pos, grad_resid, x_own, gains, norm_got),
+        [slabs],
         [],
         1,
         (0,),
     )
-    (value,) = run_kernel(
-        merge_heads,
-        "merge_heads",
-        (pos, w_keep, w_got),
-        [((blocks_all, rows_all, 9 * HEAD), BF16)],
+    grad_final = to_rows(grad_own)
+    value_got, out_rows, down_grad, out_got = together(value_got, out_rows, down_grad, out_got)
+    head_got = run_kernel(
+        add_partners,
+        "add_partners",
+        (pos, value[0], *value_got),
+        [((rows_w, 9 * HEAD), BF16)] * chips,
         [],
         1,
         (0,),
     )
-    norm_send, value, tail = together(norm_send, value, tail)
-    norm_got = [swap(v, "q", d + 1) for d, v in enumerate(norm_send)]
-    value = scatter_batch(value.reshape(blocks_all, n_batch, rows_w, 9 * HEAD), 1)
+    head_got = [head_got[0]] + [swap(head_got[d], "q", d) for d in range(1, chips)]
+    outproj_grad = scatter_bit(out_rows, 0, row, "m", 1)
+    down_grad = scatter_bit(down_grad, 0, row, "m", 1)
+    out_all = (res_own + jnp.sum(out_got.astype(F32), axis=0)).astype(BF16)
+    out_final = to_rows(out_all)
     gate_grad, up_grad = run_kernel(
         spread_pair,
         "spread_pair",
@@ -1159,27 +1252,12 @@
         [],
         2,
     )
-    value = scatter_bit(value.reshape(micro, chips, rows_w, 9 * HEAD), 0, row, "m", 1)
-    (grad_own,) = run_kernel(
-        input_gradient,
-        "input_gradient",
-        (pos, grad_resid, x_own, gains, norm_own, *norm_got),
-        [slabs],
-        [],
-        1,
-        (0,),
-    )
-    grad_final = to_rows(grad_own)
-    head_rows = tail[rows_w:, : 9 * HEAD]
-    head_rows = jnp.pad(head_rows, ((0, 0), (0, 9 * HEAD - head_rows.shape[1])))
-    head_rows = jnp.broadcast_to(head_rows, (chips,) + head_rows.shape)
-    value = jnp.concatenate([value, head_rows], axis=1).astype(BF16)
     *merged, beta_sum, gain_sums, tap_sums, head_sum = run_kernel(
         spread_heads,
         "spread_heads",
-        (pos, *to_chips(value)),
+        (pos, *head_got),
         [((rows_w, width), F32)] * 4
-        + [((rows_w, HEADS), F32), ((8, rows_w), F32), ((3 * CONV, rows_w), F32), ((1, HEAD), F32)],
+        + [((HEADS, rows_w), F32), ((8, rows_w), F32), ((3 * CONV, rows_w), F32), ((1, HEAD), F32)],
         [((HEAD, HEAD), F32)],
         1,
         (0,),
@@ -1190,9 +1268,9 @@
         merged[0],
         merged[1],
         merged[2],
-        beta_sum,
+        beta_sum.T,
         merged[3],
-        tail[:rows_w],
+        outproj_grad,
         gate_grad,
         up_grad,
         down_grad,
@@ -1201,11 +1279,6 @@
         head_sum[0],
         tap_sums,
     )
-
-
-def pick_of(pos, chips):
-    lane = lax.broadcasted_iota(jnp.int32, (1, HEAD), 1)
-    return (lane == head_of(pos, chips)).astype(F32)
 
 
 def solution(mesh):

time: 330 us -> 299 us (0.906)
  Pallas kernels: 95.3 us -> 85.2 us
  local copies, waits for them, and re-layouts: 21.8 us -> 14.5 us
  starting transfers between devices: 84.4 us -> 77.7 us
  other arithmetic: 37.6 us -> 32.9 us
    ppermute x54 -> x49, starting transfers between devices: 62.1 us -> 51.5 us  [swap(): lax.ppermute(value, axis, [(i, i ^ mask) for i in range(lax.axis_size(axi...]
    pallas_call x15 -> x13, Pallas kernels: 95.3 us -> 85.2 us  [run_kernel(): pl.pallas_call(body, name=name, out_shape=[jax.ShapeDtypeStruct(*s) for s...]
    all_to_all x3 -> x5, waiting for transfers between devices: 4.17 us -> 11.8 us  [the longest x1 9.38 us: on_device(): norm_got = lax.all_to_all(norm_send, ('q',), 0, 0, tiled=True)]
    all_to_all x1, waiting for transfers between devices: 8 us -> 1.65 us  [on_device(): dheads = lax.all_to_all(grad_heads, ('q', 'c'), 0, 0, tiled=True)]
    another operation x16 -> x12, other arithmetic: 11.7 us -> 7.78 us  [the longest x2 4.02 us: on_device(): cot_half = jnp.stack([cot_own] + cot_got, axis=0)]
    all_to_all x3 -> x5, starting transfers between devices: 15 us -> 18.5 us  [the longest x1 4.11 us: on_device(): pair_got = lax.all_to_all(pair_rows.astype(BF16), ('q',), 0, 0, tiled=True)]
    ppermute x54 -> x49, waiting for transfers between devices: 70.6 us -> 68.2 us  [swap(): lax.ppermute(value, axis, [(i, i ^ mask) for i in range(lax.axis_size(axi...]
    unnamed x83 -> x100, local copies, waits for them, and re-layouts: 9.23 us -> 6.94 us
  transfers between devices with their start and end apart: 59 -> 56, of which waited for: 27 -> 21; matrix products, arithmetic and copies ran while one was open for 13% -> 13% of each run, Pallas kernels for 24% -> 24%
where the time goes in v1:
time: 299 us; the launch traced here: 294 us
  Pallas kernels  85.2 us (28%)
  waiting for transfers between devices  81.6 us (27%)
  starting transfers between devices  77.7 us (26%)
  other arithmetic  32.9 us (11%)
  local copies, waits for them, and re-layouts  14.5 us (5%)
    pallas_call x13, Pallas kernels, run_kernel(): pl.pallas_call(body, name=name, out_shape=[jax.ShapeDtypeStruct(*s) for s...  85.2 us
    ppermute x49, waiting for transfers between devices, swap(): lax.ppermute(value, axis, [(i, i ^ mask) for i in range(lax.axis_size(axi...  68.2 us
    ppermute x49, starting transfers between devices, swap(): lax.ppermute(value, axis, [(i, i ^ mask) for i in range(lax.axis_size(axi...  51.5 us
    all_to_all x1, waiting for transfers between devices, on_device(): norm_got = lax.all_to_all(norm_send, ('q',), 0, 0, tiled=True)  9.38 us
    unnamed x100, local copies, waits for them, and re-layouts  6.94 us
  transfers between devices with their start and end apart: 56, of which 21 were waited for; matrix products, arithmetic and copies ran while one was open for 13% of the time, Pallas kernels for 24%

profile of v1, /device:TPU:0, one launch (start us, length us, event | category | flops | bytes accessed | tf_op | source)
XLA Modules:
  0.0 293.8 jit_solution(14988724761245011220)
XLA Ops:
  1.3 2.5 pack_heads.1
  3.9 3.0 %collective-permute-start = (bf16[32,1152]{1,0:T(8,128)(2,1)}, bf16[32,1152]{1,0:T(8,128)(2,1)S(1)}, u32[]{:S(2)}, u32[]{:S(2)}) collective-permute-start(bf16[32,1152]{1,0:T(8,128)(2,1)} %get-tuple-element.138), channel_id=1, source_target_pairs={{0,4},{4,0},{8,12},{12,8},{1,5},{5,1},{9,13},{13,9},{2,6},{6,2},{1... | collective-permute-start | bytes 221192 | tf_op jit(solution)/shard_map/ppermute | solution.py:864
  6.9 1.6 collective-permute-start.1
  9.4 3.1 %collective-permute-start.3 = (bf16[64,1024]{1,0:T(8,128)(2,1)S(1)}, bf16[64,1024]{1,0:T(8,128)(2,1)S(1)}, u32[]{:S(2)}, u32[]{:S(2)}) collective-permute-start(bf16[64,1024]{1,0:T(8,128)(2,1)S(1)} %get-tuple-element.333), channel_id=1, source_target_pairs={{0,16},{16,0},{1,17},{17,1},{2,18},{18,2},{3,19},{19,3},{4,20},{20... | collective-permute-start | bytes 393224 | tf_op jit(solution)/shard_map/ppermute | solution.py:864
  21.0 1.6 collective-permute-start.5
  22.5 1.6 collective-permute-start.6
  25.2 2.9 collective-permute-start.8
  28.2 11.3 %collective-permute-done.6 = bf16[2,64,1024]{2,1,0:T(8,128)(2,1)S(1)} collective-permute-done((bf16[2,64,1024]{2,1,0:T(8,128)(2,1)S(1)}, bf16[2,64,1024]{2,1,0:T(8,128)(2,1)S(1)}, u32[]{:S(2)}, u32[]{:S(2)}) %collective-permute-start.6) | collective-permute-done | bytes 262176 | tf_op jit(solution)/shard_map/ppermute | solution.py:864
  39.5 2.9 collective-permute-done.7
  42.6 1.6 collective-permute-start.9
  44.8 2.3 collective-permute-start.12
  47.7 3.5 %all-to-all-start = ((bf16[4,32,1408]{2,1,0:T(8,128)(2,1)}), bf16[4,32,1408]{2,1,0:T(8,128)(2,1)S(1)}, u32[]{:S(2)}, u32[]{:S(2)}) async-start(bf16[4,32,1408]{2,1,0:T(8,128)(2,1)} %reshape.392), calls=%async_computation | async-start | bytes 720896 | tf_op jit(solution)/shard_map/all_to_all | solution.py:1008
  51.2 7.0 %collective-permute-done.13 = bf16[2,32,1024]{2,1,0:T(8,128)(2,1)S(1)} collective-permute-done((bf16[2,32,1024]{2,1,0:T(8,128)(2,1)S(1)}, bf16[2,32,1024]{2,1,0:T(8,128)(2,1)S(1)}, u32[]{:S(2)}, u32[]{:S(2)}) %collective-permute-start.13) | collective-permute-done | bytes 131104 | tf_op jit(solution)/shard_map/ppermute | solution.py:864
  58.6 3.3 %collective-permute-done.11 = bf16[64,1024]{1,0:T(8,128)(2,1)} collective-permute-done((bf16[64,1024]{1,0:T(8,128)(2,1)}, bf16[64,1024]{1,0:T(8,128)(2,1)}, u32[]{:S(2)}, u32[]{:S(2)}) %collective-permute-start.11) | collective-permute-done | bytes 131104 | tf_op jit(solution)/shard_map/ppermute | solution.py:864
  61.9 2.4 all-to-all-done
  65.4 3.7 %all-to-all-start.2 = ((bf16[4,2,64,1024]{3,2,1,0:T(8,128)(2,1)}), bf16[4,2,64,1024]{3,2,1,0:T(8,128)(2,1)S(1)}, u32[]{:S(2)}, u32[]{:S(2)}) async-start(bf16[4,2,64,1024]{3,2,1,0:T(8,128)(2,1)} %broadcast_in_dim.28), calls=%async_computation.2 | async-start | bytes 2097152 | tf_op jit(solution)/shard_map/all_to_all | solution.py:1017
  71.1 1.6 collective-permute-start.16
  73.4 1.7 fusion.15
  75.1 2.0 collective-permute-start.17
  77.1 1.5 collective-permute-start.18
  79.7 21.8 %mixer_forward.1 = (bf16[4,2,512,128]{3,2,1,0:T(8,128)(2,1)}, f32[16,128]{1,0:T(8,128)}, f32[8,1024]{1,0:T(8,128)}, bf16[1024,1024]{1,0:T(8,128)(2,1)}, bf16[102...) custom-call(s32[4]{0:T(128)} %pad_add_fusion.pos_ref, ...), custom_call_target="tpu_custom_call" | custom-call | flops 25000000 | bytes 1024 | tf_op jit(solution)/shard_map/mixer_forward/pallas_call | solution.py:841
  103.9 1.6 collective-permute-start.21
  105.5 4.0 %all-to-all-start.1 = ((bf16[8,512,128]{2,1,0:T(8,128)(2,1)}), bf16[8,512,128]{2,1,0:T(8,128)(2,1)S(1)}, u32[]{:S(2)}, u32[]{:S(2)}) async-start(bf16[8,512,128]{2,1,0:T(8,128)(2,1)} %bitcast.211), calls=%async_computation.1 | async-start | bytes 2097152 | tf_op jit(solution)/shard_map/all_to_all | solution.py:1050
  109.5 11.4 %collective-permute-done.21 = bf16[8,32,1408]{2,1,0:T(8,128)(2,1)S(1)} collective-permute-done((bf16[8,32,1408]{2,1,0:T(8,128)(2,1)S(1)}, bf16[8,32,1408]{2,1,0:T(8,128)(2,1)S(1)}, u32[]{:S(2)}, u32[]{:S(2)}) %collective-permute-start.21) | collective-permute-done | bytes 720928 | tf_op jit(solution)/shard_map/ppermute | solution.py:864
  124.7 2.3 pad_maximum_fusion.4.cot_ref
  127.0 1.4 select_bitcast_fusion.1
  130.9 11.6 %feed_forward.1 = (bf16[1024,1024]{1,0:T(8,128)(2,1)}, bf16[512,1024]{1,0:T(8,128)(2,1)}, bf16[512,1408]{1,0:T(8,128)(2,1)}, bf16[512,704]{1,0:T(8,128)(2,1)}, b...) custom-call(s32[4]{0:T(128)} %pad_add_fusion.pos_ref, ...), custom_call_target="tpu_custom_call" | custom-call | flops 12000000 | bytes 1024 | tf_op jit(solution)/shard_map/feed_forward/pallas_call | solution.py:841
  142.5 1.7 collective-permute-start.24
  144.2 1.5 collective-permute-start.25
  146.0 7.1 %feed_forward_grads.1 = (bf16[8,64,1408]{2,1,0:T(8,128)(2,1)}, bf16[8,64,1408]{2,1,0:T(8,128)(2,1)}, bf16[2,176,1024]{2,1,0:T(8,128)(2,1)}, bf16[2,176,1024]{2,1,0:T(8,128)(2,1)}, bf16[4,2,64,1024]{3,2,1,0:T(8,128)(2,1)}) custom-call(s32[4]{0:T(128)} %pad_add_fusion.pos_ref, bf16[512,1024]{1,0:T(8,128)(2,1)} %get-tuple-element.175.normed_ref, ...), custom_call_target="tpu_custom_call" | custom-call | flops 6000000 | bytes 1024 | tf_op jit(solution)/shard_map/feed_forward_grads/pallas_call | solution.py:841
  153.6 4.3 %collective-permute-done.26.rest_2_ = bf16[2,64,1024]{2,1,0:T(8,128)(2,1)S(1)} collective-permute-done((bf16[2,64,1024]{2,1,0:T(8,128)(2,1)}, bf16[2,64,1024]{2,1,0:T(8,128)(2,1)S(1)}, u32[]{:S(2)}, u32[]{:S(2)}) %collective-permute-start.26) | collective-permute-done | bytes 262176 | tf_op jit(solution)/shard_map/ppermute | solution.py:864
  158.6 4.0 %branch_gradient.1 = (f32[2,64,1024]{2,1,0:T(8,128)}, bf16[2,64,1024]{2,1,0:T(8,128)(2,1)}, bf16[8,2,64,128]{3,2,1,0:T(8,128)(2,1)}) custom-call(s32[4]{0:T(128)} %pad_add_fusion.pos_ref, f32[2,64,1024]{2,1,0:T(8,128)} %get-tuple-element.181.norm_ref, f32[2,64,1024]{2,1,0:T(8,128)} %get-tuple-element.170.res_ref, ...), custom_call_target="tpu_custom_call" | custom-call | flops 2000000 | bytes 1024 | tf_op jit(solution)/shard_map/branch_gradient/pallas_call | solution.py:841
  162.5 3.8 %all-to-all-start.3 = ((bf16[8,2,64,128]{3,2,1,0:T(8,128)(2,1)}), bf16[8,2,64,128]{3,2,1,0:T(8,128)(2,1)S(1)}, u32[]{:S(2)}, u32[]{:S(2)}) async-start(bf16[8,2,64,128]{3,2,1,0:T(8,128)(2,1)} %get-tuple-element.186), calls=%async_computation.3 | async-start | bytes 524288 | tf_op jit(solution)/shard_map/all_to_all | solution.py:1116
  167.3 1.4 add_convert_fusion.1
  168.6 2.1 add_convert_fusion
  170.8 1.6 all-to-all-done.3.dh_ref
  172.4 3.7 %all-to-all-start.4 = ((bf16[4,2,64,1024]{3,2,1,0:T(8,128)(2,1)}), bf16[4,2,64,1024]{3,2,1,0:T(8,128)(2,1)S(1)}, u32[]{:S(2)}, u32[]{:S(2)}) async-start(bf16[4,2,64,1024]{3,2,1,0:T(8,128)(2,1)} %get-tuple-element.210), calls=%async_computation.4 | async-start | bytes 2097152 | tf_op jit(solution)/shard_map/all_to_all | solution.py:1124
  176.4 2.3 collective-permute-start.29
  179.3 2.0 collective-permute-start.31
  181.3 1.5 collective-permute-start.32
  182.8 21.7 %mixer_backward.1 = (bf16[8,64,1024]{2,1,0:T(8,128)(2,1)}, bf16[8,64,1024]{2,1,0:T(8,128)(2,1)}, bf16[8,64,640]{2,1,0:T(8,128)(2,1)}, bf16[8,64,640]{2,1,0:T(8,128)(2,1)}) custom-call(s32[4]{0:T(128)} %pad_add_fusion.pos_ref, bf16[8,2,64,128]{3,2,1,0:T(8,128)(2,1)} %copy-done.21, f32[1032,8]{1,0:T(8,128)} %pad_convert_fusion.flag_ref, ...), custom_call_target="tpu_custom_call" | custom-call | flops 25000000 | bytes 1024 | tf_op jit(solution)/shard_map/mixer_backward/pallas_call | solution.py:841
  204.7 7.4 %collective-permute-done.32.refs_2_ = bf16[2,64,1024]{2,1,0:T(8,128)(2,1)S(1)} collective-permute-done((bf16[2,64,1024]{2,1,0:T(8,128)(2,1)S(1)}, bf16[2,64,1024]{2,1,0:T(8,128)(2,1)S(1)}, u32[]{:S(2)}, u32[]{:S(2)}) %collective-permute-start.32) | collective-permute-done | bytes 262176 | tf_op jit(solution)/shard_map/ppermute | solution.py:864
  212.2 5.3 %collective-permute-done.33.refs_3_ = bf16[2,64,1024]{2,1,0:T(8,128)(2,1)S(1)} collective-permute-done((bf16[2,64,1024]{2,1,0:T(8,128)(2,1)S(1)}, bf16[2,64,1024]{2,1,0:T(8,128)(2,1)S(1)}, u32[]{:S(2)}, u32[]{:S(2)}) %collective-permute-start.33) | collective-permute-done | bytes 262176 | tf_op jit(solution)/shard_map/ppermute | solution.py:864
  219.1 2.9 output_gradient.1
  222.9 2.4 merge_heads.1
  226.5 2.8 token_pieces.1
  229.2 3.5 %all-to-all-start.5 = ((bf16[4,2,64,1024]{3,2,1,0:T(8,128)(2,1)}), bf16[4,2,64,1024]{3,2,1,0:T(8,128)(2,1)S(1)}, u32[]{:S(2)}, u32[]{:S(2)}) async-start(bf16[4,2,64,1024]{3,2,1,0:T(8,128)(2,1)} %token_pieces.1), calls=%async_computation.5 | async-start | bytes 2097152 | tf_op jit(solution)/shard_map/all_to_all | solution.py:1210
  234.7 1.5 collective-permute-start.36
  236.3 2.3 collective-permute-start.37
  240.2 5.8 %collective-permute-done.39 = bf16[4,1,32,1408]{3,2,0,1:T(8,128)(2,1)S(1)} collective-permute-done((bf16[4,1,32,1408]{3,2,0,1:T(8,128)(2,1)S(1)}, bf16[4,1,32,1408]{3,2,0,1:T(8,128)(2,1)S(1)}, u32[]{:S(2)}, u32[]{:S(2)}) %collective-permute-start.39) | collective-permute-done | bytes 360480 | tf_op jit(solution)/shard_map/ppermute | solution.py:864
  246.9 9.4 %all-to-all-done.5.got_ref = bf16[4,2,64,1024]{3,2,1,0:T(8,128)(2,1)S(1)} async-done(((bf16[4,2,64,1024]{3,2,1,0:T(8,128)(2,1)}), bf16[4,2,64,1024]{3,2,1,0:T(8,128)(2,1)S(1)}, u32[]{:S(2)}, u32[]{:S(2)}) %all-to-all-start.5) | async-done | bytes 1048608 | tf_op jit(solution)/shard_map/all_to_all | solution.py:1210
  257.4 2.5 input_gradient.1
  260.0 1.6 select_bitcast_fusion.13
  261.6 4.1 %all-to-all-start.6 = ((bf16[4,32,1408]{2,1,0:T(8,128)(2,1)}), bf16[4,32,1408]{2,1,0:T(8,128)(2,1)}, u32[]{:S(2)}, u32[]{:S(2)}) async-start(bf16[4,32,1408]{2,1,0:T(8,128)(2,1)} %fusion.2), calls=%async_computation.6 | async-start | bytes 720896 | tf_op jit(solution)/shard_map/all_to_all | solution.py:1220
  266.7 1.4 collective-permute-done.38.refs_3_
  268.1 1.7 collective-permute-start.48
  269.8 1.4 collective-permute-start.47
  271.2 2.0 add_partners.1
  273.2 2.1 collective-permute-start.44
  275.4 1.7 collective-permute-start.45
  278.7 2.7 collective-permute-done.47
  283.3 2.2 collective-permute-done.46.refs_3_
  286.1 1.9 spread_heads.1
  291.6 2.0 spread_pair.1
  (241 shorter events, 47.7 us)
Async XLA Ops:
  0.6 17.1 %copy-start.41 = (s32[2,1,1024]{2,1,0:T(1,128)S(1)}, s32[2,1,1024]{2,1,0:T(1,128)}, u32[]{:S(2)}) copy-start(s32[2,1,1024]{2,1,0:T(1,128)} %param.18) | copy-start | bytes 24580
  0.7 16.4 %copy-start.30 = (bf16[2,1,64,1024]{3,2,1,0:T(8,128)(2,1)S(1)}, bf16[2,1,64,1024]{3,2,1,0:T(8,128)(2,1)}, u32[]{:S(2)}) copy-start(bf16[2,1,64,1024]{3,2,1,0:T(8,128)(2,1)} %param.17) | copy-start | bytes 786436
  0.7 17.7 %copy-start.38 = (bf16[32,2816]{1,0:T(8,128)(2,1)S(1)}, bf16[32,2816]{1,0:T(8,128)(2,1)}, u32[]{:S(2)}) copy-start(bf16[32,2816]{1,0:T(8,128)(2,1)} %param.25) | copy-start | bytes 540676
  3.9 15.0 %copy-start.39 = (bf16[32,2816]{1,0:T(8,128)(2,1)S(1)}, bf16[32,2816]{1,0:T(8,128)(2,1)}, u32[]{:S(2)}) copy-start(bf16[32,2816]{1,0:T(8,128)(2,1)} %param.26) | copy-start | bytes 540676
  3.9 17.0 %collective-permute-start = (bf16[32,1152]{1,0:T(8,128)(2,1)}, bf16[32,1152]{1,0:T(8,128)(2,1)S(1)}, u32[]{:S(2)}, u32[]{:S(2)}) collective-permute-start(bf16[32,1152]{1,0:T(8,128)(2,1)} %get-tuple-element.138), channel_id=1, source_target_pairs={{0,4},{4,0},{8,12},{12,8},{1,5},{5,1},{9,13},{13,9},{2,6},{6,2},{1... | collective-permute-start | bytes 221192 | tf_op jit(solution)/shard_map/ppermute | solution.py:864
  6.9 14.0 %collective-permute-start.1 = (bf16[32,1152]{1,0:T(8,128)(2,1)}, bf16[32,1152]{1,0:T(8,128)(2,1)S(1)}, u32[]{:S(2)}, u32[]{:S(2)}) collective-permute-start(bf16[32,1152]{1,0:T(8,128)(2,1)} %get-tuple-element.139), channel_id=1, source_target_pairs={{0,8},{4,12},{8,0},{12,4},{1,9},{5,13},{9,1},{13,5},{2,10},{6,14},... | collective-permute-start | bytes 221192 | tf_op jit(solution)/shard_map/ppermute | solution.py:864
  8.4 12.4 %collective-permute-start.2 = (bf16[32,1152]{1,0:T(8,128)(2,1)}, bf16[32,1152]{1,0:T(8,128)(2,1)S(1)}, u32[]{:S(2)}, u32[]{:S(2)}) collective-permute-start(bf16[32,1152]{1,0:T(8,128)(2,1)} %get-tuple-element.140), channel_id=1, source_target_pairs={{0,12},{4,8},{8,4},{12,0},{1,13},{5,9},{9,5},{13,1},{2,14},{6,10},... | collective-permute-start | bytes 221192 | tf_op jit(solution)/shard_map/ppermute | solution.py:864
  9.4 11.5 %collective-permute-start.3 = (bf16[64,1024]{1,0:T(8,128)(2,1)S(1)}, bf16[64,1024]{1,0:T(8,128)(2,1)S(1)}, u32[]{:S(2)}, u32[]{:S(2)}) collective-permute-start(bf16[64,1024]{1,0:T(8,128)(2,1)S(1)} %get-tuple-element.333), channel_id=1, source_target_pairs={{0,16},{16,0},{1,17},{17,1},{2,18},{18,2},{3,19},{19,3},{4,20},{20... | collective-permute-start | bytes 393224 | tf_op jit(solution)/shard_map/ppermute | solution.py:864
  20.9 21.4 %copy-start.20 = (bf16[2,64,1024]{2,1,0:T(8,128)(2,1)}, bf16[2,64,1024]{2,1,0:T(8,128)(2,1)S(1)}, u32[]{:S(2)}) copy-start(bf16[2,64,1024]{2,1,0:T(8,128)(2,1)S(1)} %get-tuple-element.331.x_ref) | copy-start | bytes 786436
  21.0 7.2 %collective-permute-start.5 = (bf16[2,64,1024]{2,1,0:T(8,128)(2,1)S(1)}, bf16[2,64,1024]{2,1,0:T(8,128)(2,1)S(1)}, u32[]{:S(2)}, u32[]{:S(2)}) collective-permute-start(bf16[2,64,1024]{2,1,0:T(8,128)(2,1)S(1)} %get-tuple-element.331.x_ref), channel_id=1, source_target_pairs={{0,4},{4,0},{8,12},{12,8},{1,5},{5,1},{9,13},{13,9},{2,6},{6,2},{1... | collective-permute-start | bytes 786440 | tf_op jit(solution)/shard_map/ppermute | solution.py:864
  22.5 17.0 %collective-permute-start.6 = (bf16[2,64,1024]{2,1,0:T(8,128)(2,1)S(1)}, bf16[2,64,1024]{2,1,0:T(8,128)(2,1)S(1)}, u32[]{:S(2)}, u32[]{:S(2)}) collective-permute-start(bf16[2,64,1024]{2,1,0:T(8,128)(2,1)S(1)} %get-tuple-element.331.x_ref), channel_id=1, source_target_pairs={{0,8},{4,12},{8,0},{12,4},{1,9},{5,13},{9,1},{13,5},{2,10},{6,14},... | collective-permute-start | bytes 786440 | tf_op jit(solution)/shard_map/ppermute | solution.py:864
  24.1 18.3 %collective-permute-start.7 = (bf16[2,64,1024]{2,1,0:T(8,128)(2,1)S(1)}, bf16[2,64,1024]{2,1,0:T(8,128)(2,1)S(1)}, u32[]{:S(2)}, u32[]{:S(2)}) collective-permute-start(bf16[2,64,1024]{2,1,0:T(8,128)(2,1)S(1)} %get-tuple-element.331.x_ref), channel_id=1, source_target_pairs={{0,12},{4,8},{8,4},{12,0},{1,13},{5,9},{9,5},{13,1},{2,14},{6,10},... | collective-permute-start | bytes 786440 | tf_op jit(solution)/shard_map/ppermute | solution.py:864
  24.6 17.9 %collective-permute-start.4 = (bf16[4,32,1152]{2,1,0:T(8,128)(2,1)S(1)}, bf16[4,32,1152]{2,1,0:T(8,128)(2,1)S(1)}, u32[]{:S(2)}, u32[]{:S(2)}) collective-permute-start(bf16[4,32,1152]{2,1,0:T(8,128)(2,1)S(1)} %get-tuple-element.323), channel_id=1, source_target_pairs={{0,16},{16,0},{1,17},{17,1},{2,18},{18,2},{3,19},{19,3},{4,20},{20... | collective-permute-start | bytes 884744 | tf_op jit(solution)/shard_map/ppermute | solution.py:864
  25.2 17.4 %collective-permute-start.8 = (bf16[32,1024]{1,0:T(8,128)(2,1)S(1)}, bf16[32,1024]{1,0:T(8,128)(2,1)S(1)}, u32[]{:S(2)}, u32[]{:S(2)}) collective-permute-start(bf16[32,1024]{1,0:T(8,128)(2,1)S(1)} %copy-done.31), channel_id=1, source_target_pairs={{0,16},{16,0},{1,17},{17,1},{2,18},{18,2},{3,19},{19,3},{4,20},{20... | collective-permute-start | bytes 196616 | tf_op jit(solution)/shard_map/ppermute | solution.py:864
  42.5 15.8 %copy-start.1 = (bf16[4,2,64,1024]{3,2,1,0:T(8,128)(2,1)}, bf16[4,2,64,1024]{3,2,1,0:T(8,128)(2,1)S(1)}, u32[]{:S(2)}) copy-start(bf16[4,2,64,1024]{3,2,1,0:T(8,128)(2,1)S(1)} %pad_maximum_fusion.3.xown_ref) | copy-start | bytes 3145732
  42.6 15.7 %collective-permute-start.9 = (bf16[8,32,1152]{2,1,0:T(8,128)(2,1)S(1)}, bf16[8,32,1152]{2,1,0:T(8,128)(2,1)S(1)}, u32[]{:S(2)}, u32[]{:S(2)}) collective-permute-start(bf16[8,32,1152]{2,1,0:T(8,128)(2,1)S(1)} %bitcast.207), channel_id=1, source_target_pairs={{0,1},{1,0},{2,3},{3,2},{4,5},{5,4},{6,7},{7,6},{8,9},{9,8},{10,11... | collective-permute-start | bytes 1769480 | tf_op jit(solution)/shard_map/ppermute | solution.py:864
  44.2 14.0 %collective-permute-start.13 = (bf16[2,32,1024]{2,1,0:T(8,128)(2,1)S(1)}, bf16[2,32,1024]{2,1,0:T(8,128)(2,1)S(1)}, u32[]{:S(2)}, u32[]{:S(2)}) collective-permute-start(bf16[2,32,1024]{2,1,0:T(8,128)(2,1)S(1)} %pad_maximum_fusion.14), channel_id=1, source_target_pairs={{0,1},{1,0},{2,3},{3,2},{4,5},{5,4},{6,7},{7,6},{8,9},{9,8},{10,11... | collective-permute-start | bytes 393224 | tf_op jit(solution)/shard_map/ppermute | solution.py:864
  44.8 19.5 %collective-permute-start.10 = (bf16[4,2,64,1024]{3,2,1,0:T(8,128)(2,1)S(1)}, bf16[4,2,64,1024]{3,2,1,0:T(8,128)(2,1)}, u32[]{:S(2)}, u32[]{:S(2)}) collective-permute-start(bf16[4,2,64,1024]{3,2,1,0:T(8,128)(2,1)S(1)} %pad_maximum_fusion.3.xown_ref), channel_id=1, source_target_pairs={{0,2},{2,0},{1,3},{3,1},{4,6},{6,4},{5,7},{7,5},{8,10},{10,8},{9,1... | collective-permute-start | bytes 3145736 | tf_op jit(solution)/shard_map/ppermute | solution.py:864
  44.8 17.2 %collective-permute-start.12 = (bf16[88,1024]{1,0:T(8,128)(2,1)S(1)}, bf16[88,1024]{1,0:T(8,128)(2,1)}, u32[]{:S(2)}, u32[]{:S(2)}) collective-permute-start(bf16[88,1024]{1,0:T(8,128)(2,1)S(1)} %copy-done.40), channel_id=1, source_target_pairs={{0,16},{16,0},{1,17},{17,1},{2,18},{18,2},{3,19},{19,3},{4,20},{20... | collective-permute-start | bytes 540680 | tf_op jit(solution)/shard_map/ppermute | solution.py:864
  47.1 14.8 %collective-permute-start.11 = (bf16[64,1024]{1,0:T(8,128)(2,1)}, bf16[64,1024]{1,0:T(8,128)(2,1)}, u32[]{:S(2)}, u32[]{:S(2)}) collective-permute-start(bf16[64,1024]{1,0:T(8,128)(2,1)} %get-tuple-element.148), channel_id=1, source_target_pairs={{0,16},{16,0},{1,17},{17,1},{2,18},{18,2},{3,19},{19,3},{4,20},{20... | collective-permute-start | bytes 393224 | tf_op jit(solution)/shard_map/ppermute | solution.py:864
  47.7 16.6 %all-to-all-start = ((bf16[4,32,1408]{2,1,0:T(8,128)(2,1)}), bf16[4,32,1408]{2,1,0:T(8,128)(2,1)S(1)}, u32[]{:S(2)}, u32[]{:S(2)}) async-start(bf16[4,32,1408]{2,1,0:T(8,128)(2,1)} %reshape.392), calls=%async_computation | async-start | bytes 720896 | tf_op jit(solution)/shard_map/all_to_all | solution.py:1008
  58.6 10.6 %copy-start.2 = (bf16[8,2,32,1152]{3,2,1,0:T(8,128)(2,1)}, bf16[8,2,32,1152]{3,2,1,0:T(8,128)(2,1)S(1)}, u32[]{:S(2)}) copy-start(bf16[8,2,32,1152]{3,2,1,0:T(8,128)(2,1)S(1)} %pad_maximum_fusion.2) | copy-start | bytes 3538948
  65.4 36.7 %all-to-all-start.2 = ((bf16[4,2,64,1024]{3,2,1,0:T(8,128)(2,1)}), bf16[4,2,64,1024]{3,2,1,0:T(8,128)(2,1)S(1)}, u32[]{:S(2)}, u32[]{:S(2)}) async-start(bf16[4,2,64,1024]{3,2,1,0:T(8,128)(2,1)} %broadcast_in_dim.28), calls=%async_computation.2 | async-start | bytes 2097152 | tf_op jit(solution)/shard_map/all_to_all | solution.py:1017
  69.3 9.3 %collective-permute-start.14 = (bf16[8,64,640]{2,1,0:T(8,128)(2,1)S(1)}, bf16[8,64,640]{2,1,0:T(8,128)(2,1)S(1)}, u32[]{:S(2)}, u32[]{:S(2)}) collective-permute-start(bf16[8,64,640]{2,1,0:T(8,128)(2,1)S(1)} %pad_maximum_fusion.7), channel_id=1, source_target_pairs={{0,2},{2,0},{1,3},{3,1},{4,6},{6,4},{5,7},{7,5},{8,10},{10,8},{9,1... | collective-permute-start | bytes 1966088 | tf_op jit(solution)/shard_map/ppermute | solution.py:864
  71.1 31.0 %collective-permute-start.16 = (bf16[2,88,1024]{2,1,0:T(8,128)(2,1)S(1)}, bf16[2,88,1024]{2,1,0:T(8,128)(2,1)}, u32[]{:S(2)}, u32[]{:S(2)}) collective-permute-start(bf16[2,88,1024]{2,1,0:T(8,128)(2,1)S(1)} %pad_maximum_fusion.9), channel_id=1, source_target_pairs={{0,1},{1,0},{2,3},{3,2},{4,5},{5,4},{6,7},{7,6},{8,9},{9,8},{10,11... | collective-permute-start | bytes 1081352 | tf_op jit(solution)/shard_map/ppermute | solution.py:864
  72.7 29.4 %collective-permute-start.15 = (bf16[4,32,1408]{2,1,0:T(8,128)(2,1)S(1)}, bf16[4,32,1408]{2,1,0:T(8,128)(2,1)}, u32[]{:S(2)}, u32[]{:S(2)}) collective-permute-start(bf16[4,32,1408]{2,1,0:T(8,128)(2,1)S(1)} %all-to-all-done), channel_id=1, source_target_pairs={{0,16},{16,0},{1,17},{17,1},{2,18},{18,2},{3,19},{19,3},{4,20},{20... | collective-permute-start | bytes 1081352 | tf_op jit(solution)/shard_map/ppermute | solution.py:864
  75.1 26.4 %collective-permute-start.17 = (bf16[2,64,1024]{2,1,0:T(8,128)(2,1)}, bf16[2,64,1024]{2,1,0:T(8,128)(2,1)S(1)}, u32[]{:S(2)}, u32[]{:S(2)}) collective-permute-start(bf16[2,64,1024]{2,1,0:T(8,128)(2,1)} %get-tuple-element.325), channel_id=1, source_target_pairs={{0,4},{4,0},{8,12},{12,8},{1,5},{5,1},{9,13},{13,9},{2,6},{6,2},{1... | collective-permute-start | bytes 786440 | tf_op jit(solution)/shard_map/ppermute | solution.py:864
  77.1 24.4 %collective-permute-start.18 = (bf16[2,64,1024]{2,1,0:T(8,128)(2,1)}, bf16[2,64,1024]{2,1,0:T(8,128)(2,1)}, u32[]{:S(2)}, u32[]{:S(2)}) collective-permute-start(bf16[2,64,1024]{2,1,0:T(8,128)(2,1)} %get-tuple-element.325), channel_id=1, source_target_pairs={{0,8},{4,12},{8,0},{12,4},{1,9},{5,13},{9,1},{13,5},{2,10},{6,14},... | collective-permute-start | bytes 786440 | tf_op jit(solution)/shard_map/ppermute | solution.py:864
  78.6 23.5 %collective-permute-start.19 = (bf16[2,64,1024]{2,1,0:T(8,128)(2,1)}, bf16[2,64,1024]{2,1,0:T(8,128)(2,1)S(1)}, u32[]{:S(2)}, u32[]{:S(2)}) collective-permute-start(bf16[2,64,1024]{2,1,0:T(8,128)(2,1)} %get-tuple-element.325), channel_id=1, source_target_pairs={{0,12},{4,8},{8,4},{12,0},{1,13},{5,9},{9,5},{13,1},{2,14},{6,10},... | collective-permute-start | bytes 786440 | tf_op jit(solution)/shard_map/ppermute | solution.py:864
  103.9 17.0 %collective-permute-start.21 = (bf16[8,32,1408]{2,1,0:T(8,128)(2,1)S(1)}, bf16[8,32,1408]{2,1,0:T(8,128)(2,1)S(1)}, u32[]{:S(2)}, u32[]{:S(2)}) collective-permute-start(bf16[8,32,1408]{2,1,0:T(8,128)(2,1)S(1)} %bitcast.206), channel_id=1, source_target_pairs={{0,1},{1,0},{2,3},{3,2},{4,5},{5,4},{6,7},{7,6},{8,9},{9,8},{10,11... | collective-permute-start | bytes 2162696 | tf_op jit(solution)/shard_map/ppermute | solution.py:864
  105.5 24.4 %all-to-all-start.1 = ((bf16[8,512,128]{2,1,0:T(8,128)(2,1)}), bf16[8,512,128]{2,1,0:T(8,128)(2,1)S(1)}, u32[]{:S(2)}, u32[]{:S(2)}) async-start(bf16[8,512,128]{2,1,0:T(8,128)(2,1)} %bitcast.211), calls=%async_computation.1 | async-start | bytes 2097152 | tf_op jit(solution)/shard_map/all_to_all | solution.py:1050
  121.3 8.6 %collective-permute-start.22 = (bf16[2,4,64,1408]{3,2,1,0:T(8,128)(2,1)S(1)}, bf16[2,4,64,1408]{3,2,1,0:T(8,128)(2,1)}, u32[]{:S(2)}, u32[]{:S(2)}) collective-permute-start(bf16[2,4,64,1408]{3,2,1,0:T(8,128)(2,1)S(1)} %bitcast.200), channel_id=1, source_target_pairs={{0,2},{2,0},{1,3},{3,1},{4,6},{6,4},{5,7},{7,5},{8,10},{10,8},{9,1... | collective-permute-start | bytes 4325384 | tf_op jit(solution)/shard_map/ppermute | solution.py:864
  124.2 2.8 collective-permute-start.23
  124.2 5.7 %collective-permute-start.20 = (bf16[4,2,64,1024]{3,2,1,0:T(8,128)(2,1)S(1)}, bf16[4,2,64,1024]{3,2,1,0:T(8,128)(2,1)}, u32[]{:S(2)}, u32[]{:S(2)}) collective-permute-start(bf16[4,2,64,1024]{3,2,1,0:T(8,128)(2,1)S(1)} %copy-done.5), channel_id=1, source_target_pairs={{0,2},{2,0},{1,3},{3,1},{4,6},{6,4},{5,7},{7,5},{8,10},{10,8},{9,1... | collective-permute-start | bytes 3145736 | tf_op jit(solution)/shard_map/ppermute | solution.py:864
  142.5 10.6 %collective-permute-start.24 = (bf16[2,64,1024]{2,1,0:T(8,128)(2,1)}, bf16[2,64,1024]{2,1,0:T(8,128)(2,1)S(1)}, u32[]{:S(2)}, u32[]{:S(2)}) collective-permute-start(bf16[2,64,1024]{2,1,0:T(8,128)(2,1)} %get-tuple-element.171), channel_id=1, source_target_pairs={{0,4},{4,0},{8,12},{12,8},{1,5},{5,1},{9,13},{13,9},{2,6},{6,2},{1... | collective-permute-start | bytes 786440 | tf_op jit(solution)/shard_map/ppermute | solution.py:864
  144.2 9.4 %collective-permute-start.25 = (bf16[2,64,1024]{2,1,0:T(8,128)(2,1)}, bf16[2,64,1024]{2,1,0:T(8,128)(2,1)S(1)}, u32[]{:S(2)}, u32[]{:S(2)}) collective-permute-start(bf16[2,64,1024]{2,1,0:T(8,128)(2,1)} %get-tuple-element.172), channel_id=1, source_target_pairs={{0,8},{4,12},{8,0},{12,4},{1,9},{5,13},{9,1},{13,5},{2,10},{6,14},... | collective-permute-start | bytes 786440 | tf_op jit(solution)/shard_map/ppermute | solution.py:864
  145.6 12.2 %collective-permute-start.26 = (bf16[2,64,1024]{2,1,0:T(8,128)(2,1)}, bf16[2,64,1024]{2,1,0:T(8,128)(2,1)S(1)}, u32[]{:S(2)}, u32[]{:S(2)}) collective-permute-start(bf16[2,64,1024]{2,1,0:T(8,128)(2,1)} %get-tuple-element.173), channel_id=1, source_target_pairs={{0,12},{4,8},{8,4},{12,0},{1,13},{5,9},{9,5},{13,1},{2,14},{6,10},... | collective-permute-start | bytes 786440 | tf_op jit(solution)/shard_map/ppermute | solution.py:864
  157.9 8.5 %collective-permute-start.27 = (bf16[8,64,1408]{2,1,0:T(8,128)(2,1)}, bf16[8,64,1408]{2,1,0:T(8,128)(2,1)S(1)}, u32[]{:S(2)}, u32[]{:S(2)}) collective-permute-start(bf16[8,64,1408]{2,1,0:T(8,128)(2,1)} %get-tuple-element.189), channel_id=1, source_target_pairs={{0,2},{2,0},{1,3},{3,1},{4,6},{6,4},{5,7},{7,5},{8,10},{10,8},{9,1... | collective-permute-start | bytes 4325384 | tf_op jit(solution)/shard_map/ppermute | solution.py:864
  157.9 8.5 %collective-permute-start.28 = (bf16[2,176,1024]{2,1,0:T(8,128)(2,1)}, bf16[2,176,1024]{2,1,0:T(8,128)(2,1)S(1)}, u32[]{:S(2)}, u32[]{:S(2)}) collective-permute-start(bf16[2,176,1024]{2,1,0:T(8,128)(2,1)} %get-tuple-element.190), channel_id=1, source_target_pairs={{0,2},{2,0},{1,3},{3,1},{4,6},{6,4},{5,7},{7,5},{8,10},{10,8},{9,1... | collective-permute-start | bytes 2162696 | tf_op jit(solution)/shard_map/ppermute | solution.py:864
  162.5 9.9 %all-to-all-start.3 = ((bf16[8,2,64,128]{3,2,1,0:T(8,128)(2,1)}), bf16[8,2,64,128]{3,2,1,0:T(8,128)(2,1)S(1)}, u32[]{:S(2)}, u32[]{:S(2)}) async-start(bf16[8,2,64,128]{3,2,1,0:T(8,128)(2,1)} %get-tuple-element.186), calls=%async_computation.3 | async-start | bytes 524288 | tf_op jit(solution)/shard_map/all_to_all | solution.py:1116
  172.4 45.8 %all-to-all-start.4 = ((bf16[4,2,64,1024]{3,2,1,0:T(8,128)(2,1)}), bf16[4,2,64,1024]{3,2,1,0:T(8,128)(2,1)S(1)}, u32[]{:S(2)}, u32[]{:S(2)}) async-start(bf16[4,2,64,1024]{3,2,1,0:T(8,128)(2,1)} %get-tuple-element.210), calls=%async_computation.4 | async-start | bytes 2097152 | tf_op jit(solution)/shard_map/all_to_all | solution.py:1124
  176.4 41.8 %collective-permute-start.29 = (bf16[4,2,32,1408]{3,2,0,1:T(8,128)(2,1)S(1)}, bf16[4,2,32,1408]{3,2,0,1:T(8,128)(2,1)S(1)}, u32[]{:S(2)}, u32[]{:S(2)}) collective-permute-start(bf16[4,2,32,1408]{3,2,0,1:T(8,128)(2,1)S(1)} %bitcast.212), channel_id=1, source_target_pairs={{0,16},{16,0},{1,17},{17,1},{2,18},{18,2},{3,19},{19,3},{4,20},{20... | collective-permute-start | bytes 2162696 | tf_op jit(solution)/shard_map/ppermute | solution.py:864
  178.7 25.8 %collective-permute-start.30 = (bf16[2,1,88,1024]{3,2,0,1:T(8,128)(2,1)S(1)}, bf16[2,1,88,1024]{3,2,0,1:T(8,128)(2,1)S(1)}, u32[]{:S(2)}, u32[]{:S(2)}) collective-permute-start(bf16[2,1,88,1024]{3,2,0,1:T(8,128)(2,1)S(1)} %select_bitcast_fusion.7), channel_id=1, source_target_pairs={{0,1},{1,0},{2,3},{3,2},{4,5},{5,4},{6,7},{7,6},{8,9},{9,8},{10,11... | collective-permute-start | bytes 1081352 | tf_op jit(solution)/shard_map/ppermute | solution.py:864
  179.3 25.4 %collective-permute-start.31 = (bf16[2,64,1024]{2,1,0:T(8,128)(2,1)S(1)}, bf16[2,64,1024]{2,1,0:T(8,128)(2,1)S(1)}, u32[]{:S(2)}, u32[]{:S(2)}) collective-permute-start(bf16[2,64,1024]{2,1,0:T(8,128)(2,1)S(1)} %copy-done.32), channel_id=1, source_target_pairs={{0,4},{4,0},{8,12},{12,8},{1,5},{5,1},{9,13},{13,9},{2,6},{6,2},{1... | collective-permute-start | bytes 786440 | tf_op jit(solution)/shard_map/ppermute | solution.py:864
  181.3 30.9 %collective-permute-start.32 = (bf16[2,64,1024]{2,1,0:T(8,128)(2,1)S(1)}, bf16[2,64,1024]{2,1,0:T(8,128)(2,1)S(1)}, u32[]{:S(2)}, u32[]{:S(2)}) collective-permute-start(bf16[2,64,1024]{2,1,0:T(8,128)(2,1)S(1)} %copy-done.32), channel_id=1, source_target_pairs={{0,8},{4,12},{8,0},{12,4},{1,9},{5,13},{9,1},{13,5},{2,10},{6,14},... | collective-permute-start | bytes 786440 | tf_op jit(solution)/shard_map/ppermute | solution.py:864
  182.7 34.8 %collective-permute-start.33 = (bf16[2,64,1024]{2,1,0:T(8,128)(2,1)S(1)}, bf16[2,64,1024]{2,1,0:T(8,128)(2,1)S(1)}, u32[]{:S(2)}, u32[]{:S(2)}) collective-permute-start(bf16[2,64,1024]{2,1,0:T(8,128)(2,1)S(1)} %copy-done.32), channel_id=1, source_target_pairs={{0,12},{4,8},{8,4},{12,0},{1,13},{5,9},{9,5},{13,1},{2,14},{6,10},... | collective-permute-start | bytes 786440 | tf_op jit(solution)/shard_map/ppermute | solution.py:864
  204.7 12.8 %copy-start.35 = (bf16[2,64,1024]{2,1,0:T(8,128)(2,1)}, bf16[2,64,1024]{2,1,0:T(8,128)(2,1)S(1)}, u32[]{:S(2)}) copy-start(bf16[2,64,1024]{2,1,0:T(8,128)(2,1)S(1)} %collective-permute-done.31.refs_1_) | copy-start | bytes 786436
  218.2 7.1 %collective-permute-start.35 = (bf16[8,64,1024]{2,1,0:T(8,128)(2,1)}, bf16[8,64,1024]{2,1,0:T(8,128)(2,1)S(1)}, u32[]{:S(2)}, u32[]{:S(2)}) collective-permute-start(bf16[8,64,1024]{2,1,0:T(8,128)(2,1)} %get-tuple-element.222), channel_id=1, source_target_pairs={{0,2},{2,0},{1,3},{3,1},{4,6},{6,4},{5,7},{7,5},{8,10},{10,8},{9,1... | collective-permute-start | bytes 3145736 | tf_op jit(solution)/shard_map/ppermute | solution.py:864
  218.3 3.8 %collective-permute-start.34 = (bf16[8,64,640]{2,1,0:T(8,128)(2,1)}, bf16[8,64,640]{2,1,0:T(8,128)(2,1)S(1)}, u32[]{:S(2)}, u32[]{:S(2)}) collective-permute-start(bf16[8,64,640]{2,1,0:T(8,128)(2,1)} %get-tuple-element.213), channel_id=1, source_target_pairs={{0,2},{2,0},{1,3},{3,1},{4,6},{6,4},{5,7},{7,5},{8,10},{10,8},{9,1... | collective-permute-start | bytes 1966088 | tf_op jit(solution)/shard_map/ppermute | solution.py:864
  226.3 12.8 %collective-permute-start.40 = (bf16[2,2,32,1024]{3,2,0,1:T(8,128)(2,1)}, bf16[2,2,32,1024]{3,2,0,1:T(8,128)(2,1)}, u32[]{:S(2)}, u32[]{:S(2)}) collective-permute-start(bf16[2,2,32,1024]{3,2,0,1:T(8,128)(2,1)} %select_bitcast_fusion.10), channel_id=1, source_target_pairs={{0,2},{2,0},{1,3},{3,1},{4,6},{6,4},{5,7},{7,5},{8,10},{10,8},{9,1... | collective-permute-start | bytes 786440 | tf_op jit(solution)/shard_map/ppermute | solution.py:864
  229.2 27.0 %all-to-all-start.5 = ((bf16[4,2,64,1024]{3,2,1,0:T(8,128)(2,1)}), bf16[4,2,64,1024]{3,2,1,0:T(8,128)(2,1)S(1)}, u32[]{:S(2)}, u32[]{:S(2)}) async-start(bf16[4,2,64,1024]{3,2,1,0:T(8,128)(2,1)} %token_pieces.1), calls=%async_computation.5 | async-start | bytes 2097152 | tf_op jit(solution)/shard_map/all_to_all | solution.py:1210
  234.2 11.8 %collective-permute-start.39 = (bf16[4,1,32,1408]{3,2,0,1:T(8,128)(2,1)S(1)}, bf16[4,1,32,1408]{3,2,0,1:T(8,128)(2,1)S(1)}, u32[]{:S(2)}, u32[]{:S(2)}) collective-permute-start(bf16[4,1,32,1408]{3,2,0,1:T(8,128)(2,1)S(1)} %select_bitcast_fusion.6), channel_id=1, source_target_pairs={{0,1},{1,0},{2,3},{3,2},{4,5},{5,4},{6,7},{7,6},{8,9},{9,8},{10,11... | collective-permute-start | bytes 1081352 | tf_op jit(solution)/shard_map/ppermute | solution.py:864
  234.7 32.0 %collective-permute-start.36 = (bf16[4,32,1152]{2,1,0:T(8,128)(2,1)}, bf16[4,32,1152]{2,1,0:T(8,128)(2,1)}, u32[]{:S(2)}, u32[]{:S(2)}) collective-permute-start(bf16[4,32,1152]{2,1,0:T(8,128)(2,1)} %get-tuple-element.225), channel_id=1, source_target_pairs={{0,1},{1,0},{2,3},{3,2},{4,5},{5,4},{6,7},{7,6},{8,9},{9,8},{10,11... | collective-permute-start | bytes 884744 | tf_op jit(solution)/shard_map/ppermute | solution.py:864
  236.3 30.5 %collective-permute-start.37 = (bf16[4,32,1152]{2,1,0:T(8,128)(2,1)}, bf16[4,32,1152]{2,1,0:T(8,128)(2,1)}, u32[]{:S(2)}, u32[]{:S(2)}) collective-permute-start(bf16[4,32,1152]{2,1,0:T(8,128)(2,1)} %get-tuple-element.226), channel_id=1, source_target_pairs={{0,16},{16,0},{1,17},{17,1},{2,18},{18,2},{3,19},{19,3},{4,20},{20... | collective-permute-start | bytes 884744 | tf_op jit(solution)/shard_map/ppermute | solution.py:864
  238.5 29.6 %collective-permute-start.38 = (bf16[4,32,1152]{2,1,0:T(8,128)(2,1)}, bf16[4,32,1152]{2,1,0:T(8,128)(2,1)}, u32[]{:S(2)}, u32[]{:S(2)}) collective-permute-start(bf16[4,32,1152]{2,1,0:T(8,128)(2,1)} %get-tuple-element.227), channel_id=1, source_target_pairs={{0,17},{1,16},{16,1},{17,0},{2,19},{3,18},{18,3},{19,2},{4,21},{5,... | collective-permute-start | bytes 884744 | tf_op jit(solution)/shard_map/ppermute | solution.py:864
  257.0 8.8 %collective-permute-start.41 = (bf16[2,1,32,1024]{3,2,0,1:T(8,128)(2,1)}, bf16[2,1,32,1024]{3,2,0,1:T(8,128)(2,1)}, u32[]{:S(2)}, u32[]{:S(2)}) collective-permute-start(bf16[2,1,32,1024]{3,2,0,1:T(8,128)(2,1)} %fusion.6), channel_id=1, source_target_pairs={{0,1},{1,0},{2,3},{3,2},{4,5},{5,4},{6,7},{7,6},{8,9},{9,8},{10,11... | collective-permute-start | bytes 393224 | tf_op jit(solution)/shard_map/ppermute | solution.py:864
  261.6 15.7 %collective-permute-start.43 = (bf16[64,1024]{1,0:T(8,128)(2,1)}, bf16[64,1024]{1,0:T(8,128)(2,1)S(1)}, u32[]{:S(2)}, u32[]{:S(2)}) collective-permute-start(bf16[64,1024]{1,0:T(8,128)(2,1)} %select_bitcast_fusion.13), channel_id=1, source_target_pairs={{0,16},{16,0},{1,17},{17,1},{2,18},{18,2},{3,19},{19,3},{4,20},{20... | collective-permute-start | bytes 393224 | tf_op jit(solution)/shard_map/ppermute | solution.py:864
  261.6 30.0 %all-to-all-start.6 = ((bf16[4,32,1408]{2,1,0:T(8,128)(2,1)}), bf16[4,32,1408]{2,1,0:T(8,128)(2,1)}, u32[]{:S(2)}, u32[]{:S(2)}) async-start(bf16[4,32,1408]{2,1,0:T(8,128)(2,1)} %fusion.2), calls=%async_computation.6 | async-start | bytes 720896 | tf_op jit(solution)/shard_map/all_to_all | solution.py:1220
  268.1 22.7 %collective-permute-start.48 = (bf16[88,1024]{1,0:T(8,128)(2,1)S(1)}, bf16[88,1024]{1,0:T(8,128)(2,1)S(1)}, u32[]{:S(2)}, u32[]{:S(2)}) collective-permute-start(bf16[88,1024]{1,0:T(8,128)(2,1)S(1)} %fusion.5), channel_id=1, source_target_pairs={{0,16},{16,0},{1,17},{17,1},{2,18},{18,2},{3,19},{19,3},{4,20},{20... | collective-permute-start | bytes 540680 | tf_op jit(solution)/shard_map/ppermute | solution.py:864
  269.8 11.6 %collective-permute-start.47 = (bf16[32,1024]{1,0:T(8,128)(2,1)S(1)}, bf16[32,1024]{1,0:T(8,128)(2,1)S(1)}, u32[]{:S(2)}, u32[]{:S(2)}) collective-permute-start(bf16[32,1024]{1,0:T(8,128)(2,1)S(1)} %fusion.11), channel_id=1, source_target_pairs={{0,16},{16,0},{1,17},{17,1},{2,18},{18,2},{3,19},{19,3},{4,20},{20... | collective-permute-start | bytes 196616 | tf_op jit(solution)/shard_map/ppermute | solution.py:864
  273.2 9.0 %collective-permute-start.44 = (bf16[32,1152]{1,0:T(8,128)(2,1)}, bf16[32,1152]{1,0:T(8,128)(2,1)S(1)}, u32[]{:S(2)}, u32[]{:S(2)}) collective-permute-start(bf16[32,1152]{1,0:T(8,128)(2,1)} %get-tuple-element.243), channel_id=1, source_target_pairs={{0,4},{4,0},{8,12},{12,8},{1,5},{5,1},{9,13},{13,9},{2,6},{6,2},{1... | collective-permute-start | bytes 221192 | tf_op jit(solution)/shard_map/ppermute | solution.py:864
  275.4 8.0 %collective-permute-start.45 = (bf16[32,1152]{1,0:T(8,128)(2,1)}, bf16[32,1152]{1,0:T(8,128)(2,1)S(1)}, u32[]{:S(2)}, u32[]{:S(2)}) collective-permute-start(bf16[32,1152]{1,0:T(8,128)(2,1)} %get-tuple-element.244), channel_id=1, source_target_pairs={{0,8},{4,12},{8,0},{12,4},{1,9},{5,13},{9,1},{13,5},{2,10},{6,14},... | collective-permute-start | bytes 221192 | tf_op jit(solution)/shard_map/ppermute | solution.py:864
  277.3 8.2 %collective-permute-start.46 = (bf16[32,1152]{1,0:T(8,128)(2,1)S(1)}, bf16[32,1152]{1,0:T(8,128)(2,1)S(1)}, u32[]{:S(2)}, u32[]{:S(2)}) collective-permute-start(bf16[32,1152]{1,0:T(8,128)(2,1)S(1)} %copy-done.47), channel_id=1, source_target_pairs={{0,12},{4,8},{8,4},{12,0},{1,13},{5,9},{9,5},{13,1},{2,14},{6,10},... | collective-permute-start | bytes 221192 | tf_op jit(solution)/shard_map/ppermute | solution.py:864
  281.4 8.7 %collective-permute-start.42 = (bf16[64,1024]{1,0:T(8,128)(2,1)S(1)}, bf16[64,1024]{1,0:T(8,128)(2,1)S(1)}, u32[]{:S(2)}, u32[]{:S(2)}) collective-permute-start(bf16[64,1024]{1,0:T(8,128)(2,1)S(1)} %select_bitcast_fusion.14), channel_id=1, source_target_pairs={{0,16},{16,0},{1,17},{17,1},{2,18},{18,2},{3,19},{19,3},{4,20},{20... | collective-permute-start | bytes 393224 | tf_op jit(solution)/shard_map/ppermute | solution.py:864
  (41 other events, 130.7 us)

commit v2 on v1

--- a/solution.py
+++ b/solution.py
@@ -16,7 +16,9 @@
 GROUP = 4
 FREE = 24
 COST = 10**6
-VMEM_BYTES = 56 * 1024 * 1024
+MEGA = 1024 * 1024
+VMEM_BYTES = 56 * MEGA
+ROOM = {"branch_gradient": 12, "output_gradient": 12, "token_pieces": 12, "merge_heads": 12, "add_partners": 12, "input_gradient": 12, "spread_heads": 12, "spread_pair": 12, "feed_forward": 32, "feed_forward_grads": 24}
 F32 = jnp.float32
 BF16 = jnp.bfloat16
 NN = (((1,), (0,)), ((), ()))
@@ -826,7 +828,7 @@
 VMEM_SPEC = pl.BlockSpec(memory_space=pltpu.VMEM)
 
 
-def run_kernel(body, name, operands, out_shapes, scratch, micros, scalars=(), stays=(), leaves=()):
+def run_kernel(body, name, operands, out_shapes, scratch, micros, scalars=(), stays=(), leaves=(), scale=1):
     specs = [VMEM_SPEC] * len(operands)
     for i in scalars:
         specs[i] = pl.BlockSpec(memory_space=pltpu.SMEM)
@@ -845,7 +847,7 @@
         in_specs=specs,
         out_specs=outs,
         scratch_shapes=room,
-        compiler_params=pltpu.CompilerParams(vmem_limit_bytes=VMEM_BYTES),
+        compiler_params=pltpu.CompilerParams(vmem_limit_bytes=min(ROOM.get(name, 56) * scale * MEGA, VMEM_BYTES)),
         cost_estimate=pl.CostEstimate(
             flops=micros * COST, bytes_accessed=1 << 10, transcendentals=0
         ),
@@ -1020,6 +1022,8 @@
     cot_got = [swap(cot_own, "q", d) for d in range(1, chips)]
 
     count = length // CHUNK
+    run = partial(run_kernel, scale=max(1, length // 1024))
+
     def tall(n):
         return ((n, length, HEAD), F32)
 
@@ -1034,7 +1038,7 @@
         tall(3),
         tall(2),
     ]
-    heads_here, taps, gains, normed, w_cat, p_pad, kept, slopes, found, shaped = run_kernel(
+    heads_here, taps, gains, normed, w_cat, p_pad, kept, slopes, found, shaped = run(
         mixer_forward,
         "mixer_forward",
         (pos, x_half, x_sib, head_b, head_sib, flags, id_cols, id_rows, gain_vec),
@@ -1059,7 +1063,7 @@
     pair_sib = swap(pair_b, "c", 1)
     w_down = jnp.stack(ordered(core, down_b, down_sib), axis=1).reshape(ff_here, width)
     half = length // 2
-    w_out, normed_two, pair_up, hidden, cot_rows, swiglu_part, res_own, norm_own, *norm_send = run_kernel(
+    w_out, normed_two, pair_up, hidden, cot_rows, swiglu_part, res_own, norm_own, *norm_send = run(
         feed_forward,
         "feed_forward",
         (pos, got_heads, x_half, cot_half, out_q, out_sib, pair_b, pair_sib, w_down, gains),
@@ -1085,7 +1089,7 @@
         (0,),
     )
     norm_got = [swap(v, "q", d + 1) for d, v in enumerate(norm_send)]
-    pair_keep, pair_send, down_keep, down_send, out_part = run_kernel(
+    pair_keep, pair_send, down_keep, down_send, out_part = run(
         feed_forward_grads,
         "feed_forward_grads",
         (pos, normed_two, pair_up, hidden, cot_rows, w_down),
@@ -1101,7 +1105,7 @@
         (0,),
     )
     norm_got, norm_own, pair_send, down_send = together(norm_got, norm_own, pair_send, down_send)
-    grad_resid, grad_branch, grad_heads = run_kernel(
+    grad_resid, grad_branch, grad_heads = run(
         branch_gradient,
         "branch_gradient",
         (pos, norm_own, res_own, cot_own[None], gains, w_out, *norm_got),
@@ -1135,7 +1139,7 @@
 
     blocks_out = ((blocks_all, span, width), BF16)
     weights_out = ((blocks_all, rows_all, 5 * HEAD), BF16)
-    norm_keep, norm_send, w_keep, w_send = run_kernel(
+    norm_keep, norm_send, w_keep, w_send = run(
         partial(mixer_backward, rows_w),
         "mixer_backward",
         (pos, dheads, flags, id_cols, id_rows, gain_vec, taps, swiglu_part)
@@ -1160,7 +1164,7 @@
 
     norm_got = swap(norm_send, "c", 1)
     w_got = swap(w_send, "c", 1)
-    (out_rows,) = run_kernel(
+    (out_rows,) = run(
         output_gradient,
         "output_gradient",
         (pos, got_heads, grad_branch, *branch_got),
@@ -1172,12 +1176,12 @@
     w_got, out_rows = together(w_got, out_rows)
     piece = ((chips, rows_w, 9 * HEAD), BF16)
     if n_batch == 2:
-        value = run_kernel(
+        value = run(
             merge_heads, "merge_heads", (pos, w_keep, w_got), [piece] * 4, [], 1, (0,)
         )
     else:
         merged_all = ((blocks_all, rows_all, 9 * HEAD), BF16)
-        (value,) = run_kernel(
+        (value,) = run(
             merge_heads, "merge_heads", (pos, w_keep, w_got), [merged_all], [], 1, (0,)
         )
         value = value.reshape(blocks_all, n_batch, rows_w, 9 * HEAD)
@@ -1193,7 +1197,7 @@
             for i in range(4)
         ]
     value, norm_got, out_rows, pair_got = together(value, norm_got, out_rows, pair_got)
-    (norm_send,) = run_kernel(
+    (norm_send,) = run(
         token_pieces,
         "token_pieces",
         (norm_keep, norm_got),
@@ -1219,7 +1223,7 @@
     norm_got, pair_rows, out_rows = together(norm_got, pair_rows, out_rows)
     pair_got = lax.all_to_all(pair_rows.astype(BF16), ("q",), 0, 0, tiled=True)
     out_rows = scatter_batch(out_rows, 1)
-    (grad_own,) = run_kernel(
+    (grad_own,) = run(
         input_gradient,
         "input_gradient",
         (pos, grad_resid, x_own, gains, norm_got),
@@ -1230,7 +1234,7 @@
     )
     grad_final = to_rows(grad_own)
     value_got, out_rows, down_grad, out_got = together(value_got, out_rows, down_grad, out_got)
-    head_got = run_kernel(
+    head_got = run(
         add_partners,
         "add_partners",
         (pos, value[0], *value_got),
@@ -1244,7 +1248,7 @@
     down_grad = scatter_bit(down_grad, 0, row, "m", 1)
     out_all = (res_own + jnp.sum(out_got.astype(F32), axis=0)).astype(BF16)
     out_final = to_rows(out_all)
-    gate_grad, up_grad = run_kernel(
+    gate_grad, up_grad = run(
         spread_pair,
         "spread_pair",
         (pair_got,),
@@ -1252,7 +1256,7 @@
         [],
         2,
     )
-    *merged, beta_sum, gain_sums, tap_sums, head_sum = run_kernel(
+    *merged, beta_sum, gain_sums, tap_sums, head_sum = run(
         spread_heads,
         "spread_heads",
         (pos, *head_got),

time: 299 us -> 290 us (0.970)
  Pallas kernels: 85.2 us -> 70.6 us
  starting transfers between devices: 77.7 us -> 81.7 us
  waiting for transfers between devices: 81.6 us -> 85.3 us
  local copies, waits for them, and re-layouts: 14.5 us -> 11.2 us
    pallas_call x13, Pallas kernels: 85.2 us -> 70.6 us  [run_kernel(): pl.pallas_call(body, name=name, out_shape=[jax.ShapeDtypeStruct(*s) for s...]
    ppermute x49, waiting for transfers between devices: 68.2 us -> 72.4 us  [swap(): lax.ppermute(value, axis, [(i, i ^ mask) for i in range(lax.axis_size(axi...]
    unnamed x100 -> x84, local copies, waits for them, and re-layouts: 6.94 us -> 4.66 us
  transfers between devices with their start and end apart: 56 -> 56, of which waited for: 21 -> 23; matrix products, arithmetic and copies ran while one was open for 13% -> 14% of each run, Pallas kernels for 24% -> 20%
where the time goes in v2:
time: 290 us; the launch traced here: 285 us
  waiting for transfers between devices  85.3 us (29%)
  starting transfers between devices  81.7 us (28%)
  Pallas kernels  70.6 us (24%)
  other arithmetic  34.6 us (12%)
  local copies, waits for them, and re-layouts  11.2 us (4%)
    ppermute x49, waiting for transfers between devices, swap(): lax.ppermute(value, axis, [(i, i ^ mask) for i in range(lax.axis_size(axi...  72.4 us
    pallas_call x13, Pallas kernels, run_kernel(): pl.pallas_call(body, name=name, out_shape=[jax.ShapeDtypeStruct(*s) for s...  70.6 us
    ppermute x49, starting transfers between devices, swap(): lax.ppermute(value, axis, [(i, i ^ mask) for i in range(lax.axis_size(axi...  53.9 us
    all_to_all x1, waiting for transfers between devices, on_device(): norm_got = lax.all_to_all(norm_send, ('q',), 0, 0, tiled=True)  9.87 us
  transfers between devices with their start and end apart: 56, of which 23 were waited for; matrix products, arithmetic and copies ran while one was open for 14% of the time, Pallas kernels for 20%

profile of v2, /device:TPU:0, one launch (start us, length us, event | category | flops | bytes accessed | tf_op | source)
XLA Modules:
  0.0 285.1 jit_solution(17056578780992754509)
XLA Ops:
  1.3 2.5 pack_heads.1
  3.8 3.0 %collective-permute-start = (bf16[32,1152]{1,0:T(8,128)(2,1)}, bf16[32,1152]{1,0:T(8,128)(2,1)S(1)}, u32[]{:S(2)}, u32[]{:S(2)}) collective-permute-start(bf16[32,1152]{1,0:T(8,128)(2,1)} %get-tuple-element.138), channel_id=1, source_target_pairs={{0,4},{4,0},{8,12},{12,8},{1,5},{5,1},{9,13},{13,9},{2,6},{6,2},{1... | collective-permute-start | bytes 221192 | tf_op jit(solution)/shard_map/ppermute | solution.py:866
  6.8 1.6 collective-permute-start.1
  9.4 3.1 %collective-permute-start.3 = (bf16[64,1024]{1,0:T(8,128)(2,1)S(1)}, bf16[64,1024]{1,0:T(8,128)(2,1)S(1)}, u32[]{:S(2)}, u32[]{:S(2)}) collective-permute-start(bf16[64,1024]{1,0:T(8,128)(2,1)S(1)} %get-tuple-element.333), channel_id=1, source_target_pairs={{0,16},{16,0},{1,17},{17,1},{2,18},{18,2},{3,19},{19,3},{4,20},{20... | collective-permute-start | bytes 393224 | tf_op jit(solution)/shard_map/ppermute | solution.py:866
  20.3 1.6 collective-permute-start.5
  21.9 1.6 collective-permute-start.6
  24.6 2.9 %collective-permute-start.8 = (bf16[32,1024]{1,0:T(8,128)(2,1)S(1)}, bf16[32,1024]{1,0:T(8,128)(2,1)S(1)}, u32[]{:S(2)}, u32[]{:S(2)}) collective-permute-start(bf16[32,1024]{1,0:T(8,128)(2,1)S(1)} %copy-done.33), channel_id=1, source_target_pairs={{0,16},{16,0},{1,17},{17,1},{2,18},{18,2},{3,19},{19,3},{4,20},{20... | collective-permute-start | bytes 196616 | tf_op jit(solution)/shard_map/ppermute | solution.py:866
  27.6 11.3 %collective-permute-done.6 = bf16[2,64,1024]{2,1,0:T(8,128)(2,1)S(1)} collective-permute-done((bf16[2,64,1024]{2,1,0:T(8,128)(2,1)S(1)}, bf16[2,64,1024]{2,1,0:T(8,128)(2,1)S(1)}, u32[]{:S(2)}, u32[]{:S(2)}) %collective-permute-start.6) | collective-permute-done | bytes 262176 | tf_op jit(solution)/shard_map/ppermute | solution.py:866
  38.9 3.0 %collective-permute-done.7 = bf16[2,64,1024]{2,1,0:T(8,128)(2,1)S(1)} collective-permute-done((bf16[2,64,1024]{2,1,0:T(8,128)(2,1)S(1)}, bf16[2,64,1024]{2,1,0:T(8,128)(2,1)S(1)}, u32[]{:S(2)}, u32[]{:S(2)}) %collective-permute-start.7) | collective-permute-done | bytes 262176 | tf_op jit(solution)/shard_map/ppermute | solution.py:866
  42.1 1.6 collective-permute-start.9
  44.3 2.2 collective-permute-start.12
  47.2 3.5 %all-to-all-start = ((bf16[4,32,1408]{2,1,0:T(8,128)(2,1)}), bf16[4,32,1408]{2,1,0:T(8,128)(2,1)S(1)}, u32[]{:S(2)}, u32[]{:S(2)}) async-start(bf16[4,32,1408]{2,1,0:T(8,128)(2,1)} %reshape.392), calls=%async_computation | async-start | bytes 720896 | tf_op jit(solution)/shard_map/all_to_all | solution.py:1010
  50.7 7.0 %collective-permute-done.13 = bf16[2,32,1024]{2,1,0:T(8,128)(2,1)S(1)} collective-permute-done((bf16[2,32,1024]{2,1,0:T(8,128)(2,1)S(1)}, bf16[2,32,1024]{2,1,0:T(8,128)(2,1)S(1)}, u32[]{:S(2)}, u32[]{:S(2)}) %collective-permute-start.13) | collective-permute-done | bytes 131104 | tf_op jit(solution)/shard_map/ppermute | solution.py:866
  58.8 3.0 %collective-permute-done.11 = bf16[64,1024]{1,0:T(8,128)(2,1)} collective-permute-done((bf16[64,1024]{1,0:T(8,128)(2,1)}, bf16[64,1024]{1,0:T(8,128)(2,1)}, u32[]{:S(2)}, u32[]{:S(2)}) %collective-permute-start.11) | collective-permute-done | bytes 131104 | tf_op jit(solution)/shard_map/ppermute | solution.py:866
  61.8 2.0 all-to-all-done
  64.9 4.4 %all-to-all-start.2 = ((bf16[4,2,64,1024]{3,2,1,0:T(8,128)(2,1)}), bf16[4,2,64,1024]{3,2,1,0:T(8,128)(2,1)}, u32[]{:S(2)}, u32[]{:S(2)}) async-start(bf16[4,2,64,1024]{3,2,1,0:T(8,128)(2,1)} %broadcast_in_dim.28), calls=%async_computation.2 | async-start | bytes 2097152 | tf_op jit(solution)/shard_map/all_to_all | solution.py:1019
  70.7 1.6 collective-permute-start.16
  72.7 1.6 fusion.15
  74.3 2.0 collective-permute-start.17
  76.3 1.5 collective-permute-start.18
  78.9 21.8 %mixer_forward.1 = (bf16[4,2,512,128]{3,2,1,0:T(8,128)(2,1)}, f32[16,128]{1,0:T(8,128)}, f32[8,1024]{1,0:T(8,128)}, bf16[1024,1024]{1,0:T(8,128)(2,1)}, bf16[102...) custom-call(s32[4]{0:T(128)} %pad_add_fusion.pos_ref, ...), custom_call_target="tpu_custom_call" | custom-call | flops 25000000 | bytes 1024 | tf_op jit(solution)/shard_map/mixer_forward/pallas_call | solution.py:843
  100.7 1.6 collective-permute-done.19
  103.1 1.5 collective-permute-start.21
  104.6 4.0 %all-to-all-start.1 = ((bf16[8,512,128]{2,1,0:T(8,128)(2,1)}), bf16[8,512,128]{2,1,0:T(8,128)(2,1)S(1)}, u32[]{:S(2)}, u32[]{:S(2)}) async-start(bf16[8,512,128]{2,1,0:T(8,128)(2,1)} %bitcast.42), calls=%async_computation.1 | async-start | bytes 2097152 | tf_op jit(solution)/shard_map/all_to_all | solution.py:1054
  108.6 10.8 %collective-permute-done.21 = bf16[8,32,1408]{2,1,0:T(8,128)(2,1)S(1)} collective-permute-done((bf16[8,32,1408]{2,1,0:T(8,128)(2,1)S(1)}, bf16[8,32,1408]{2,1,0:T(8,128)(2,1)S(1)}, u32[]{:S(2)}, u32[]{:S(2)}) %collective-permute-start.21) | collective-permute-done | bytes 720928 | tf_op jit(solution)/shard_map/ppermute | solution.py:866
  121.8 2.1 pad_maximum_fusion.4.cot_ref
  124.0 2.2 collective-permute-done.23
  129.7 9.4 %feed_forward.1 = (bf16[1024,1024]{1,0:T(8,128)(2,1)S(1)}, bf16[512,1024]{1,0:T(8,128)(2,1)S(1)}, bf16[512,1408]{1,0:T(8,128)(2,1)S(1)}, bf16[512,704]{1,0:T(8,1...) custom-call(s32[4]{0:T(128)S(1)} %copy-done.17, ...), custom_call_target="tpu_custom_call" | custom-call | flops 12000000 | bytes 1024 | tf_op jit(solution)/shard_map/feed_forward/pallas_call | solution.py:843
  139.0 1.4 collective-permute-start.24
  140.4 1.5 collective-permute-start.25
  142.6 5.1 %feed_forward_grads.1 = (bf16[8,64,1408]{2,1,0:T(8,128)(2,1)S(1)}, bf16[8,64,1408]{2,1,0:T(8,128)(2,1)}, bf16[2,176,1024]{2,1,0:T(8,128)(2,1)S(1)}, bf16[2,176,1...) custom-call(s32[4]{0:T(128)S(1)} %copy-done.17, bf16[512,1024]{1,0:T(8,128)(2,1)S(1)} %get-tuple-element.175.normed_ref, ...), custom_call_target="tpu_custom_call" | custom-call | flops 6000000 | bytes 1024 | tf_op jit(solution)/shard_map/feed_forward_grads/pallas_call | solution.py:843
  147.7 1.9 collective-permute-done.25.rest_1_
  149.6 4.7 %collective-permute-done.26.rest_2_ = bf16[2,64,1024]{2,1,0:T(8,128)(2,1)S(1)} collective-permute-done((bf16[2,64,1024]{2,1,0:T(8,128)(2,1)S(1)}, bf16[2,64,1024]{2,1,0:T(8,128)(2,1)S(1)}, u32[]{:S(2)}, u32[]{:S(2)}) %collective-permute-start.26) | collective-permute-done | bytes 262176 | tf_op jit(solution)/shard_map/ppermute | solution.py:866
  154.8 2.3 branch_gradient.1
  157.9 4.2 %all-to-all-start.3 = ((bf16[8,2,64,128]{3,2,1,0:T(8,128)(2,1)}), bf16[8,2,64,128]{3,2,1,0:T(8,128)(2,1)}, u32[]{:S(2)}, u32[]{:S(2)}) async-start(bf16[8,2,64,128]{3,2,1,0:T(8,128)(2,1)} %get-tuple-element.186), calls=%async_computation.3 | async-start | bytes 524288 | tf_op jit(solution)/shard_map/all_to_all | solution.py:1120
  162.1 2.2 add_convert_fusion.1
  164.4 2.8 add_convert_fusion
  168.2 4.6 %all-to-all-start.4 = ((bf16[4,2,64,1024]{3,2,1,0:T(8,128)(2,1)}), bf16[4,2,64,1024]{3,2,1,0:T(8,128)(2,1)}, u32[]{:S(2)}, u32[]{:S(2)}) async-start(bf16[4,2,64,1024]{3,2,1,0:T(8,128)(2,1)} %get-tuple-element.210), calls=%async_computation.4 | async-start | bytes 2097152 | tf_op jit(solution)/shard_map/all_to_all | solution.py:1128
  173.9 2.2 collective-permute-start.29
  176.7 2.0 collective-permute-start.31
  178.7 1.5 collective-permute-start.32
  180.2 21.7 %mixer_backward.1 = (bf16[8,64,1024]{2,1,0:T(8,128)(2,1)}, bf16[8,64,1024]{2,1,0:T(8,128)(2,1)}, bf16[8,64,640]{2,1,0:T(8,128)(2,1)}, bf16[8,64,640]{2,1,0:T(8,128)(2,1)}) custom-call(s32[4]{0:T(128)} %pad_add_fusion.pos_ref, bf16[8,2,64,128]{3,2,1,0:T(8,128)(2,1)} %all-to-all-done.3.dh_ref, f32[1032,8]{1,0:T(8,128)} %pad_convert_fusion.flag_ref, ...), custom_call_target="tpu_custom_call" | custom-call | flops 25000000 | bytes 1024 | tf_op jit(solution)/shard_map/mixer_backward/pallas_call | solution.py:843
  203.0 5.8 %collective-permute-done.32.refs_2_ = bf16[2,64,1024]{2,1,0:T(8,128)(2,1)S(1)} collective-permute-done((bf16[2,64,1024]{2,1,0:T(8,128)(2,1)S(1)}, bf16[2,64,1024]{2,1,0:T(8,128)(2,1)S(1)}, u32[]{:S(2)}, u32[]{:S(2)}) %collective-permute-start.32) | collective-permute-done | bytes 262176 | tf_op jit(solution)/shard_map/ppermute | solution.py:866
  208.8 5.3 %collective-permute-done.33.refs_3_ = bf16[2,64,1024]{2,1,0:T(8,128)(2,1)S(1)} collective-permute-done((bf16[2,64,1024]{2,1,0:T(8,128)(2,1)S(1)}, bf16[2,64,1024]{2,1,0:T(8,128)(2,1)S(1)}, u32[]{:S(2)}, u32[]{:S(2)}) %collective-permute-start.33) | collective-permute-done | bytes 262176 | tf_op jit(solution)/shard_map/ppermute | solution.py:866
  215.7 2.2 collective-permute-done.34.got_ref
  217.9 1.5 merge_heads.1
  221.6 3.6 %all-to-all-start.5 = ((bf16[4,2,64,1024]{3,2,1,0:T(8,128)(2,1)}), bf16[4,2,64,1024]{3,2,1,0:T(8,128)(2,1)S(1)}, u32[]{:S(2)}, u32[]{:S(2)}) async-start(bf16[4,2,64,1024]{3,2,1,0:T(8,128)(2,1)} %token_pieces.1), calls=%async_computation.5 | async-start | bytes 2097152 | tf_op jit(solution)/shard_map/all_to_all | solution.py:1214
  225.3 1.3 fusion.1
  226.7 1.6 collective-permute-start.39
  228.8 2.2 collective-permute-start.37
  231.0 1.7 collective-permute-start.38
  232.7 1.8 convert_add_fusion.3
  234.6 3.5 %collective-permute-done.39 = bf16[4,1,32,1408]{3,2,0,1:T(8,128)(2,1)S(1)} collective-permute-done((bf16[4,1,32,1408]{3,2,0,1:T(8,128)(2,1)S(1)}, bf16[4,1,32,1408]{3,2,0,1:T(8,128)(2,1)S(1)}, u32[]{:S(2)}, u32[]{:S(2)}) %collective-permute-start.39) | collective-permute-done | bytes 360480 | tf_op jit(solution)/shard_map/ppermute | solution.py:866
  238.9 9.9 %all-to-all-done.5.got_ref = bf16[4,2,64,1024]{3,2,1,0:T(8,128)(2,1)S(1)} async-done(((bf16[4,2,64,1024]{3,2,1,0:T(8,128)(2,1)}), bf16[4,2,64,1024]{3,2,1,0:T(8,128)(2,1)S(1)}, u32[]{:S(2)}, u32[]{:S(2)}) %all-to-all-start.5) | async-done | bytes 1048608 | tf_op jit(solution)/shard_map/all_to_all | solution.py:1214
  248.8 1.7 fusion.6
  252.0 3.6 %all-to-all-start.6 = ((bf16[4,32,1408]{2,1,0:T(8,128)(2,1)}), bf16[4,32,1408]{2,1,0:T(8,128)(2,1)S(1)}, u32[]{:S(2)}, u32[]{:S(2)}) async-start(bf16[4,32,1408]{2,1,0:T(8,128)(2,1)} %fusion.2), calls=%async_computation.6 | async-start | bytes 720896 | tf_op jit(solution)/shard_map/all_to_all | solution.py:1224
  257.8 4.8 %collective-permute-done.38.refs_3_ = bf16[4,32,1152]{2,1,0:T(8,128)(2,1)S(1)} collective-permute-done((bf16[4,32,1152]{2,1,0:T(8,128)(2,1)}, bf16[4,32,1152]{2,1,0:T(8,128)(2,1)S(1)}, u32[]{:S(2)}, u32[]{:S(2)}) %collective-permute-start.38) | collective-permute-done | bytes 294944 | tf_op jit(solution)/shard_map/ppermute | solution.py:866
  262.8 3.0 %collective-permute-start.47 = (bf16[32,1024]{1,0:T(8,128)(2,1)S(1)}, bf16[32,1024]{1,0:T(8,128)(2,1)S(1)}, u32[]{:S(2)}, u32[]{:S(2)}) collective-permute-start(bf16[32,1024]{1,0:T(8,128)(2,1)S(1)} %fusion.11), channel_id=1, source_target_pairs={{0,16},{16,0},{1,17},{17,1},{2,18},{18,2},{3,19},{19,3},{4,20},{20... | collective-permute-start | bytes 196616 | tf_op jit(solution)/shard_map/ppermute | solution.py:866
  266.5 2.0 collective-permute-start.44
  268.5 1.7 collective-permute-start.45
  270.2 1.5 convert_reduce_fusion
  274.1 2.5 collective-permute-start.42
  278.5 1.4 spread_heads.1
  280.5 1.9 collective-permute-done.42
  (225 shorter events, 46.5 us)
Async XLA Ops:
  0.6 16.5 %copy-start.38 = (s32[2,1,1024]{2,1,0:T(1,128)S(1)}, s32[2,1,1024]{2,1,0:T(1,128)}, u32[]{:S(2)}) copy-start(s32[2,1,1024]{2,1,0:T(1,128)} %param.18) | copy-start | bytes 24580
  0.7 17.1 %copy-start.36 = (bf16[32,2816]{1,0:T(8,128)(2,1)S(1)}, bf16[32,2816]{1,0:T(8,128)(2,1)}, u32[]{:S(2)}) copy-start(bf16[32,2816]{1,0:T(8,128)(2,1)} %param.25) | copy-start | bytes 540676
  3.8 16.5 %collective-permute-start = (bf16[32,1152]{1,0:T(8,128)(2,1)}, bf16[32,1152]{1,0:T(8,128)(2,1)S(1)}, u32[]{:S(2)}, u32[]{:S(2)}) collective-permute-start(bf16[32,1152]{1,0:T(8,128)(2,1)} %get-tuple-element.138), channel_id=1, source_target_pairs={{0,4},{4,0},{8,12},{12,8},{1,5},{5,1},{9,13},{13,9},{2,6},{6,2},{1... | collective-permute-start | bytes 221192 | tf_op jit(solution)/shard_map/ppermute | solution.py:866
  6.8 13.5 %collective-permute-start.1 = (bf16[32,1152]{1,0:T(8,128)(2,1)}, bf16[32,1152]{1,0:T(8,128)(2,1)S(1)}, u32[]{:S(2)}, u32[]{:S(2)}) collective-permute-start(bf16[32,1152]{1,0:T(8,128)(2,1)} %get-tuple-element.139), channel_id=1, source_target_pairs={{0,8},{4,12},{8,0},{12,4},{1,9},{5,13},{9,1},{13,5},{2,10},{6,14},... | collective-permute-start | bytes 221192 | tf_op jit(solution)/shard_map/ppermute | solution.py:866
  8.4 11.9 %collective-permute-start.2 = (bf16[32,1152]{1,0:T(8,128)(2,1)}, bf16[32,1152]{1,0:T(8,128)(2,1)S(1)}, u32[]{:S(2)}, u32[]{:S(2)}) collective-permute-start(bf16[32,1152]{1,0:T(8,128)(2,1)} %get-tuple-element.140), channel_id=1, source_target_pairs={{0,12},{4,8},{8,4},{12,0},{1,13},{5,9},{9,5},{13,1},{2,14},{6,10},... | collective-permute-start | bytes 221192 | tf_op jit(solution)/shard_map/ppermute | solution.py:866
  9.4 10.9 %collective-permute-start.3 = (bf16[64,1024]{1,0:T(8,128)(2,1)S(1)}, bf16[64,1024]{1,0:T(8,128)(2,1)S(1)}, u32[]{:S(2)}, u32[]{:S(2)}) collective-permute-start(bf16[64,1024]{1,0:T(8,128)(2,1)S(1)} %get-tuple-element.333), channel_id=1, source_target_pairs={{0,16},{16,0},{1,17},{17,1},{2,18},{18,2},{3,19},{19,3},{4,20},{20... | collective-permute-start | bytes 393224 | tf_op jit(solution)/shard_map/ppermute | solution.py:866
  20.3 21.5 %copy-start.10 = (bf16[2,64,1024]{2,1,0:T(8,128)(2,1)}, bf16[2,64,1024]{2,1,0:T(8,128)(2,1)S(1)}, u32[]{:S(2)}) copy-start(bf16[2,64,1024]{2,1,0:T(8,128)(2,1)S(1)} %get-tuple-element.331.x_ref) | copy-start | bytes 786436
  20.3 7.2 %collective-permute-start.5 = (bf16[2,64,1024]{2,1,0:T(8,128)(2,1)S(1)}, bf16[2,64,1024]{2,1,0:T(8,128)(2,1)S(1)}, u32[]{:S(2)}, u32[]{:S(2)}) collective-permute-start(bf16[2,64,1024]{2,1,0:T(8,128)(2,1)S(1)} %get-tuple-element.331.x_ref), channel_id=1, source_target_pairs={{0,4},{4,0},{8,12},{12,8},{1,5},{5,1},{9,13},{13,9},{2,6},{6,2},{1... | collective-permute-start | bytes 786440 | tf_op jit(solution)/shard_map/ppermute | solution.py:866
  21.9 17.0 %collective-permute-start.6 = (bf16[2,64,1024]{2,1,0:T(8,128)(2,1)S(1)}, bf16[2,64,1024]{2,1,0:T(8,128)(2,1)S(1)}, u32[]{:S(2)}, u32[]{:S(2)}) collective-permute-start(bf16[2,64,1024]{2,1,0:T(8,128)(2,1)S(1)} %get-tuple-element.331.x_ref), channel_id=1, source_target_pairs={{0,8},{4,12},{8,0},{12,4},{1,9},{5,13},{9,1},{13,5},{2,10},{6,14},... | collective-permute-start | bytes 786440 | tf_op jit(solution)/shard_map/ppermute | solution.py:866
  23.5 18.4 %collective-permute-start.7 = (bf16[2,64,1024]{2,1,0:T(8,128)(2,1)S(1)}, bf16[2,64,1024]{2,1,0:T(8,128)(2,1)S(1)}, u32[]{:S(2)}, u32[]{:S(2)}) collective-permute-start(bf16[2,64,1024]{2,1,0:T(8,128)(2,1)S(1)} %get-tuple-element.331.x_ref), channel_id=1, source_target_pairs={{0,12},{4,8},{8,4},{12,0},{1,13},{5,9},{9,5},{13,1},{2,14},{6,10},... | collective-permute-start | bytes 786440 | tf_op jit(solution)/shard_map/ppermute | solution.py:866
  24.0 18.1 %collective-permute-start.4 = (bf16[4,32,1152]{2,1,0:T(8,128)(2,1)S(1)}, bf16[4,32,1152]{2,1,0:T(8,128)(2,1)S(1)}, u32[]{:S(2)}, u32[]{:S(2)}) collective-permute-start(bf16[4,32,1152]{2,1,0:T(8,128)(2,1)S(1)} %get-tuple-element.323), channel_id=1, source_target_pairs={{0,16},{16,0},{1,17},{17,1},{2,18},{18,2},{3,19},{19,3},{4,20},{20... | collective-permute-start | bytes 884744 | tf_op jit(solution)/shard_map/ppermute | solution.py:866
  24.6 17.5 %collective-permute-start.8 = (bf16[32,1024]{1,0:T(8,128)(2,1)S(1)}, bf16[32,1024]{1,0:T(8,128)(2,1)S(1)}, u32[]{:S(2)}, u32[]{:S(2)}) collective-permute-start(bf16[32,1024]{1,0:T(8,128)(2,1)S(1)} %copy-done.33), channel_id=1, source_target_pairs={{0,16},{16,0},{1,17},{17,1},{2,18},{18,2},{3,19},{19,3},{4,20},{20... | collective-permute-start | bytes 196616 | tf_op jit(solution)/shard_map/ppermute | solution.py:866
  42.0 16.5 %copy-start = (bf16[4,2,64,1024]{3,2,1,0:T(8,128)(2,1)}, bf16[4,2,64,1024]{3,2,1,0:T(8,128)(2,1)S(1)}, u32[]{:S(2)}) copy-start(bf16[4,2,64,1024]{3,2,1,0:T(8,128)(2,1)S(1)} %pad_maximum_fusion.3.xown_ref) | copy-start | bytes 3145732
  42.1 16.4 %collective-permute-start.9 = (bf16[8,32,1152]{2,1,0:T(8,128)(2,1)S(1)}, bf16[8,32,1152]{2,1,0:T(8,128)(2,1)S(1)}, u32[]{:S(2)}, u32[]{:S(2)}) collective-permute-start(bf16[8,32,1152]{2,1,0:T(8,128)(2,1)S(1)} %bitcast.207), channel_id=1, source_target_pairs={{0,1},{1,0},{2,3},{3,2},{4,5},{5,4},{6,7},{7,6},{8,9},{9,8},{10,11... | collective-permute-start | bytes 1769480 | tf_op jit(solution)/shard_map/ppermute | solution.py:866
  43.7 14.0 %collective-permute-start.13 = (bf16[2,32,1024]{2,1,0:T(8,128)(2,1)S(1)}, bf16[2,32,1024]{2,1,0:T(8,128)(2,1)S(1)}, u32[]{:S(2)}, u32[]{:S(2)}) collective-permute-start(bf16[2,32,1024]{2,1,0:T(8,128)(2,1)S(1)} %pad_maximum_fusion.14), channel_id=1, source_target_pairs={{0,1},{1,0},{2,3},{3,2},{4,5},{5,4},{6,7},{7,6},{8,9},{9,8},{10,11... | collective-permute-start | bytes 393224 | tf_op jit(solution)/shard_map/ppermute | solution.py:866
  44.3 19.5 %collective-permute-start.10 = (bf16[4,2,64,1024]{3,2,1,0:T(8,128)(2,1)S(1)}, bf16[4,2,64,1024]{3,2,1,0:T(8,128)(2,1)}, u32[]{:S(2)}, u32[]{:S(2)}) collective-permute-start(bf16[4,2,64,1024]{3,2,1,0:T(8,128)(2,1)S(1)} %pad_maximum_fusion.3.xown_ref), channel_id=1, source_target_pairs={{0,2},{2,0},{1,3},{3,1},{4,6},{6,4},{5,7},{7,5},{8,10},{10,8},{9,1... | collective-permute-start | bytes 3145736 | tf_op jit(solution)/shard_map/ppermute | solution.py:866
  44.3 17.6 %collective-permute-start.12 = (bf16[88,1024]{1,0:T(8,128)(2,1)}, bf16[88,1024]{1,0:T(8,128)(2,1)}, u32[]{:S(2)}, u32[]{:S(2)}) collective-permute-start(bf16[88,1024]{1,0:T(8,128)(2,1)} %param.27), channel_id=1, source_target_pairs={{0,16},{16,0},{1,17},{17,1},{2,18},{18,2},{3,19},{19,3},{4,20},{20... | collective-permute-start | bytes 540680 | tf_op jit(solution)/shard_map/ppermute | solution.py:866
  46.5 15.4 %collective-permute-start.11 = (bf16[64,1024]{1,0:T(8,128)(2,1)}, bf16[64,1024]{1,0:T(8,128)(2,1)}, u32[]{:S(2)}, u32[]{:S(2)}) collective-permute-start(bf16[64,1024]{1,0:T(8,128)(2,1)} %get-tuple-element.148), channel_id=1, source_target_pairs={{0,16},{16,0},{1,17},{17,1},{2,18},{18,2},{3,19},{19,3},{4,20},{20... | collective-permute-start | bytes 393224 | tf_op jit(solution)/shard_map/ppermute | solution.py:866
  47.2 16.6 %all-to-all-start = ((bf16[4,32,1408]{2,1,0:T(8,128)(2,1)}), bf16[4,32,1408]{2,1,0:T(8,128)(2,1)S(1)}, u32[]{:S(2)}, u32[]{:S(2)}) async-start(bf16[4,32,1408]{2,1,0:T(8,128)(2,1)} %reshape.392), calls=%async_computation | async-start | bytes 720896 | tf_op jit(solution)/shard_map/all_to_all | solution.py:1010
  64.9 37.4 %all-to-all-start.2 = ((bf16[4,2,64,1024]{3,2,1,0:T(8,128)(2,1)}), bf16[4,2,64,1024]{3,2,1,0:T(8,128)(2,1)}, u32[]{:S(2)}, u32[]{:S(2)}) async-start(bf16[4,2,64,1024]{3,2,1,0:T(8,128)(2,1)} %broadcast_in_dim.28), calls=%async_computation.2 | async-start | bytes 2097152 | tf_op jit(solution)/shard_map/all_to_all | solution.py:1019
  69.6 8.3 %collective-permute-start.14 = (bf16[8,64,640]{2,1,0:T(8,128)(2,1)S(1)}, bf16[8,64,640]{2,1,0:T(8,128)(2,1)S(1)}, u32[]{:S(2)}, u32[]{:S(2)}) collective-permute-start(bf16[8,64,640]{2,1,0:T(8,128)(2,1)S(1)} %pad_maximum_fusion.7), channel_id=1, source_target_pairs={{0,2},{2,0},{1,3},{3,1},{4,6},{6,4},{5,7},{7,5},{8,10},{10,8},{9,1... | collective-permute-start | bytes 1966088 | tf_op jit(solution)/shard_map/ppermute | solution.py:866
  70.7 31.6 %collective-permute-start.16 = (bf16[2,88,1024]{2,1,0:T(8,128)(2,1)S(1)}, bf16[2,88,1024]{2,1,0:T(8,128)(2,1)S(1)}, u32[]{:S(2)}, u32[]{:S(2)}) collective-permute-start(bf16[2,88,1024]{2,1,0:T(8,128)(2,1)S(1)} %pad_maximum_fusion.9), channel_id=1, source_target_pairs={{0,1},{1,0},{2,3},{3,2},{4,5},{5,4},{6,7},{7,6},{8,9},{9,8},{10,11... | collective-permute-start | bytes 1081352 | tf_op jit(solution)/shard_map/ppermute | solution.py:866
  72.3 30.0 %collective-permute-start.15 = (bf16[4,32,1408]{2,1,0:T(8,128)(2,1)S(1)}, bf16[4,32,1408]{2,1,0:T(8,128)(2,1)S(1)}, u32[]{:S(2)}, u32[]{:S(2)}) collective-permute-start(bf16[4,32,1408]{2,1,0:T(8,128)(2,1)S(1)} %all-to-all-done), channel_id=1, source_target_pairs={{0,16},{16,0},{1,17},{17,1},{2,18},{18,2},{3,19},{19,3},{4,20},{20... | collective-permute-start | bytes 1081352 | tf_op jit(solution)/shard_map/ppermute | solution.py:866
  74.3 47.4 %copy-start.3 = (bf16[1,2,64,1024]{3,2,1,0:T(8,128)(2,1)}, bf16[1,2,64,1024]{3,2,1,0:T(8,128)(2,1)S(1)}, u32[]{:S(2)}) copy-start(bf16[1,2,64,1024]{3,2,1,0:T(8,128)(2,1)S(1)} %get-tuple-element.324.cot_ref) | copy-start | bytes 786436
  74.3 26.4 %collective-permute-start.17 = (bf16[2,64,1024]{2,1,0:T(8,128)(2,1)}, bf16[2,64,1024]{2,1,0:T(8,128)(2,1)}, u32[]{:S(2)}, u32[]{:S(2)}) collective-permute-start(bf16[2,64,1024]{2,1,0:T(8,128)(2,1)} %get-tuple-element.325), channel_id=1, source_target_pairs={{0,4},{4,0},{8,12},{12,8},{1,5},{5,1},{9,13},{13,9},{2,6},{6,2},{1... | collective-permute-start | bytes 786440 | tf_op jit(solution)/shard_map/ppermute | solution.py:866
  76.3 24.4 %collective-permute-start.18 = (bf16[2,64,1024]{2,1,0:T(8,128)(2,1)}, bf16[2,64,1024]{2,1,0:T(8,128)(2,1)}, u32[]{:S(2)}, u32[]{:S(2)}) collective-permute-start(bf16[2,64,1024]{2,1,0:T(8,128)(2,1)} %get-tuple-element.325), channel_id=1, source_target_pairs={{0,8},{4,12},{8,0},{12,4},{1,9},{5,13},{9,1},{13,5},{2,10},{6,14},... | collective-permute-start | bytes 786440 | tf_op jit(solution)/shard_map/ppermute | solution.py:866
  77.8 24.5 %collective-permute-start.19 = (bf16[2,64,1024]{2,1,0:T(8,128)(2,1)}, bf16[2,64,1024]{2,1,0:T(8,128)(2,1)S(1)}, u32[]{:S(2)}, u32[]{:S(2)}) collective-permute-start(bf16[2,64,1024]{2,1,0:T(8,128)(2,1)} %get-tuple-element.325), channel_id=1, source_target_pairs={{0,12},{4,8},{8,4},{12,0},{1,13},{5,9},{9,5},{13,1},{2,14},{6,10},... | collective-permute-start | bytes 786440 | tf_op jit(solution)/shard_map/ppermute | solution.py:866
  103.1 16.3 %collective-permute-start.21 = (bf16[8,32,1408]{2,1,0:T(8,128)(2,1)S(1)}, bf16[8,32,1408]{2,1,0:T(8,128)(2,1)S(1)}, u32[]{:S(2)}, u32[]{:S(2)}) collective-permute-start(bf16[8,32,1408]{2,1,0:T(8,128)(2,1)S(1)} %bitcast.206), channel_id=1, source_target_pairs={{0,1},{1,0},{2,3},{3,2},{4,5},{5,4},{6,7},{7,6},{8,9},{9,8},{10,11... | collective-permute-start | bytes 2162696 | tf_op jit(solution)/shard_map/ppermute | solution.py:866
  104.6 22.0 %all-to-all-start.1 = ((bf16[8,512,128]{2,1,0:T(8,128)(2,1)}), bf16[8,512,128]{2,1,0:T(8,128)(2,1)S(1)}, u32[]{:S(2)}, u32[]{:S(2)}) async-start(bf16[8,512,128]{2,1,0:T(8,128)(2,1)} %bitcast.42), calls=%async_computation.1 | async-start | bytes 2097152 | tf_op jit(solution)/shard_map/all_to_all | solution.py:1054
  120.9 6.1 %collective-permute-start.22 = (bf16[2,4,64,1408]{3,2,1,0:T(8,128)(2,1)}, bf16[2,4,64,1408]{3,2,1,0:T(8,128)(2,1)}, u32[]{:S(2)}, u32[]{:S(2)}) collective-permute-start(bf16[2,4,64,1408]{3,2,1,0:T(8,128)(2,1)} %bitcast.57.pown_ref), channel_id=1, source_target_pairs={{0,2},{2,0},{1,3},{3,1},{4,6},{6,4},{5,7},{7,5},{8,10},{10,8},{9,1... | collective-permute-start | bytes 4325384 | tf_op jit(solution)/shard_map/ppermute | solution.py:866
  121.0 5.1 %collective-permute-start.23 = (bf16[2,176,1024]{2,1,0:T(8,128)(2,1)S(1)}, bf16[2,176,1024]{2,1,0:T(8,128)(2,1)S(1)}, u32[]{:S(2)}, u32[]{:S(2)}) collective-permute-start(bf16[2,176,1024]{2,1,0:T(8,128)(2,1)S(1)} %bitcast.205), channel_id=1, source_target_pairs={{0,2},{2,0},{1,3},{3,1},{4,6},{6,4},{5,7},{7,5},{8,10},{10,8},{9,1... | collective-permute-start | bytes 2162696 | tf_op jit(solution)/shard_map/ppermute | solution.py:866
  121.6 5.4 %collective-permute-start.20 = (bf16[4,2,64,1024]{3,2,1,0:T(8,128)(2,1)}, bf16[4,2,64,1024]{3,2,1,0:T(8,128)(2,1)}, u32[]{:S(2)}, u32[]{:S(2)}) collective-permute-start(bf16[4,2,64,1024]{3,2,1,0:T(8,128)(2,1)} %all-to-all-done.2.oown_ref), channel_id=1, source_target_pairs={{0,2},{2,0},{1,3},{3,1},{4,6},{6,4},{5,7},{7,5},{8,10},{10,8},{9,1... | collective-permute-start | bytes 3145736 | tf_op jit(solution)/shard_map/ppermute | solution.py:866
  139.0 8.6 %collective-permute-start.24 = (bf16[2,64,1024]{2,1,0:T(8,128)(2,1)S(1)}, bf16[2,64,1024]{2,1,0:T(8,128)(2,1)S(1)}, u32[]{:S(2)}, u32[]{:S(2)}) collective-permute-start(bf16[2,64,1024]{2,1,0:T(8,128)(2,1)S(1)} %get-tuple-element.171), channel_id=1, source_target_pairs={{0,4},{4,0},{8,12},{12,8},{1,5},{5,1},{9,13},{13,9},{2,6},{6,2},{1... | collective-permute-start | bytes 786440 | tf_op jit(solution)/shard_map/ppermute | solution.py:866
  140.4 9.2 %collective-permute-start.25 = (bf16[2,64,1024]{2,1,0:T(8,128)(2,1)S(1)}, bf16[2,64,1024]{2,1,0:T(8,128)(2,1)S(1)}, u32[]{:S(2)}, u32[]{:S(2)}) collective-permute-start(bf16[2,64,1024]{2,1,0:T(8,128)(2,1)S(1)} %get-tuple-element.172), channel_id=1, source_target_pairs={{0,8},{4,12},{8,0},{12,4},{1,9},{5,13},{9,1},{13,5},{2,10},{6,14},... | collective-permute-start | bytes 786440 | tf_op jit(solution)/shard_map/ppermute | solution.py:866
  141.9 12.4 %collective-permute-start.26 = (bf16[2,64,1024]{2,1,0:T(8,128)(2,1)S(1)}, bf16[2,64,1024]{2,1,0:T(8,128)(2,1)S(1)}, u32[]{:S(2)}, u32[]{:S(2)}) collective-permute-start(bf16[2,64,1024]{2,1,0:T(8,128)(2,1)S(1)} %get-tuple-element.173), channel_id=1, source_target_pairs={{0,12},{4,8},{8,4},{12,0},{1,13},{5,9},{9,5},{13,1},{2,14},{6,10},... | collective-permute-start | bytes 786440 | tf_op jit(solution)/shard_map/ppermute | solution.py:866
  154.3 7.8 %collective-permute-start.27 = (bf16[8,64,1408]{2,1,0:T(8,128)(2,1)}, bf16[8,64,1408]{2,1,0:T(8,128)(2,1)}, u32[]{:S(2)}, u32[]{:S(2)}) collective-permute-start(bf16[8,64,1408]{2,1,0:T(8,128)(2,1)} %get-tuple-element.189), channel_id=1, source_target_pairs={{0,2},{2,0},{1,3},{3,1},{4,6},{6,4},{5,7},{7,5},{8,10},{10,8},{9,1... | collective-permute-start | bytes 4325384 | tf_op jit(solution)/shard_map/ppermute | solution.py:866
  154.3 7.8 %collective-permute-start.28 = (bf16[2,176,1024]{2,1,0:T(8,128)(2,1)}, bf16[2,176,1024]{2,1,0:T(8,128)(2,1)}, u32[]{:S(2)}, u32[]{:S(2)}) collective-permute-start(bf16[2,176,1024]{2,1,0:T(8,128)(2,1)} %get-tuple-element.190), channel_id=1, source_target_pairs={{0,2},{2,0},{1,3},{3,1},{4,6},{6,4},{5,7},{7,5},{8,10},{10,8},{9,1... | collective-permute-start | bytes 2162696 | tf_op jit(solution)/shard_map/ppermute | solution.py:866
  157.9 10.2 %all-to-all-start.3 = ((bf16[8,2,64,128]{3,2,1,0:T(8,128)(2,1)}), bf16[8,2,64,128]{3,2,1,0:T(8,128)(2,1)}, u32[]{:S(2)}, u32[]{:S(2)}) async-start(bf16[8,2,64,128]{3,2,1,0:T(8,128)(2,1)} %get-tuple-element.186), calls=%async_computation.3 | async-start | bytes 524288 | tf_op jit(solution)/shard_map/all_to_all | solution.py:1120
  168.2 45.9 %all-to-all-start.4 = ((bf16[4,2,64,1024]{3,2,1,0:T(8,128)(2,1)}), bf16[4,2,64,1024]{3,2,1,0:T(8,128)(2,1)}, u32[]{:S(2)}, u32[]{:S(2)}) async-start(bf16[4,2,64,1024]{3,2,1,0:T(8,128)(2,1)} %get-tuple-element.210), calls=%async_computation.4 | async-start | bytes 2097152 | tf_op jit(solution)/shard_map/all_to_all | solution.py:1128
  173.9 40.2 %collective-permute-start.29 = (bf16[4,2,32,1408]{3,2,0,1:T(8,128)(2,1)S(1)}, bf16[4,2,32,1408]{3,2,0,1:T(8,128)(2,1)}, u32[]{:S(2)}, u32[]{:S(2)}) collective-permute-start(bf16[4,2,32,1408]{3,2,0,1:T(8,128)(2,1)S(1)} %bitcast.210), channel_id=1, source_target_pairs={{0,16},{16,0},{1,17},{17,1},{2,18},{18,2},{3,19},{19,3},{4,20},{20... | collective-permute-start | bytes 2162696 | tf_op jit(solution)/shard_map/ppermute | solution.py:866
  176.2 25.8 %collective-permute-start.30 = (bf16[2,1,88,1024]{3,2,0,1:T(8,128)(2,1)S(1)}, bf16[2,1,88,1024]{3,2,0,1:T(8,128)(2,1)S(1)}, u32[]{:S(2)}, u32[]{:S(2)}) collective-permute-start(bf16[2,1,88,1024]{3,2,0,1:T(8,128)(2,1)S(1)} %select_bitcast_fusion.7), channel_id=1, source_target_pairs={{0,1},{1,0},{2,3},{3,2},{4,5},{5,4},{6,7},{7,6},{8,9},{9,8},{10,11... | collective-permute-start | bytes 1081352 | tf_op jit(solution)/shard_map/ppermute | solution.py:866
  176.7 26.3 %collective-permute-start.31 = (bf16[2,64,1024]{2,1,0:T(8,128)(2,1)S(1)}, bf16[2,64,1024]{2,1,0:T(8,128)(2,1)S(1)}, u32[]{:S(2)}, u32[]{:S(2)}) collective-permute-start(bf16[2,64,1024]{2,1,0:T(8,128)(2,1)S(1)} %get-tuple-element.209.refs_0_), channel_id=1, source_target_pairs={{0,4},{4,0},{8,12},{12,8},{1,5},{5,1},{9,13},{13,9},{2,6},{6,2},{1... | collective-permute-start | bytes 786440 | tf_op jit(solution)/shard_map/ppermute | solution.py:866
  178.7 30.1 %collective-permute-start.32 = (bf16[2,64,1024]{2,1,0:T(8,128)(2,1)S(1)}, bf16[2,64,1024]{2,1,0:T(8,128)(2,1)S(1)}, u32[]{:S(2)}, u32[]{:S(2)}) collective-permute-start(bf16[2,64,1024]{2,1,0:T(8,128)(2,1)S(1)} %get-tuple-element.209.refs_0_), channel_id=1, source_target_pairs={{0,8},{4,12},{8,0},{12,4},{1,9},{5,13},{9,1},{13,5},{2,10},{6,14},... | collective-permute-start | bytes 786440 | tf_op jit(solution)/shard_map/ppermute | solution.py:866
  180.1 33.9 %collective-permute-start.33 = (bf16[2,64,1024]{2,1,0:T(8,128)(2,1)S(1)}, bf16[2,64,1024]{2,1,0:T(8,128)(2,1)S(1)}, u32[]{:S(2)}, u32[]{:S(2)}) collective-permute-start(bf16[2,64,1024]{2,1,0:T(8,128)(2,1)S(1)} %get-tuple-element.209.refs_0_), channel_id=1, source_target_pairs={{0,12},{4,8},{8,4},{12,0},{1,13},{5,9},{9,5},{13,1},{2,14},{6,10},... | collective-permute-start | bytes 786440 | tf_op jit(solution)/shard_map/ppermute | solution.py:866
  214.1 5.3 %collective-permute-start.35 = (bf16[8,64,1024]{2,1,0:T(8,128)(2,1)}, bf16[8,64,1024]{2,1,0:T(8,128)(2,1)S(1)}, u32[]{:S(2)}, u32[]{:S(2)}) collective-permute-start(bf16[8,64,1024]{2,1,0:T(8,128)(2,1)} %get-tuple-element.222), channel_id=1, source_target_pairs={{0,2},{2,0},{1,3},{3,1},{4,6},{6,4},{5,7},{7,5},{8,10},{10,8},{9,1... | collective-permute-start | bytes 3145736 | tf_op jit(solution)/shard_map/ppermute | solution.py:866
  214.1 3.8 %collective-permute-start.34 = (bf16[8,64,640]{2,1,0:T(8,128)(2,1)}, bf16[8,64,640]{2,1,0:T(8,128)(2,1)S(1)}, u32[]{:S(2)}, u32[]{:S(2)}) collective-permute-start(bf16[8,64,640]{2,1,0:T(8,128)(2,1)} %get-tuple-element.213), channel_id=1, source_target_pairs={{0,2},{2,0},{1,3},{3,1},{4,6},{6,4},{5,7},{7,5},{8,10},{10,8},{9,1... | collective-permute-start | bytes 1966088 | tf_op jit(solution)/shard_map/ppermute | solution.py:866
  220.3 12.4 %collective-permute-start.40 = (bf16[2,2,32,1024]{3,2,0,1:T(8,128)(2,1)}, bf16[2,2,32,1024]{3,2,0,1:T(8,128)(2,1)}, u32[]{:S(2)}, u32[]{:S(2)}) collective-permute-start(bf16[2,2,32,1024]{3,2,0,1:T(8,128)(2,1)} %select_bitcast_fusion.10), channel_id=1, source_target_pairs={{0,2},{2,0},{1,3},{3,1},{4,6},{6,4},{5,7},{7,5},{8,10},{10,8},{9,1... | collective-permute-start | bytes 786440 | tf_op jit(solution)/shard_map/ppermute | solution.py:866
  221.6 27.1 %all-to-all-start.5 = ((bf16[4,2,64,1024]{3,2,1,0:T(8,128)(2,1)}), bf16[4,2,64,1024]{3,2,1,0:T(8,128)(2,1)S(1)}, u32[]{:S(2)}, u32[]{:S(2)}) async-start(bf16[4,2,64,1024]{3,2,1,0:T(8,128)(2,1)} %token_pieces.1), calls=%async_computation.5 | async-start | bytes 2097152 | tf_op jit(solution)/shard_map/all_to_all | solution.py:1214
  226.7 24.3 %copy-start.11 = (bf16[2,64,1024]{2,1,0:T(8,128)(2,1)S(1)}, bf16[2,64,1024]{2,1,0:T(8,128)(2,1)}, u32[]{:S(2)}) copy-start(bf16[2,64,1024]{2,1,0:T(8,128)(2,1)} %copy-done.10) | copy-start | bytes 786436
  226.7 24.3 %copy-start.14 = (f32[2,64,1024]{2,1,0:T(8,128)S(1)}, f32[2,64,1024]{2,1,0:T(8,128)}, u32[]{:S(2)}) copy-start(f32[2,64,1024]{2,1,0:T(8,128)} %copy-done.13) | copy-start | bytes 1572868
  226.7 24.3 %copy-start.16 = (f32[8,1024]{1,0:T(8,128)S(1)}, f32[8,1024]{1,0:T(8,128)}, u32[]{:S(2)}) copy-start(f32[8,1024]{1,0:T(8,128)} %get-tuple-element.169.gains_ref) | copy-start | bytes 98308
  226.7 11.3 %collective-permute-start.39 = (bf16[4,1,32,1408]{3,2,0,1:T(8,128)(2,1)S(1)}, bf16[4,1,32,1408]{3,2,0,1:T(8,128)(2,1)S(1)}, u32[]{:S(2)}, u32[]{:S(2)}) collective-permute-start(bf16[4,1,32,1408]{3,2,0,1:T(8,128)(2,1)S(1)} %select_bitcast_fusion.6), channel_id=1, source_target_pairs={{0,1},{1,0},{2,3},{3,2},{4,5},{5,4},{6,7},{7,6},{8,9},{9,8},{10,11... | collective-permute-start | bytes 1081352 | tf_op jit(solution)/shard_map/ppermute | solution.py:866
  228.3 29.5 %collective-permute-start.36 = (bf16[4,32,1152]{2,1,0:T(8,128)(2,1)}, bf16[4,32,1152]{2,1,0:T(8,128)(2,1)S(1)}, u32[]{:S(2)}, u32[]{:S(2)}) collective-permute-start(bf16[4,32,1152]{2,1,0:T(8,128)(2,1)} %get-tuple-element.225), channel_id=1, source_target_pairs={{0,1},{1,0},{2,3},{3,2},{4,5},{5,4},{6,7},{7,6},{8,9},{9,8},{10,11... | collective-permute-start | bytes 884744 | tf_op jit(solution)/shard_map/ppermute | solution.py:866
  228.8 29.0 %collective-permute-start.37 = (bf16[4,32,1152]{2,1,0:T(8,128)(2,1)}, bf16[4,32,1152]{2,1,0:T(8,128)(2,1)S(1)}, u32[]{:S(2)}, u32[]{:S(2)}) collective-permute-start(bf16[4,32,1152]{2,1,0:T(8,128)(2,1)} %get-tuple-element.226), channel_id=1, source_target_pairs={{0,16},{16,0},{1,17},{17,1},{2,18},{18,2},{3,19},{19,3},{4,20},{20... | collective-permute-start | bytes 884744 | tf_op jit(solution)/shard_map/ppermute | solution.py:866
  231.0 31.6 %collective-permute-start.38 = (bf16[4,32,1152]{2,1,0:T(8,128)(2,1)}, bf16[4,32,1152]{2,1,0:T(8,128)(2,1)S(1)}, u32[]{:S(2)}, u32[]{:S(2)}) collective-permute-start(bf16[4,32,1152]{2,1,0:T(8,128)(2,1)} %get-tuple-element.227), channel_id=1, source_target_pairs={{0,17},{1,16},{16,1},{17,0},{2,19},{3,18},{18,3},{19,2},{4,21},{5,... | collective-permute-start | bytes 884744 | tf_op jit(solution)/shard_map/ppermute | solution.py:866
  250.5 6.2 %collective-permute-start.41 = (bf16[2,1,32,1024]{3,2,0,1:T(8,128)(2,1)}, bf16[2,1,32,1024]{3,2,0,1:T(8,128)(2,1)S(1)}, u32[]{:S(2)}, u32[]{:S(2)}) collective-permute-start(bf16[2,1,32,1024]{3,2,0,1:T(8,128)(2,1)} %fusion.6), channel_id=1, source_target_pairs={{0,1},{1,0},{2,3},{3,2},{4,5},{5,4},{6,7},{7,6},{8,9},{9,8},{10,11... | collective-permute-start | bytes 393224 | tf_op jit(solution)/shard_map/ppermute | solution.py:866
  251.9 19.9 %collective-permute-start.43 = (bf16[64,1024]{1,0:T(8,128)(2,1)S(1)}, bf16[64,1024]{1,0:T(8,128)(2,1)}, u32[]{:S(2)}, u32[]{:S(2)}) collective-permute-start(bf16[64,1024]{1,0:T(8,128)(2,1)S(1)} %select_bitcast_fusion.13), channel_id=1, source_target_pairs={{0,16},{16,0},{1,17},{17,1},{2,18},{18,2},{3,19},{19,3},{4,20},{20... | collective-permute-start | bytes 393224 | tf_op jit(solution)/shard_map/ppermute | solution.py:866
  252.0 31.9 %all-to-all-start.6 = ((bf16[4,32,1408]{2,1,0:T(8,128)(2,1)}), bf16[4,32,1408]{2,1,0:T(8,128)(2,1)S(1)}, u32[]{:S(2)}, u32[]{:S(2)}) async-start(bf16[4,32,1408]{2,1,0:T(8,128)(2,1)} %fusion.2), calls=%async_computation.6 | async-start | bytes 720896 | tf_op jit(solution)/shard_map/all_to_all | solution.py:1224
  262.7 20.4 %collective-permute-start.48 = (bf16[88,1024]{1,0:T(8,128)(2,1)S(1)}, bf16[88,1024]{1,0:T(8,128)(2,1)S(1)}, u32[]{:S(2)}, u32[]{:S(2)}) collective-permute-start(bf16[88,1024]{1,0:T(8,128)(2,1)S(1)} %fusion.5), channel_id=1, source_target_pairs={{0,16},{16,0},{1,17},{17,1},{2,18},{18,2},{3,19},{19,3},{4,20},{20... | collective-permute-start | bytes 540680 | tf_op jit(solution)/shard_map/ppermute | solution.py:866
  262.8 11.3 %collective-permute-start.47 = (bf16[32,1024]{1,0:T(8,128)(2,1)S(1)}, bf16[32,1024]{1,0:T(8,128)(2,1)S(1)}, u32[]{:S(2)}, u32[]{:S(2)}) collective-permute-start(bf16[32,1024]{1,0:T(8,128)(2,1)S(1)} %fusion.11), channel_id=1, source_target_pairs={{0,16},{16,0},{1,17},{17,1},{2,18},{18,2},{3,19},{19,3},{4,20},{20... | collective-permute-start | bytes 196616 | tf_op jit(solution)/shard_map/ppermute | solution.py:866
  266.5 10.8 %collective-permute-start.44 = (bf16[32,1152]{1,0:T(8,128)(2,1)S(1)}, bf16[32,1152]{1,0:T(8,128)(2,1)S(1)}, u32[]{:S(2)}, u32[]{:S(2)}) collective-permute-start(bf16[32,1152]{1,0:T(8,128)(2,1)S(1)} %get-tuple-element.243), channel_id=1, source_target_pairs={{0,4},{4,0},{8,12},{12,8},{1,5},{5,1},{9,13},{13,9},{2,6},{6,2},{1... | collective-permute-start | bytes 221192 | tf_op jit(solution)/shard_map/ppermute | solution.py:866
  268.5 8.8 %collective-permute-start.45 = (bf16[32,1152]{1,0:T(8,128)(2,1)S(1)}, bf16[32,1152]{1,0:T(8,128)(2,1)S(1)}, u32[]{:S(2)}, u32[]{:S(2)}) collective-permute-start(bf16[32,1152]{1,0:T(8,128)(2,1)S(1)} %get-tuple-element.244), channel_id=1, source_target_pairs={{0,8},{4,12},{8,0},{12,4},{1,9},{5,13},{9,1},{13,5},{2,10},{6,14},... | collective-permute-start | bytes 221192 | tf_op jit(solution)/shard_map/ppermute | solution.py:866
  271.8 6.7 %collective-permute-start.46 = (bf16[32,1152]{1,0:T(8,128)(2,1)S(1)}, bf16[32,1152]{1,0:T(8,128)(2,1)S(1)}, u32[]{:S(2)}, u32[]{:S(2)}) collective-permute-start(bf16[32,1152]{1,0:T(8,128)(2,1)S(1)} %get-tuple-element.245), channel_id=1, source_target_pairs={{0,12},{4,8},{8,4},{12,0},{1,13},{5,9},{9,5},{13,1},{2,14},{6,10},... | collective-permute-start | bytes 221192 | tf_op jit(solution)/shard_map/ppermute | solution.py:866
  274.1 8.3 %collective-permute-start.42 = (bf16[64,1024]{1,0:T(8,128)(2,1)S(1)}, bf16[64,1024]{1,0:T(8,128)(2,1)S(1)}, u32[]{:S(2)}, u32[]{:S(2)}) collective-permute-start(bf16[64,1024]{1,0:T(8,128)(2,1)S(1)} %select_bitcast_fusion.14), channel_id=1, source_target_pairs={{0,16},{16,0},{1,17},{17,1},{2,18},{18,2},{3,19},{19,3},{4,20},{20... | collective-permute-start | bytes 393224 | tf_op jit(solution)/shard_map/ppermute | solution.py:866
  (33 other events, 203.3 us)

commit v3 on v2

--- a/solution.py
+++ b/solution.py
@@ -13,7 +13,7 @@
 EPSILON = 1e-05
 UNIT_EPSILON = 1e-06
 CHUNK = 128
-GROUP = 4
+GROUP = 8
 FREE = 24
 COST = 10**6
 MEGA = 1024 * 1024
@@ -38,6 +38,13 @@
     return dot(left[0], right[0]) + (dot(left[0], right[1]) + dot(left[1], right[0]))
 
 
+def long_mm(left, right, dims):
+    ((a_dim,), (b_dim,)), _ = dims
+    long_left = jnp.concatenate([left[0], left[0], left[1]], axis=a_dim)
+    long_right = jnp.concatenate([right[0], right[1], right[0]], axis=b_dim)
+    return lax.dot_general(long_left, long_right, dims, preferred_element_type=F32)
+
+
 def block_mask(size, width):
     row = lax.broadcasted_iota(jnp.int32, (size, size), 0)
     col = lax.broadcasted_iota(jnp.int32, (size, size), 1)
@@ -55,19 +62,19 @@
     eye = tri_masks(size)[2].astype(F32)
     near = block_mask(size, 8)
     base = [split(jnp.where(near, m, 0.0)) for m in mats]
-    square = [split(mm(b, b, NN)) for b in base]
+    square = [split(long_mm(b, b, NN)) for b in base]
     first = [eye - jnp.where(near, m, 0.0) for m in mats]
-    second = [f + mm(split(f), s, NN) for f, s in zip(first, square)]
-    fourth = [split(mm(s, s, NN)) for s in square]
-    inverse = [f + mm(split(f), s, NN) for f, s in zip(second, fourth)]
+    second = [f + long_mm(split(f), s, NN) for f, s in zip(first, square)]
+    fourth = [split(long_mm(s, s, NN)) for s in square]
+    inverse = [f + long_mm(split(f), s, NN) for f, s in zip(second, fourth)]
     width = 8
     while width < size:
         inside, wider = block_mask(size, width), block_mask(size, 2 * width)
         cut = jnp.logical_and(wider, jnp.logical_not(inside))
         off = [split(jnp.where(cut, m, 0.0)) for m in mats]
         halves = [split(t) for t in inverse]
-        step = [split(mm(t, o, NN)) for t, o in zip(halves, off)]
-        inverse = [t - mm(s, h, NN) for t, s, h in zip(inverse, step, halves)]
+        step = [split(long_mm(t, o, NN)) for t, o in zip(halves, off)]
+        inverse = [t - long_mm(s, h, NN) for t, s, h in zip(inverse, step, halves)]
         width *= 2
     return inverse
 
@@ -235,26 +242,26 @@
         ]
         beta = [beta_ref[r, :] for r in rows]
         mats = [
-            jnp.where(jnp.logical_and(s, strict), b * mm(k, k, NT), 0.0)
+            jnp.where(jnp.logical_and(s, strict), b * long_mm(k, k, NT), 0.0)
             for s, b, k in zip(same, beta, key)
         ]
         inverse = unit_lower_inverses(mats)
         for i, r in enumerate(rows):
             t_ref[r, :] = inverse[i]
             inv = split(inverse[i])
-            pseudo = mm(inv, split(beta[i] * v_ref[r, :]), NN)
+            pseudo = long_mm(inv, split(beta[i] * v_ref[r, :]), NN)
             weighed = split(
-                mm(inv, split(beta[i] * flag_ref[r, 3:4] * k_ref[r, :]), NN)
+                long_mm(inv, split(beta[i] * flag_ref[r, 3:4] * k_ref[r, :]), NN)
             )
             ends = split(flag_ref[r, 4:5] * k_ref[r, :])
             query = split(qh_ref[r, :] * HEAD ** (-0.5))
             sc_ref[r, :] = jnp.where(
-                jnp.logical_and(same[i], incl), mm(query, key[i], NT), 0.0
+                jnp.logical_and(same[i], incl), long_mm(query, key[i], NT), 0.0
             )
             pb_ref[r, :] = pseudo
             w_ref[r, :] = weighed[0].astype(F32) + weighed[1].astype(F32)
-            map_ref[r, :] = mm(weighed, ends, TN)
-            add_ref[r, :] = mm(split(pseudo), ends, TN)
+            map_ref[r, :] = long_mm(weighed, ends, TN)
+            add_ref[r, :] = long_mm(split(pseudo), ends, TN)
         return carry
 
     lax.fori_loop(0, count // GROUP, prepare, 0)
@@ -265,7 +272,7 @@
         rows = slice(n * CHUNK, (n + 1) * CHUNK)
         state_ref[rows, :] = state
         last = flag_ref[(n + 1) * CHUNK - 1 : (n + 1) * CHUNK, 3:4]
-        state = last * state - mm(split(state), split(map_ref[rows, :]), NN) + add_ref[rows, :]
+        state = last * state - long_mm(split(state), split(map_ref[rows, :]), NN) + add_ref[rows, :]
 
     def produce(group, carry):
         for i in range(GROUP):
@@ -274,15 +281,15 @@
             key = split(k_ref[r, :])
             state_i = split(state_ref[r, :])
             flag = flag_ref[r, 3:4]
-            pseudo = pb_ref[r, :] - mm(split(w_ref[r, :]), state_i, NT)
+            pseudo = pb_ref[r, :] - long_mm(split(w_ref[r, :]), state_i, NT)
             ps_ref[r, :] = pseudo
             halves = split(pseudo)
-            gram = jnp.where(jnp.logical_and(same, strict), mm(key, key, NT), 0.0)
+            gram = jnp.where(jnp.logical_and(same, strict), long_mm(key, key, NT), 0.0)
             er_ref[r, :] = (
-                v_ref[r, :] - flag * mm(key, state_i, NT) - mm(split(gram), halves, NN)
+                v_ref[r, :] - flag * long_mm(key, state_i, NT) - long_mm(split(gram), halves, NN)
             )
             query = split(qh_ref[r, :] * HEAD ** (-0.5))
-            out = flag * mm(query, state_i, NT) + mm(split(sc_ref[r, :]), halves, NN)
+            out = flag * long_mm(query, state_i, NT) + long_mm(split(sc_ref[r, :]), halves, NN)
             scale = lax.rsqrt(jnp.mean(out * out, axis=-1, keepdims=True) + EPSILON)
             hat = out * scale
             oh_ref[r, :] = hat

time: 290 us -> 291 us (level)
  waiting for transfers between devices: 85.3 us -> 90.6 us
  Pallas kernels: 70.6 us -> 65.6 us
    ppermute x49, waiting for transfers between devices: 72.4 us -> 79.5 us  [swap(): lax.ppermute(value, axis, [(i, i ^ mask) for i in range(lax.axis_size(axi...]
    pallas_call x13, Pallas kernels: 70.6 us -> 65.6 us  [run_kernel(): pl.pallas_call(body, name=name, out_shape=[jax.ShapeDtypeStruct(*s) for s...]
  transfers between devices with their start and end apart: 56 -> 56, of which waited for: 23 -> 22; matrix products, arithmetic and copies ran while one was open for 14% -> 14% of each run, Pallas kernels for 20% -> 18%
where the time goes in v3:
time: 291 us; the launch traced here: 286 us
  waiting for transfers between devices  90.6 us (31%)
  starting transfers between devices  82.1 us (28%)
  Pallas kernels  65.6 us (23%)
  other arithmetic  34.6 us (12%)
  local copies, waits for them, and re-layouts  11.2 us (4%)
    ppermute x49, waiting for transfers between devices, swap(): lax.ppermute(value, axis, [(i, i ^ mask) for i in range(lax.axis_size(axi...  79.5 us
    pallas_call x13, Pallas kernels, run_kernel(): pl.pallas_call(body, name=name, out_shape=[jax.ShapeDtypeStruct(*s) for s...  65.6 us
    ppermute x49, starting transfers between devices, swap(): lax.ppermute(value, axis, [(i, i ^ mask) for i in range(lax.axis_size(axi...  54.2 us
    all_to_all x1, waiting for transfers between devices, on_device(): norm_got = lax.all_to_all(norm_send, ('q',), 0, 0, tiled=True)  8.14 us
  transfers between devices with their start and end apart: 56, of which 22 were waited for; matrix products, arithmetic and copies ran while one was open for 14% of the time, Pallas kernels for 18%

profile of v3, /device:TPU:0, one launch (start us, length us, event | category | flops | bytes accessed | tf_op | source)
XLA Modules:
  0.0 285.8 jit_solution(14499003707965689320)
XLA Ops:
  1.3 2.5 pack_heads.1
  3.8 3.0 %collective-permute-start = (bf16[32,1152]{1,0:T(8,128)(2,1)}, bf16[32,1152]{1,0:T(8,128)(2,1)S(1)}, u32[]{:S(2)}, u32[]{:S(2)}) collective-permute-start(bf16[32,1152]{1,0:T(8,128)(2,1)} %get-tuple-element.138), channel_id=1, source_target_pairs={{0,4},{4,0},{8,12},{12,8},{1,5},{5,1},{9,13},{13,9},{2,6},{6,2},{1... | collective-permute-start | bytes 221192 | tf_op jit(solution)/shard_map/ppermute | solution.py:873
  6.8 1.6 collective-permute-start.1
  9.4 3.1 %collective-permute-start.3 = (bf16[64,1024]{1,0:T(8,128)(2,1)S(1)}, bf16[64,1024]{1,0:T(8,128)(2,1)S(1)}, u32[]{:S(2)}, u32[]{:S(2)}) collective-permute-start(bf16[64,1024]{1,0:T(8,128)(2,1)S(1)} %get-tuple-element.333), channel_id=1, source_target_pairs={{0,16},{16,0},{1,17},{17,1},{2,18},{18,2},{3,19},{19,3},{4,20},{20... | collective-permute-start | bytes 393224 | tf_op jit(solution)/shard_map/ppermute | solution.py:873
  20.3 1.6 collective-permute-start.5
  21.9 1.6 collective-permute-start.6
  24.6 2.9 %collective-permute-start.8 = (bf16[32,1024]{1,0:T(8,128)(2,1)S(1)}, bf16[32,1024]{1,0:T(8,128)(2,1)S(1)}, u32[]{:S(2)}, u32[]{:S(2)}) collective-permute-start(bf16[32,1024]{1,0:T(8,128)(2,1)S(1)} %copy-done.33), channel_id=1, source_target_pairs={{0,16},{16,0},{1,17},{17,1},{2,18},{18,2},{3,19},{19,3},{4,20},{20... | collective-permute-start | bytes 196616 | tf_op jit(solution)/shard_map/ppermute | solution.py:873
  27.6 11.3 %collective-permute-done.6 = bf16[2,64,1024]{2,1,0:T(8,128)(2,1)S(1)} collective-permute-done((bf16[2,64,1024]{2,1,0:T(8,128)(2,1)S(1)}, bf16[2,64,1024]{2,1,0:T(8,128)(2,1)S(1)}, u32[]{:S(2)}, u32[]{:S(2)}) %collective-permute-start.6) | collective-permute-done | bytes 262176 | tf_op jit(solution)/shard_map/ppermute | solution.py:873
  38.9 3.0 %collective-permute-done.7 = bf16[2,64,1024]{2,1,0:T(8,128)(2,1)S(1)} collective-permute-done((bf16[2,64,1024]{2,1,0:T(8,128)(2,1)S(1)}, bf16[2,64,1024]{2,1,0:T(8,128)(2,1)S(1)}, u32[]{:S(2)}, u32[]{:S(2)}) %collective-permute-start.7) | collective-permute-done | bytes 262176 | tf_op jit(solution)/shard_map/ppermute | solution.py:873
  42.1 1.6 collective-permute-start.9
  44.3 2.2 collective-permute-start.12
  47.2 3.5 %all-to-all-start = ((bf16[4,32,1408]{2,1,0:T(8,128)(2,1)}), bf16[4,32,1408]{2,1,0:T(8,128)(2,1)S(1)}, u32[]{:S(2)}, u32[]{:S(2)}) async-start(bf16[4,32,1408]{2,1,0:T(8,128)(2,1)} %reshape.392), calls=%async_computation | async-start | bytes 720896 | tf_op jit(solution)/shard_map/all_to_all | solution.py:1017
  50.7 7.0 %collective-permute-done.13 = bf16[2,32,1024]{2,1,0:T(8,128)(2,1)S(1)} collective-permute-done((bf16[2,32,1024]{2,1,0:T(8,128)(2,1)S(1)}, bf16[2,32,1024]{2,1,0:T(8,128)(2,1)S(1)}, u32[]{:S(2)}, u32[]{:S(2)}) %collective-permute-start.13) | collective-permute-done | bytes 131104 | tf_op jit(solution)/shard_map/ppermute | solution.py:873
  58.8 3.0 %collective-permute-done.11 = bf16[64,1024]{1,0:T(8,128)(2,1)} collective-permute-done((bf16[64,1024]{1,0:T(8,128)(2,1)}, bf16[64,1024]{1,0:T(8,128)(2,1)}, u32[]{:S(2)}, u32[]{:S(2)}) %collective-permute-start.11) | collective-permute-done | bytes 131104 | tf_op jit(solution)/shard_map/ppermute | solution.py:873
  61.8 2.0 all-to-all-done
  64.9 4.4 %all-to-all-start.2 = ((bf16[4,2,64,1024]{3,2,1,0:T(8,128)(2,1)}), bf16[4,2,64,1024]{3,2,1,0:T(8,128)(2,1)}, u32[]{:S(2)}, u32[]{:S(2)}) async-start(bf16[4,2,64,1024]{3,2,1,0:T(8,128)(2,1)} %broadcast_in_dim.28), calls=%async_computation.2 | async-start | bytes 2097152 | tf_op jit(solution)/shard_map/all_to_all | solution.py:1026
  70.7 1.6 collective-permute-start.16
  72.6 1.6 fusion.15
  74.3 2.0 collective-permute-start.17
  76.3 1.5 collective-permute-start.18
  78.9 17.5 %mixer_forward.1 = (bf16[4,2,512,128]{3,2,1,0:T(8,128)(2,1)}, f32[16,128]{1,0:T(8,128)}, f32[8,1024]{1,0:T(8,128)}, bf16[1024,1024]{1,0:T(8,128)(2,1)}, bf16[102...) custom-call(s32[4]{0:T(128)} %pad_add_fusion.pos_ref, ...), custom_call_target="tpu_custom_call" | custom-call | flops 25000000 | bytes 1024 | tf_op jit(solution)/shard_map/mixer_forward/pallas_call | solution.py:850
  96.4 1.2 collective-permute-done.18
  97.7 4.5 %collective-permute-done.19 = bf16[2,64,1024]{2,1,0:T(8,128)(2,1)S(1)} collective-permute-done((bf16[2,64,1024]{2,1,0:T(8,128)(2,1)}, bf16[2,64,1024]{2,1,0:T(8,128)(2,1)S(1)}, u32[]{:S(2)}, u32[]{:S(2)}) %collective-permute-start.19) | collective-permute-done | bytes 262176 | tf_op jit(solution)/shard_map/ppermute | solution.py:873
  102.9 1.5 collective-permute-start.21
  104.5 3.6 %all-to-all-start.1 = ((bf16[8,512,128]{2,1,0:T(8,128)(2,1)}), bf16[8,512,128]{2,1,0:T(8,128)(2,1)S(1)}, u32[]{:S(2)}, u32[]{:S(2)}) async-start(bf16[8,512,128]{2,1,0:T(8,128)(2,1)} %bitcast.42), calls=%async_computation.1 | async-start | bytes 2097152 | tf_op jit(solution)/shard_map/all_to_all | solution.py:1061
  108.0 11.2 %collective-permute-done.21 = bf16[8,32,1408]{2,1,0:T(8,128)(2,1)S(1)} collective-permute-done((bf16[8,32,1408]{2,1,0:T(8,128)(2,1)S(1)}, bf16[8,32,1408]{2,1,0:T(8,128)(2,1)S(1)}, u32[]{:S(2)}, u32[]{:S(2)}) %collective-permute-start.21) | collective-permute-done | bytes 720928 | tf_op jit(solution)/shard_map/ppermute | solution.py:873
  119.4 1.3 pad_maximum_fusion
  121.7 2.1 pad_maximum_fusion.4.cot_ref
  123.8 2.2 collective-permute-done.23
  129.5 9.4 %feed_forward.1 = (bf16[1024,1024]{1,0:T(8,128)(2,1)S(1)}, bf16[512,1024]{1,0:T(8,128)(2,1)S(1)}, bf16[512,1408]{1,0:T(8,128)(2,1)S(1)}, bf16[512,704]{1,0:T(8,1...) custom-call(s32[4]{0:T(128)S(1)} %copy-done.17, ...), custom_call_target="tpu_custom_call" | custom-call | flops 12000000 | bytes 1024 | tf_op jit(solution)/shard_map/feed_forward/pallas_call | solution.py:850
  140.1 2.3 collective-permute-start.26
  142.4 5.1 %feed_forward_grads.1 = (bf16[8,64,1408]{2,1,0:T(8,128)(2,1)S(1)}, bf16[8,64,1408]{2,1,0:T(8,128)(2,1)}, bf16[2,176,1024]{2,1,0:T(8,128)(2,1)S(1)}, bf16[2,176,1...) custom-call(s32[4]{0:T(128)S(1)} %copy-done.17, bf16[512,1024]{1,0:T(8,128)(2,1)S(1)} %get-tuple-element.175.normed_ref, ...), custom_call_target="tpu_custom_call" | custom-call | flops 6000000 | bytes 1024 | tf_op jit(solution)/shard_map/feed_forward_grads/pallas_call | solution.py:850
  148.7 5.4 %collective-permute-done.26.rest_2_ = bf16[2,64,1024]{2,1,0:T(8,128)(2,1)S(1)} collective-permute-done((bf16[2,64,1024]{2,1,0:T(8,128)(2,1)S(1)}, bf16[2,64,1024]{2,1,0:T(8,128)(2,1)S(1)}, u32[]{:S(2)}, u32[]{:S(2)}) %collective-permute-start.26) | collective-permute-done | bytes 262176 | tf_op jit(solution)/shard_map/ppermute | solution.py:873
  154.6 2.3 branch_gradient.1
  157.7 4.2 %all-to-all-start.3 = ((bf16[8,2,64,128]{3,2,1,0:T(8,128)(2,1)}), bf16[8,2,64,128]{3,2,1,0:T(8,128)(2,1)}, u32[]{:S(2)}, u32[]{:S(2)}) async-start(bf16[8,2,64,128]{3,2,1,0:T(8,128)(2,1)} %get-tuple-element.186), calls=%async_computation.3 | async-start | bytes 524288 | tf_op jit(solution)/shard_map/all_to_all | solution.py:1127
  161.9 2.2 add_convert_fusion.1
  164.2 2.8 add_convert_fusion
  168.0 4.6 %all-to-all-start.4 = ((bf16[4,2,64,1024]{3,2,1,0:T(8,128)(2,1)}), bf16[4,2,64,1024]{3,2,1,0:T(8,128)(2,1)}, u32[]{:S(2)}, u32[]{:S(2)}) async-start(bf16[4,2,64,1024]{3,2,1,0:T(8,128)(2,1)} %get-tuple-element.210), calls=%async_computation.4 | async-start | bytes 2097152 | tf_op jit(solution)/shard_map/all_to_all | solution.py:1135
  174.3 1.6 collective-permute-start.30
  175.8 2.0 collective-permute-start.31
  177.8 1.5 collective-permute-start.32
  179.3 20.9 %mixer_backward.1 = (bf16[8,64,1024]{2,1,0:T(8,128)(2,1)}, bf16[8,64,1024]{2,1,0:T(8,128)(2,1)}, bf16[8,64,640]{2,1,0:T(8,128)(2,1)}, bf16[8,64,640]{2,1,0:T(8,128)(2,1)}) custom-call(s32[4]{0:T(128)} %pad_add_fusion.pos_ref, bf16[8,2,64,128]{3,2,1,0:T(8,128)(2,1)} %all-to-all-done.3.dh_ref, f32[1032,8]{1,0:T(8,128)} %pad_convert_fusion.flag_ref, ...), custom_call_target="tpu_custom_call" | custom-call | flops 25000000 | bytes 1024 | tf_op jit(solution)/shard_map/mixer_backward/pallas_call | solution.py:850
  201.4 7.1 %collective-permute-done.32.refs_2_ = bf16[2,64,1024]{2,1,0:T(8,128)(2,1)S(1)} collective-permute-done((bf16[2,64,1024]{2,1,0:T(8,128)(2,1)S(1)}, bf16[2,64,1024]{2,1,0:T(8,128)(2,1)S(1)}, u32[]{:S(2)}, u32[]{:S(2)}) %collective-permute-start.32) | collective-permute-done | bytes 262176 | tf_op jit(solution)/shard_map/ppermute | solution.py:873
  208.4 5.3 %collective-permute-done.33.refs_3_ = bf16[2,64,1024]{2,1,0:T(8,128)(2,1)S(1)} collective-permute-done((bf16[2,64,1024]{2,1,0:T(8,128)(2,1)S(1)}, bf16[2,64,1024]{2,1,0:T(8,128)(2,1)S(1)}, u32[]{:S(2)}, u32[]{:S(2)}) %collective-permute-start.33) | collective-permute-done | bytes 262176 | tf_op jit(solution)/shard_map/ppermute | solution.py:873
  215.3 2.2 collective-permute-done.34.got_ref
  217.6 1.5 merge_heads.1
  221.3 3.6 %all-to-all-start.5 = ((bf16[4,2,64,1024]{3,2,1,0:T(8,128)(2,1)}), bf16[4,2,64,1024]{3,2,1,0:T(8,128)(2,1)S(1)}, u32[]{:S(2)}, u32[]{:S(2)}) async-start(bf16[4,2,64,1024]{3,2,1,0:T(8,128)(2,1)} %token_pieces.1), calls=%async_computation.5 | async-start | bytes 2097152 | tf_op jit(solution)/shard_map/all_to_all | solution.py:1221
  225.0 1.3 fusion.1
  226.4 1.6 collective-permute-start.39
  229.0 3.4 %collective-permute-start.38 = (bf16[4,32,1152]{2,1,0:T(8,128)(2,1)}, bf16[4,32,1152]{2,1,0:T(8,128)(2,1)S(1)}, u32[]{:S(2)}, u32[]{:S(2)}) collective-permute-start(bf16[4,32,1152]{2,1,0:T(8,128)(2,1)} %get-tuple-element.227), channel_id=1, source_target_pairs={{0,17},{1,16},{16,1},{17,0},{2,19},{3,18},{18,3},{19,2},{4,21},{5,... | collective-permute-start | bytes 884744 | tf_op jit(solution)/shard_map/ppermute | solution.py:873
  232.4 1.8 convert_add_fusion.3
  234.2 3.5 %collective-permute-done.39 = bf16[4,1,32,1408]{3,2,0,1:T(8,128)(2,1)S(1)} collective-permute-done((bf16[4,1,32,1408]{3,2,0,1:T(8,128)(2,1)S(1)}, bf16[4,1,32,1408]{3,2,0,1:T(8,128)(2,1)S(1)}, u32[]{:S(2)}, u32[]{:S(2)}) %collective-permute-start.39) | collective-permute-done | bytes 360480 | tf_op jit(solution)/shard_map/ppermute | solution.py:873
  238.6 8.1 %all-to-all-done.5.got_ref = bf16[4,2,64,1024]{3,2,1,0:T(8,128)(2,1)S(1)} async-done(((bf16[4,2,64,1024]{3,2,1,0:T(8,128)(2,1)}), bf16[4,2,64,1024]{3,2,1,0:T(8,128)(2,1)S(1)}, u32[]{:S(2)}, u32[]{:S(2)}) %all-to-all-start.5) | async-done | bytes 1048608 | tf_op jit(solution)/shard_map/all_to_all | solution.py:1221
  246.7 1.7 fusion.6
  248.4 1.5 collective-permute-start.41
  250.9 4.1 %all-to-all-start.6 = ((bf16[4,32,1408]{2,1,0:T(8,128)(2,1)}), bf16[4,32,1408]{2,1,0:T(8,128)(2,1)S(1)}, u32[]{:S(2)}, u32[]{:S(2)}) async-start(bf16[4,32,1408]{2,1,0:T(8,128)(2,1)} %fusion.2), calls=%async_computation.6 | async-start | bytes 720896 | tf_op jit(solution)/shard_map/all_to_all | solution.py:1231
  256.1 6.3 %collective-permute-done.38.refs_3_ = bf16[4,32,1152]{2,1,0:T(8,128)(2,1)S(1)} collective-permute-done((bf16[4,32,1152]{2,1,0:T(8,128)(2,1)}, bf16[4,32,1152]{2,1,0:T(8,128)(2,1)S(1)}, u32[]{:S(2)}, u32[]{:S(2)}) %collective-permute-start.38) | collective-permute-done | bytes 294944 | tf_op jit(solution)/shard_map/ppermute | solution.py:873
  262.5 3.0 %collective-permute-start.47 = (bf16[32,1024]{1,0:T(8,128)(2,1)S(1)}, bf16[32,1024]{1,0:T(8,128)(2,1)S(1)}, u32[]{:S(2)}, u32[]{:S(2)}) collective-permute-start(bf16[32,1024]{1,0:T(8,128)(2,1)S(1)} %fusion.11), channel_id=1, source_target_pairs={{0,16},{16,0},{1,17},{17,1},{2,18},{18,2},{3,19},{19,3},{4,20},{20... | collective-permute-start | bytes 196616 | tf_op jit(solution)/shard_map/ppermute | solution.py:873
  266.2 4.8 %collective-permute-start.44 = (bf16[32,1152]{1,0:T(8,128)(2,1)S(1)}, bf16[32,1152]{1,0:T(8,128)(2,1)S(1)}, u32[]{:S(2)}, u32[]{:S(2)}) collective-permute-start(bf16[32,1152]{1,0:T(8,128)(2,1)S(1)} %get-tuple-element.243), channel_id=1, source_target_pairs={{0,4},{4,0},{8,12},{12,8},{1,5},{5,1},{9,13},{13,9},{2,6},{6,2},{1... | collective-permute-start | bytes 221192 | tf_op jit(solution)/shard_map/ppermute | solution.py:873
  270.9 1.5 convert_reduce_fusion
  272.5 1.6 collective-permute-start.46
  276.5 2.3 collective-permute-done.46.refs_3_
  278.8 1.4 spread_heads.1
  280.7 2.3 collective-permute-done.42
  (225 shorter events, 43.8 us)
Async XLA Ops:
  0.6 16.5 %copy-start.38 = (s32[2,1,1024]{2,1,0:T(1,128)S(1)}, s32[2,1,1024]{2,1,0:T(1,128)}, u32[]{:S(2)}) copy-start(s32[2,1,1024]{2,1,0:T(1,128)} %param.18) | copy-start | bytes 24580
  0.7 17.1 %copy-start.36 = (bf16[32,2816]{1,0:T(8,128)(2,1)S(1)}, bf16[32,2816]{1,0:T(8,128)(2,1)}, u32[]{:S(2)}) copy-start(bf16[32,2816]{1,0:T(8,128)(2,1)} %param.25) | copy-start | bytes 540676
  3.8 16.5 %collective-permute-start = (bf16[32,1152]{1,0:T(8,128)(2,1)}, bf16[32,1152]{1,0:T(8,128)(2,1)S(1)}, u32[]{:S(2)}, u32[]{:S(2)}) collective-permute-start(bf16[32,1152]{1,0:T(8,128)(2,1)} %get-tuple-element.138), channel_id=1, source_target_pairs={{0,4},{4,0},{8,12},{12,8},{1,5},{5,1},{9,13},{13,9},{2,6},{6,2},{1... | collective-permute-start | bytes 221192 | tf_op jit(solution)/shard_map/ppermute | solution.py:873
  6.8 13.5 %collective-permute-start.1 = (bf16[32,1152]{1,0:T(8,128)(2,1)}, bf16[32,1152]{1,0:T(8,128)(2,1)S(1)}, u32[]{:S(2)}, u32[]{:S(2)}) collective-permute-start(bf16[32,1152]{1,0:T(8,128)(2,1)} %get-tuple-element.139), channel_id=1, source_target_pairs={{0,8},{4,12},{8,0},{12,4},{1,9},{5,13},{9,1},{13,5},{2,10},{6,14},... | collective-permute-start | bytes 221192 | tf_op jit(solution)/shard_map/ppermute | solution.py:873
  8.4 11.9 %collective-permute-start.2 = (bf16[32,1152]{1,0:T(8,128)(2,1)}, bf16[32,1152]{1,0:T(8,128)(2,1)S(1)}, u32[]{:S(2)}, u32[]{:S(2)}) collective-permute-start(bf16[32,1152]{1,0:T(8,128)(2,1)} %get-tuple-element.140), channel_id=1, source_target_pairs={{0,12},{4,8},{8,4},{12,0},{1,13},{5,9},{9,5},{13,1},{2,14},{6,10},... | collective-permute-start | bytes 221192 | tf_op jit(solution)/shard_map/ppermute | solution.py:873
  9.4 10.9 %collective-permute-start.3 = (bf16[64,1024]{1,0:T(8,128)(2,1)S(1)}, bf16[64,1024]{1,0:T(8,128)(2,1)S(1)}, u32[]{:S(2)}, u32[]{:S(2)}) collective-permute-start(bf16[64,1024]{1,0:T(8,128)(2,1)S(1)} %get-tuple-element.333), channel_id=1, source_target_pairs={{0,16},{16,0},{1,17},{17,1},{2,18},{18,2},{3,19},{19,3},{4,20},{20... | collective-permute-start | bytes 393224 | tf_op jit(solution)/shard_map/ppermute | solution.py:873
  20.3 21.5 %copy-start.10 = (bf16[2,64,1024]{2,1,0:T(8,128)(2,1)}, bf16[2,64,1024]{2,1,0:T(8,128)(2,1)S(1)}, u32[]{:S(2)}) copy-start(bf16[2,64,1024]{2,1,0:T(8,128)(2,1)S(1)} %get-tuple-element.331.x_ref) | copy-start | bytes 786436
  20.3 7.2 %collective-permute-start.5 = (bf16[2,64,1024]{2,1,0:T(8,128)(2,1)S(1)}, bf16[2,64,1024]{2,1,0:T(8,128)(2,1)S(1)}, u32[]{:S(2)}, u32[]{:S(2)}) collective-permute-start(bf16[2,64,1024]{2,1,0:T(8,128)(2,1)S(1)} %get-tuple-element.331.x_ref), channel_id=1, source_target_pairs={{0,4},{4,0},{8,12},{12,8},{1,5},{5,1},{9,13},{13,9},{2,6},{6,2},{1... | collective-permute-start | bytes 786440 | tf_op jit(solution)/shard_map/ppermute | solution.py:873
  21.9 17.0 %collective-permute-start.6 = (bf16[2,64,1024]{2,1,0:T(8,128)(2,1)S(1)}, bf16[2,64,1024]{2,1,0:T(8,128)(2,1)S(1)}, u32[]{:S(2)}, u32[]{:S(2)}) collective-permute-start(bf16[2,64,1024]{2,1,0:T(8,128)(2,1)S(1)} %get-tuple-element.331.x_ref), channel_id=1, source_target_pairs={{0,8},{4,12},{8,0},{12,4},{1,9},{5,13},{9,1},{13,5},{2,10},{6,14},... | collective-permute-start | bytes 786440 | tf_op jit(solution)/shard_map/ppermute | solution.py:873
  23.5 18.4 %collective-permute-start.7 = (bf16[2,64,1024]{2,1,0:T(8,128)(2,1)S(1)}, bf16[2,64,1024]{2,1,0:T(8,128)(2,1)S(1)}, u32[]{:S(2)}, u32[]{:S(2)}) collective-permute-start(bf16[2,64,1024]{2,1,0:T(8,128)(2,1)S(1)} %get-tuple-element.331.x_ref), channel_id=1, source_target_pairs={{0,12},{4,8},{8,4},{12,0},{1,13},{5,9},{9,5},{13,1},{2,14},{6,10},... | collective-permute-start | bytes 786440 | tf_op jit(solution)/shard_map/ppermute | solution.py:873
  24.0 18.1 %collective-permute-start.4 = (bf16[4,32,1152]{2,1,0:T(8,128)(2,1)S(1)}, bf16[4,32,1152]{2,1,0:T(8,128)(2,1)S(1)}, u32[]{:S(2)}, u32[]{:S(2)}) collective-permute-start(bf16[4,32,1152]{2,1,0:T(8,128)(2,1)S(1)} %get-tuple-element.323), channel_id=1, source_target_pairs={{0,16},{16,0},{1,17},{17,1},{2,18},{18,2},{3,19},{19,3},{4,20},{20... | collective-permute-start | bytes 884744 | tf_op jit(solution)/shard_map/ppermute | solution.py:873
  24.6 17.5 %collective-permute-start.8 = (bf16[32,1024]{1,0:T(8,128)(2,1)S(1)}, bf16[32,1024]{1,0:T(8,128)(2,1)S(1)}, u32[]{:S(2)}, u32[]{:S(2)}) collective-permute-start(bf16[32,1024]{1,0:T(8,128)(2,1)S(1)} %copy-done.33), channel_id=1, source_target_pairs={{0,16},{16,0},{1,17},{17,1},{2,18},{18,2},{3,19},{19,3},{4,20},{20... | collective-permute-start | bytes 196616 | tf_op jit(solution)/shard_map/ppermute | solution.py:873
  42.0 16.5 %copy-start = (bf16[4,2,64,1024]{3,2,1,0:T(8,128)(2,1)}, bf16[4,2,64,1024]{3,2,1,0:T(8,128)(2,1)S(1)}, u32[]{:S(2)}) copy-start(bf16[4,2,64,1024]{3,2,1,0:T(8,128)(2,1)S(1)} %pad_maximum_fusion.3.xown_ref) | copy-start | bytes 3145732
  42.1 16.4 %collective-permute-start.9 = (bf16[8,32,1152]{2,1,0:T(8,128)(2,1)S(1)}, bf16[8,32,1152]{2,1,0:T(8,128)(2,1)S(1)}, u32[]{:S(2)}, u32[]{:S(2)}) collective-permute-start(bf16[8,32,1152]{2,1,0:T(8,128)(2,1)S(1)} %bitcast.207), channel_id=1, source_target_pairs={{0,1},{1,0},{2,3},{3,2},{4,5},{5,4},{6,7},{7,6},{8,9},{9,8},{10,11... | collective-permute-start | bytes 1769480 | tf_op jit(solution)/shard_map/ppermute | solution.py:873
  43.7 14.0 %collective-permute-start.13 = (bf16[2,32,1024]{2,1,0:T(8,128)(2,1)S(1)}, bf16[2,32,1024]{2,1,0:T(8,128)(2,1)S(1)}, u32[]{:S(2)}, u32[]{:S(2)}) collective-permute-start(bf16[2,32,1024]{2,1,0:T(8,128)(2,1)S(1)} %pad_maximum_fusion.14), channel_id=1, source_target_pairs={{0,1},{1,0},{2,3},{3,2},{4,5},{5,4},{6,7},{7,6},{8,9},{9,8},{10,11... | collective-permute-start | bytes 393224 | tf_op jit(solution)/shard_map/ppermute | solution.py:873
  44.3 19.5 %collective-permute-start.10 = (bf16[4,2,64,1024]{3,2,1,0:T(8,128)(2,1)S(1)}, bf16[4,2,64,1024]{3,2,1,0:T(8,128)(2,1)}, u32[]{:S(2)}, u32[]{:S(2)}) collective-permute-start(bf16[4,2,64,1024]{3,2,1,0:T(8,128)(2,1)S(1)} %pad_maximum_fusion.3.xown_ref), channel_id=1, source_target_pairs={{0,2},{2,0},{1,3},{3,1},{4,6},{6,4},{5,7},{7,5},{8,10},{10,8},{9,1... | collective-permute-start | bytes 3145736 | tf_op jit(solution)/shard_map/ppermute | solution.py:873
  44.3 17.6 %collective-permute-start.12 = (bf16[88,1024]{1,0:T(8,128)(2,1)}, bf16[88,1024]{1,0:T(8,128)(2,1)}, u32[]{:S(2)}, u32[]{:S(2)}) collective-permute-start(bf16[88,1024]{1,0:T(8,128)(2,1)} %param.27), channel_id=1, source_target_pairs={{0,16},{16,0},{1,17},{17,1},{2,18},{18,2},{3,19},{19,3},{4,20},{20... | collective-permute-start | bytes 540680 | tf_op jit(solution)/shard_map/ppermute | solution.py:873
  46.5 15.4 %collective-permute-start.11 = (bf16[64,1024]{1,0:T(8,128)(2,1)}, bf16[64,1024]{1,0:T(8,128)(2,1)}, u32[]{:S(2)}, u32[]{:S(2)}) collective-permute-start(bf16[64,1024]{1,0:T(8,128)(2,1)} %get-tuple-element.148), channel_id=1, source_target_pairs={{0,16},{16,0},{1,17},{17,1},{2,18},{18,2},{3,19},{19,3},{4,20},{20... | collective-permute-start | bytes 393224 | tf_op jit(solution)/shard_map/ppermute | solution.py:873
  47.2 16.6 %all-to-all-start = ((bf16[4,32,1408]{2,1,0:T(8,128)(2,1)}), bf16[4,32,1408]{2,1,0:T(8,128)(2,1)S(1)}, u32[]{:S(2)}, u32[]{:S(2)}) async-start(bf16[4,32,1408]{2,1,0:T(8,128)(2,1)} %reshape.392), calls=%async_computation | async-start | bytes 720896 | tf_op jit(solution)/shard_map/all_to_all | solution.py:1017
  64.9 37.3 %all-to-all-start.2 = ((bf16[4,2,64,1024]{3,2,1,0:T(8,128)(2,1)}), bf16[4,2,64,1024]{3,2,1,0:T(8,128)(2,1)}, u32[]{:S(2)}, u32[]{:S(2)}) async-start(bf16[4,2,64,1024]{3,2,1,0:T(8,128)(2,1)} %broadcast_in_dim.28), calls=%async_computation.2 | async-start | bytes 2097152 | tf_op jit(solution)/shard_map/all_to_all | solution.py:1026
  69.6 8.3 %collective-permute-start.14 = (bf16[8,64,640]{2,1,0:T(8,128)(2,1)S(1)}, bf16[8,64,640]{2,1,0:T(8,128)(2,1)S(1)}, u32[]{:S(2)}, u32[]{:S(2)}) collective-permute-start(bf16[8,64,640]{2,1,0:T(8,128)(2,1)S(1)} %pad_maximum_fusion.7), channel_id=1, source_target_pairs={{0,2},{2,0},{1,3},{3,1},{4,6},{6,4},{5,7},{7,5},{8,10},{10,8},{9,1... | collective-permute-start | bytes 1966088 | tf_op jit(solution)/shard_map/ppermute | solution.py:873
  70.7 31.5 %collective-permute-start.16 = (bf16[2,88,1024]{2,1,0:T(8,128)(2,1)S(1)}, bf16[2,88,1024]{2,1,0:T(8,128)(2,1)S(1)}, u32[]{:S(2)}, u32[]{:S(2)}) collective-permute-start(bf16[2,88,1024]{2,1,0:T(8,128)(2,1)S(1)} %pad_maximum_fusion.9), channel_id=1, source_target_pairs={{0,1},{1,0},{2,3},{3,2},{4,5},{5,4},{6,7},{7,6},{8,9},{9,8},{10,11... | collective-permute-start | bytes 1081352 | tf_op jit(solution)/shard_map/ppermute | solution.py:873
  72.3 29.9 %collective-permute-start.15 = (bf16[4,32,1408]{2,1,0:T(8,128)(2,1)S(1)}, bf16[4,32,1408]{2,1,0:T(8,128)(2,1)S(1)}, u32[]{:S(2)}, u32[]{:S(2)}) collective-permute-start(bf16[4,32,1408]{2,1,0:T(8,128)(2,1)S(1)} %all-to-all-done), channel_id=1, source_target_pairs={{0,16},{16,0},{1,17},{17,1},{2,18},{18,2},{3,19},{19,3},{4,20},{20... | collective-permute-start | bytes 1081352 | tf_op jit(solution)/shard_map/ppermute | solution.py:873
  74.3 47.2 %copy-start.3 = (bf16[1,2,64,1024]{3,2,1,0:T(8,128)(2,1)}, bf16[1,2,64,1024]{3,2,1,0:T(8,128)(2,1)S(1)}, u32[]{:S(2)}) copy-start(bf16[1,2,64,1024]{3,2,1,0:T(8,128)(2,1)S(1)} %get-tuple-element.324.cot_ref) | copy-start | bytes 786436
  74.3 22.1 %collective-permute-start.17 = (bf16[2,64,1024]{2,1,0:T(8,128)(2,1)}, bf16[2,64,1024]{2,1,0:T(8,128)(2,1)}, u32[]{:S(2)}, u32[]{:S(2)}) collective-permute-start(bf16[2,64,1024]{2,1,0:T(8,128)(2,1)} %get-tuple-element.325), channel_id=1, source_target_pairs={{0,4},{4,0},{8,12},{12,8},{1,5},{5,1},{9,13},{13,9},{2,6},{6,2},{1... | collective-permute-start | bytes 786440 | tf_op jit(solution)/shard_map/ppermute | solution.py:873
  76.3 21.4 %collective-permute-start.18 = (bf16[2,64,1024]{2,1,0:T(8,128)(2,1)}, bf16[2,64,1024]{2,1,0:T(8,128)(2,1)}, u32[]{:S(2)}, u32[]{:S(2)}) collective-permute-start(bf16[2,64,1024]{2,1,0:T(8,128)(2,1)} %get-tuple-element.325), channel_id=1, source_target_pairs={{0,8},{4,12},{8,0},{12,4},{1,9},{5,13},{9,1},{13,5},{2,10},{6,14},... | collective-permute-start | bytes 786440 | tf_op jit(solution)/shard_map/ppermute | solution.py:873
  77.8 24.3 %collective-permute-start.19 = (bf16[2,64,1024]{2,1,0:T(8,128)(2,1)}, bf16[2,64,1024]{2,1,0:T(8,128)(2,1)S(1)}, u32[]{:S(2)}, u32[]{:S(2)}) collective-permute-start(bf16[2,64,1024]{2,1,0:T(8,128)(2,1)} %get-tuple-element.325), channel_id=1, source_target_pairs={{0,12},{4,8},{8,4},{12,0},{1,13},{5,9},{9,5},{13,1},{2,14},{6,10},... | collective-permute-start | bytes 786440 | tf_op jit(solution)/shard_map/ppermute | solution.py:873
  102.9 16.3 %collective-permute-start.21 = (bf16[8,32,1408]{2,1,0:T(8,128)(2,1)S(1)}, bf16[8,32,1408]{2,1,0:T(8,128)(2,1)S(1)}, u32[]{:S(2)}, u32[]{:S(2)}) collective-permute-start(bf16[8,32,1408]{2,1,0:T(8,128)(2,1)S(1)} %bitcast.206), channel_id=1, source_target_pairs={{0,1},{1,0},{2,3},{3,2},{4,5},{5,4},{6,7},{7,6},{8,9},{9,8},{10,11... | collective-permute-start | bytes 2162696 | tf_op jit(solution)/shard_map/ppermute | solution.py:873
  104.5 22.0 %all-to-all-start.1 = ((bf16[8,512,128]{2,1,0:T(8,128)(2,1)}), bf16[8,512,128]{2,1,0:T(8,128)(2,1)S(1)}, u32[]{:S(2)}, u32[]{:S(2)}) async-start(bf16[8,512,128]{2,1,0:T(8,128)(2,1)} %bitcast.42), calls=%async_computation.1 | async-start | bytes 2097152 | tf_op jit(solution)/shard_map/all_to_all | solution.py:1061
  120.7 6.1 %collective-permute-start.22 = (bf16[2,4,64,1408]{3,2,1,0:T(8,128)(2,1)}, bf16[2,4,64,1408]{3,2,1,0:T(8,128)(2,1)}, u32[]{:S(2)}, u32[]{:S(2)}) collective-permute-start(bf16[2,4,64,1408]{3,2,1,0:T(8,128)(2,1)} %bitcast.57.pown_ref), channel_id=1, source_target_pairs={{0,2},{2,0},{1,3},{3,1},{4,6},{6,4},{5,7},{7,5},{8,10},{10,8},{9,1... | collective-permute-start | bytes 4325384 | tf_op jit(solution)/shard_map/ppermute | solution.py:873
  120.9 5.1 %collective-permute-start.23 = (bf16[2,176,1024]{2,1,0:T(8,128)(2,1)S(1)}, bf16[2,176,1024]{2,1,0:T(8,128)(2,1)S(1)}, u32[]{:S(2)}, u32[]{:S(2)}) collective-permute-start(bf16[2,176,1024]{2,1,0:T(8,128)(2,1)S(1)} %bitcast.205), channel_id=1, source_target_pairs={{0,2},{2,0},{1,3},{3,1},{4,6},{6,4},{5,7},{7,5},{8,10},{10,8},{9,1... | collective-permute-start | bytes 2162696 | tf_op jit(solution)/shard_map/ppermute | solution.py:873
  121.4 5.4 %collective-permute-start.20 = (bf16[4,2,64,1024]{3,2,1,0:T(8,128)(2,1)}, bf16[4,2,64,1024]{3,2,1,0:T(8,128)(2,1)}, u32[]{:S(2)}, u32[]{:S(2)}) collective-permute-start(bf16[4,2,64,1024]{3,2,1,0:T(8,128)(2,1)} %all-to-all-done.2.oown_ref), channel_id=1, source_target_pairs={{0,2},{2,0},{1,3},{3,1},{4,6},{6,4},{5,7},{7,5},{8,10},{10,8},{9,1... | collective-permute-start | bytes 3145736 | tf_op jit(solution)/shard_map/ppermute | solution.py:873
  138.9 8.6 %collective-permute-start.24 = (bf16[2,64,1024]{2,1,0:T(8,128)(2,1)S(1)}, bf16[2,64,1024]{2,1,0:T(8,128)(2,1)S(1)}, u32[]{:S(2)}, u32[]{:S(2)}) collective-permute-start(bf16[2,64,1024]{2,1,0:T(8,128)(2,1)S(1)} %get-tuple-element.171), channel_id=1, source_target_pairs={{0,4},{4,0},{8,12},{12,8},{1,5},{5,1},{9,13},{13,9},{2,6},{6,2},{1... | collective-permute-start | bytes 786440 | tf_op jit(solution)/shard_map/ppermute | solution.py:873
  139.5 9.2 %collective-permute-start.25 = (bf16[2,64,1024]{2,1,0:T(8,128)(2,1)S(1)}, bf16[2,64,1024]{2,1,0:T(8,128)(2,1)S(1)}, u32[]{:S(2)}, u32[]{:S(2)}) collective-permute-start(bf16[2,64,1024]{2,1,0:T(8,128)(2,1)S(1)} %get-tuple-element.172), channel_id=1, source_target_pairs={{0,8},{4,12},{8,0},{12,4},{1,9},{5,13},{9,1},{13,5},{2,10},{6,14},... | collective-permute-start | bytes 786440 | tf_op jit(solution)/shard_map/ppermute | solution.py:873
  140.1 14.0 %collective-permute-start.26 = (bf16[2,64,1024]{2,1,0:T(8,128)(2,1)S(1)}, bf16[2,64,1024]{2,1,0:T(8,128)(2,1)S(1)}, u32[]{:S(2)}, u32[]{:S(2)}) collective-permute-start(bf16[2,64,1024]{2,1,0:T(8,128)(2,1)S(1)} %get-tuple-element.173), channel_id=1, source_target_pairs={{0,12},{4,8},{8,4},{12,0},{1,13},{5,9},{9,5},{13,1},{2,14},{6,10},... | collective-permute-start | bytes 786440 | tf_op jit(solution)/shard_map/ppermute | solution.py:873
  154.1 7.8 %collective-permute-start.27 = (bf16[8,64,1408]{2,1,0:T(8,128)(2,1)}, bf16[8,64,1408]{2,1,0:T(8,128)(2,1)}, u32[]{:S(2)}, u32[]{:S(2)}) collective-permute-start(bf16[8,64,1408]{2,1,0:T(8,128)(2,1)} %get-tuple-element.189), channel_id=1, source_target_pairs={{0,2},{2,0},{1,3},{3,1},{4,6},{6,4},{5,7},{7,5},{8,10},{10,8},{9,1... | collective-permute-start | bytes 4325384 | tf_op jit(solution)/shard_map/ppermute | solution.py:873
  154.1 7.8 %collective-permute-start.28 = (bf16[2,176,1024]{2,1,0:T(8,128)(2,1)}, bf16[2,176,1024]{2,1,0:T(8,128)(2,1)}, u32[]{:S(2)}, u32[]{:S(2)}) collective-permute-start(bf16[2,176,1024]{2,1,0:T(8,128)(2,1)} %get-tuple-element.190), channel_id=1, source_target_pairs={{0,2},{2,0},{1,3},{3,1},{4,6},{6,4},{5,7},{7,5},{8,10},{10,8},{9,1... | collective-permute-start | bytes 2162696 | tf_op jit(solution)/shard_map/ppermute | solution.py:873
  157.7 10.2 %all-to-all-start.3 = ((bf16[8,2,64,128]{3,2,1,0:T(8,128)(2,1)}), bf16[8,2,64,128]{3,2,1,0:T(8,128)(2,1)}, u32[]{:S(2)}, u32[]{:S(2)}) async-start(bf16[8,2,64,128]{3,2,1,0:T(8,128)(2,1)} %get-tuple-element.186), calls=%async_computation.3 | async-start | bytes 524288 | tf_op jit(solution)/shard_map/all_to_all | solution.py:1127
  168.0 45.8 %all-to-all-start.4 = ((bf16[4,2,64,1024]{3,2,1,0:T(8,128)(2,1)}), bf16[4,2,64,1024]{3,2,1,0:T(8,128)(2,1)}, u32[]{:S(2)}, u32[]{:S(2)}) async-start(bf16[4,2,64,1024]{3,2,1,0:T(8,128)(2,1)} %get-tuple-element.210), calls=%async_computation.4 | async-start | bytes 2097152 | tf_op jit(solution)/shard_map/all_to_all | solution.py:1135
  173.7 40.0 %collective-permute-start.29 = (bf16[4,2,32,1408]{3,2,0,1:T(8,128)(2,1)S(1)}, bf16[4,2,32,1408]{3,2,0,1:T(8,128)(2,1)}, u32[]{:S(2)}, u32[]{:S(2)}) collective-permute-start(bf16[4,2,32,1408]{3,2,0,1:T(8,128)(2,1)S(1)} %bitcast.210), channel_id=1, source_target_pairs={{0,16},{16,0},{1,17},{17,1},{2,18},{18,2},{3,19},{19,3},{4,20},{20... | collective-permute-start | bytes 2162696 | tf_op jit(solution)/shard_map/ppermute | solution.py:873
  174.3 26.0 %collective-permute-start.30 = (bf16[2,1,88,1024]{3,2,0,1:T(8,128)(2,1)S(1)}, bf16[2,1,88,1024]{3,2,0,1:T(8,128)(2,1)S(1)}, u32[]{:S(2)}, u32[]{:S(2)}) collective-permute-start(bf16[2,1,88,1024]{3,2,0,1:T(8,128)(2,1)S(1)} %select_bitcast_fusion.7), channel_id=1, source_target_pairs={{0,1},{1,0},{2,3},{3,2},{4,5},{5,4},{6,7},{7,6},{8,9},{9,8},{10,11... | collective-permute-start | bytes 1081352 | tf_op jit(solution)/shard_map/ppermute | solution.py:873
  175.8 25.5 %collective-permute-start.31 = (bf16[2,64,1024]{2,1,0:T(8,128)(2,1)S(1)}, bf16[2,64,1024]{2,1,0:T(8,128)(2,1)S(1)}, u32[]{:S(2)}, u32[]{:S(2)}) collective-permute-start(bf16[2,64,1024]{2,1,0:T(8,128)(2,1)S(1)} %get-tuple-element.209.refs_0_), channel_id=1, source_target_pairs={{0,4},{4,0},{8,12},{12,8},{1,5},{5,1},{9,13},{13,9},{2,6},{6,2},{1... | collective-permute-start | bytes 786440 | tf_op jit(solution)/shard_map/ppermute | solution.py:873
  177.8 30.6 %collective-permute-start.32 = (bf16[2,64,1024]{2,1,0:T(8,128)(2,1)S(1)}, bf16[2,64,1024]{2,1,0:T(8,128)(2,1)S(1)}, u32[]{:S(2)}, u32[]{:S(2)}) collective-permute-start(bf16[2,64,1024]{2,1,0:T(8,128)(2,1)S(1)} %get-tuple-element.209.refs_0_), channel_id=1, source_target_pairs={{0,8},{4,12},{8,0},{12,4},{1,9},{5,13},{9,1},{13,5},{2,10},{6,14},... | collective-permute-start | bytes 786440 | tf_op jit(solution)/shard_map/ppermute | solution.py:873
  179.3 34.5 %collective-permute-start.33 = (bf16[2,64,1024]{2,1,0:T(8,128)(2,1)S(1)}, bf16[2,64,1024]{2,1,0:T(8,128)(2,1)S(1)}, u32[]{:S(2)}, u32[]{:S(2)}) collective-permute-start(bf16[2,64,1024]{2,1,0:T(8,128)(2,1)S(1)} %get-tuple-element.209.refs_0_), channel_id=1, source_target_pairs={{0,12},{4,8},{8,4},{12,0},{1,13},{5,9},{9,5},{13,1},{2,14},{6,10},... | collective-permute-start | bytes 786440 | tf_op jit(solution)/shard_map/ppermute | solution.py:873
  213.7 5.3 %collective-permute-start.35 = (bf16[8,64,1024]{2,1,0:T(8,128)(2,1)}, bf16[8,64,1024]{2,1,0:T(8,128)(2,1)S(1)}, u32[]{:S(2)}, u32[]{:S(2)}) collective-permute-start(bf16[8,64,1024]{2,1,0:T(8,128)(2,1)} %get-tuple-element.222), channel_id=1, source_target_pairs={{0,2},{2,0},{1,3},{3,1},{4,6},{6,4},{5,7},{7,5},{8,10},{10,8},{9,1... | collective-permute-start | bytes 3145736 | tf_op jit(solution)/shard_map/ppermute | solution.py:873
  213.7 3.8 %collective-permute-start.34 = (bf16[8,64,640]{2,1,0:T(8,128)(2,1)}, bf16[8,64,640]{2,1,0:T(8,128)(2,1)S(1)}, u32[]{:S(2)}, u32[]{:S(2)}) collective-permute-start(bf16[8,64,640]{2,1,0:T(8,128)(2,1)} %get-tuple-element.213), channel_id=1, source_target_pairs={{0,2},{2,0},{1,3},{3,1},{4,6},{6,4},{5,7},{7,5},{8,10},{10,8},{9,1... | collective-permute-start | bytes 1966088 | tf_op jit(solution)/shard_map/ppermute | solution.py:873
  219.9 12.5 %collective-permute-start.40 = (bf16[2,2,32,1024]{3,2,0,1:T(8,128)(2,1)}, bf16[2,2,32,1024]{3,2,0,1:T(8,128)(2,1)}, u32[]{:S(2)}, u32[]{:S(2)}) collective-permute-start(bf16[2,2,32,1024]{3,2,0,1:T(8,128)(2,1)} %select_bitcast_fusion.10), channel_id=1, source_target_pairs={{0,2},{2,0},{1,3},{3,1},{4,6},{6,4},{5,7},{7,5},{8,10},{10,8},{9,1... | collective-permute-start | bytes 786440 | tf_op jit(solution)/shard_map/ppermute | solution.py:873
  221.3 25.4 %all-to-all-start.5 = ((bf16[4,2,64,1024]{3,2,1,0:T(8,128)(2,1)}), bf16[4,2,64,1024]{3,2,1,0:T(8,128)(2,1)S(1)}, u32[]{:S(2)}, u32[]{:S(2)}) async-start(bf16[4,2,64,1024]{3,2,1,0:T(8,128)(2,1)} %token_pieces.1), calls=%async_computation.5 | async-start | bytes 2097152 | tf_op jit(solution)/shard_map/all_to_all | solution.py:1221
  226.4 23.6 %copy-start.11 = (bf16[2,64,1024]{2,1,0:T(8,128)(2,1)S(1)}, bf16[2,64,1024]{2,1,0:T(8,128)(2,1)}, u32[]{:S(2)}) copy-start(bf16[2,64,1024]{2,1,0:T(8,128)(2,1)} %copy-done.10) | copy-start | bytes 786436
  226.4 23.6 %copy-start.14 = (f32[2,64,1024]{2,1,0:T(8,128)S(1)}, f32[2,64,1024]{2,1,0:T(8,128)}, u32[]{:S(2)}) copy-start(f32[2,64,1024]{2,1,0:T(8,128)} %copy-done.13) | copy-start | bytes 1572868
  226.4 23.6 %copy-start.16 = (f32[8,1024]{1,0:T(8,128)S(1)}, f32[8,1024]{1,0:T(8,128)}, u32[]{:S(2)}) copy-start(f32[8,1024]{1,0:T(8,128)} %get-tuple-element.169.gains_ref) | copy-start | bytes 98308
  226.4 11.3 %collective-permute-start.39 = (bf16[4,1,32,1408]{3,2,0,1:T(8,128)(2,1)S(1)}, bf16[4,1,32,1408]{3,2,0,1:T(8,128)(2,1)S(1)}, u32[]{:S(2)}, u32[]{:S(2)}) collective-permute-start(bf16[4,1,32,1408]{3,2,0,1:T(8,128)(2,1)S(1)} %select_bitcast_fusion.6), channel_id=1, source_target_pairs={{0,1},{1,0},{2,3},{3,2},{4,5},{5,4},{6,7},{7,6},{8,9},{9,8},{10,11... | collective-permute-start | bytes 1081352 | tf_op jit(solution)/shard_map/ppermute | solution.py:873
  228.0 28.1 %collective-permute-start.36 = (bf16[4,32,1152]{2,1,0:T(8,128)(2,1)}, bf16[4,32,1152]{2,1,0:T(8,128)(2,1)S(1)}, u32[]{:S(2)}, u32[]{:S(2)}) collective-permute-start(bf16[4,32,1152]{2,1,0:T(8,128)(2,1)} %get-tuple-element.225), channel_id=1, source_target_pairs={{0,1},{1,0},{2,3},{3,2},{4,5},{5,4},{6,7},{7,6},{8,9},{9,8},{10,11... | collective-permute-start | bytes 884744 | tf_op jit(solution)/shard_map/ppermute | solution.py:873
  228.5 27.6 %collective-permute-start.37 = (bf16[4,32,1152]{2,1,0:T(8,128)(2,1)}, bf16[4,32,1152]{2,1,0:T(8,128)(2,1)S(1)}, u32[]{:S(2)}, u32[]{:S(2)}) collective-permute-start(bf16[4,32,1152]{2,1,0:T(8,128)(2,1)} %get-tuple-element.226), channel_id=1, source_target_pairs={{0,16},{16,0},{1,17},{17,1},{2,18},{18,2},{3,19},{19,3},{4,20},{20... | collective-permute-start | bytes 884744 | tf_op jit(solution)/shard_map/ppermute | solution.py:873
  229.0 33.4 %collective-permute-start.38 = (bf16[4,32,1152]{2,1,0:T(8,128)(2,1)}, bf16[4,32,1152]{2,1,0:T(8,128)(2,1)S(1)}, u32[]{:S(2)}, u32[]{:S(2)}) collective-permute-start(bf16[4,32,1152]{2,1,0:T(8,128)(2,1)} %get-tuple-element.227), channel_id=1, source_target_pairs={{0,17},{1,16},{16,1},{17,0},{2,19},{3,18},{18,3},{19,2},{4,21},{5,... | collective-permute-start | bytes 884744 | tf_op jit(solution)/shard_map/ppermute | solution.py:873
  248.4 6.6 %collective-permute-start.41 = (bf16[2,1,32,1024]{3,2,0,1:T(8,128)(2,1)}, bf16[2,1,32,1024]{3,2,0,1:T(8,128)(2,1)S(1)}, u32[]{:S(2)}, u32[]{:S(2)}) collective-permute-start(bf16[2,1,32,1024]{3,2,0,1:T(8,128)(2,1)} %fusion.6), channel_id=1, source_target_pairs={{0,1},{1,0},{2,3},{3,2},{4,5},{5,4},{6,7},{7,6},{8,9},{9,8},{10,11... | collective-permute-start | bytes 393224 | tf_op jit(solution)/shard_map/ppermute | solution.py:873
  250.9 21.6 %collective-permute-start.43 = (bf16[64,1024]{1,0:T(8,128)(2,1)S(1)}, bf16[64,1024]{1,0:T(8,128)(2,1)}, u32[]{:S(2)}, u32[]{:S(2)}) collective-permute-start(bf16[64,1024]{1,0:T(8,128)(2,1)S(1)} %select_bitcast_fusion.13), channel_id=1, source_target_pairs={{0,16},{16,0},{1,17},{17,1},{2,18},{18,2},{3,19},{19,3},{4,20},{20... | collective-permute-start | bytes 393224 | tf_op jit(solution)/shard_map/ppermute | solution.py:873
  250.9 33.6 %all-to-all-start.6 = ((bf16[4,32,1408]{2,1,0:T(8,128)(2,1)}), bf16[4,32,1408]{2,1,0:T(8,128)(2,1)S(1)}, u32[]{:S(2)}, u32[]{:S(2)}) async-start(bf16[4,32,1408]{2,1,0:T(8,128)(2,1)} %fusion.2), calls=%async_computation.6 | async-start | bytes 720896 | tf_op jit(solution)/shard_map/all_to_all | solution.py:1231
  262.4 21.3 %collective-permute-start.48 = (bf16[88,1024]{1,0:T(8,128)(2,1)S(1)}, bf16[88,1024]{1,0:T(8,128)(2,1)S(1)}, u32[]{:S(2)}, u32[]{:S(2)}) collective-permute-start(bf16[88,1024]{1,0:T(8,128)(2,1)S(1)} %fusion.5), channel_id=1, source_target_pairs={{0,16},{16,0},{1,17},{17,1},{2,18},{18,2},{3,19},{19,3},{4,20},{20... | collective-permute-start | bytes 540680 | tf_op jit(solution)/shard_map/ppermute | solution.py:873
  262.5 13.3 %collective-permute-start.47 = (bf16[32,1024]{1,0:T(8,128)(2,1)S(1)}, bf16[32,1024]{1,0:T(8,128)(2,1)S(1)}, u32[]{:S(2)}, u32[]{:S(2)}) collective-permute-start(bf16[32,1024]{1,0:T(8,128)(2,1)S(1)} %fusion.11), channel_id=1, source_target_pairs={{0,16},{16,0},{1,17},{17,1},{2,18},{18,2},{3,19},{19,3},{4,20},{20... | collective-permute-start | bytes 196616 | tf_op jit(solution)/shard_map/ppermute | solution.py:873
  266.2 10.3 %collective-permute-start.44 = (bf16[32,1152]{1,0:T(8,128)(2,1)S(1)}, bf16[32,1152]{1,0:T(8,128)(2,1)S(1)}, u32[]{:S(2)}, u32[]{:S(2)}) collective-permute-start(bf16[32,1152]{1,0:T(8,128)(2,1)S(1)} %get-tuple-element.243), channel_id=1, source_target_pairs={{0,4},{4,0},{8,12},{12,8},{1,5},{5,1},{9,13},{13,9},{2,6},{6,2},{1... | collective-permute-start | bytes 221192 | tf_op jit(solution)/shard_map/ppermute | solution.py:873
  270.9 5.5 %collective-permute-start.45 = (bf16[32,1152]{1,0:T(8,128)(2,1)S(1)}, bf16[32,1152]{1,0:T(8,128)(2,1)S(1)}, u32[]{:S(2)}, u32[]{:S(2)}) collective-permute-start(bf16[32,1152]{1,0:T(8,128)(2,1)S(1)} %get-tuple-element.244), channel_id=1, source_target_pairs={{0,8},{4,12},{8,0},{12,4},{1,9},{5,13},{9,1},{13,5},{2,10},{6,14},... | collective-permute-start | bytes 221192 | tf_op jit(solution)/shard_map/ppermute | solution.py:873
  272.5 6.3 %collective-permute-start.46 = (bf16[32,1152]{1,0:T(8,128)(2,1)S(1)}, bf16[32,1152]{1,0:T(8,128)(2,1)S(1)}, u32[]{:S(2)}, u32[]{:S(2)}) collective-permute-start(bf16[32,1152]{1,0:T(8,128)(2,1)S(1)} %get-tuple-element.245), channel_id=1, source_target_pairs={{0,12},{4,8},{8,4},{12,0},{1,13},{5,9},{9,5},{13,1},{2,14},{6,10},... | collective-permute-start | bytes 221192 | tf_op jit(solution)/shard_map/ppermute | solution.py:873
  275.8 7.2 %collective-permute-start.42 = (bf16[64,1024]{1,0:T(8,128)(2,1)S(1)}, bf16[64,1024]{1,0:T(8,128)(2,1)S(1)}, u32[]{:S(2)}, u32[]{:S(2)}) collective-permute-start(bf16[64,1024]{1,0:T(8,128)(2,1)S(1)} %select_bitcast_fusion.14), channel_id=1, source_target_pairs={{0,16},{16,0},{1,17},{17,1},{2,18},{18,2},{3,19},{19,3},{4,20},{20... | collective-permute-start | bytes 393224 | tf_op jit(solution)/shard_map/ppermute | solution.py:873
  (33 other events, 207.7 us)
